TPU v7x, 128 devices: a whole 4x4x4 slice. The times are simulated.
128 devices in a mesh: rows: 8 (over y, x_hi), seq: 16 (over z, x_lo, core).
Axes of the slice: x: 4 (x_hi: 2, x_lo: 2; x = x_hi * 2 + x_lo), y: 4, z: 4, core: 2. Of those that a mesh axis runs over, the one named last changes fastest.
Arguments:
- tokens: bfloat16 [8, 2048, 1024], P('rows', 'seq'), may hold values from -6 to 6
- cotangent: bfloat16 [8, 2048, 1024], P('rows', 'seq'), may hold values from -6 to 6
- segment: int32 [8, 2048], P('rows', 'seq'), may hold values from 0 to 3, never falling along the last dimension, each value on 1 to 1024 neighbouring positions
- routes: int32 [8, 2048, 2], P('rows', 'seq'), may hold values from 0 to 2, all different within a row
- attn_gain: bfloat16 [1024], replicated, may hold values from 0.5 to 1.5
- w_query: bfloat16 [1024, 1024], replicated, may hold values from -0.25 to 0.25
- w_key: bfloat16 [1024, 512], replicated, may hold values from -0.25 to 0.25
- w_value: bfloat16 [1024, 512], replicated, may hold values from -0.1875 to 0.1875
- w_output: bfloat16 [1024, 1024], replicated, may hold values from -0.75 to 0.75
- expert_norm_gain: bfloat16 [1024], replicated, may hold values from 0.5 to 1.5
- w_router: bfloat16 [1024, 3], replicated, may hold values from -0.375 to 0.375
- w_gate: bfloat16 [3, 1024, 512], replicated, may hold values from -0.1875 to 0.1875
- w_up: bfloat16 [3, 1024, 512], replicated, may hold values from -0.1875 to 0.1875
- w_down: bfloat16 [3, 512, 1024], replicated, may hold values from -0.5 to 0.5
Outputs:
- output: bfloat16 [8, 2048, 1024], P('rows', 'seq')
- token_grad: bfloat16 [8, 2048, 1024], P('rows', 'seq')
- attn_gain_grad: float32 [1024], replicated
- query_w_grad: float32 [1024, 1024], replicated
- key_w_grad: float32 [1024, 512], replicated
- value_w_grad: float32 [1024, 512], replicated
- output_w_grad: float32 [1024, 1024], replicated
- moe_gain_grad: float32 [1024], replicated
- router_grad: float32 [1024, 3], replicated
- gate_grad: float32 [3, 1024, 512], replicated
- up_grad: float32 [3, 1024, 512], replicated
- down_grad: float32 [3, 512, 1024], replicated
Inputs may be any that keep to these rules, and one draw needn't show every extreme that they name: `segment`: in each packed row the ids never fall; each of the 4 ids names one document of 1 to 1024 tokens, and one document has exactly 1024. `routes`: each token names 2 different experts.
All inputs are finite; a program needn't handle non-finite values.
Results may differ from a plain program's by a relative error of at most 0.02.
The roundings to bfloat16 on the way count: a program that leaves them out, or rounds other values in their place, can miss the bound.
Values may be sent and summed in bfloat16 or wider, within the bound.
No kernel may reach another device: no remote copies, remote signals or barrier semaphores. Data moves between devices by JAX's collectives and lax.ppermute only.
A program may use at most 192 MiB of HBM per device.

v0:
```python
import math

import jax
import jax.numpy as jnp
from jax import lax
from jax.sharding import PartitionSpec as P

HD = 64


EPSILON = 1e-06
THETA_BASE = 10000.0
SOFT_SCALE = 0.125
NEG_FILL = -1e30


def joined_along(parts, dim):
    parts = jnp.moveaxis(parts, 0, dim)
    lengths = parts.shape
    return parts.reshape(*lengths[:dim], lengths[dim] * lengths[dim + 1], *lengths[dim + 2 :])


def sent_to_all(array, axis):
    devices = lax.axis_size(axis)
    return lax.all_to_all(
        jnp.broadcast_to(array[None], (devices, *array.shape)), axis, 0, 0, tiled=True
    )


def collect(array, axis, dim):
    return joined_along(sent_to_all(array, axis), dim)


def side_by_side(arrays, axis, dim, along):
    both = jnp.concatenate(arrays, axis=along)
    whole, at, finished = (lax.all_gather(both, axis, axis=dim, tiled=True), 0, [])
    for a in arrays:
        finished.append(lax.slice_in_dim(whole, at, at + a.shape[along], axis=along))
        at += a.shape[along]
    return tuple(finished)


def side_by_side_2(arrays, axis, dim, along):
    ends, at = ([], 0)
    for a in arrays[:-1]:
        at += a.shape[along]
        ends.append(at)
    both = jnp.concatenate(arrays, axis=along)
    return tuple(
        jnp.split(lax.psum_scatter(both, axis, scatter_dimension=dim, tiled=True), ends, axis=along)
    )


def rms_apply(hidden, gain):
    inverse = lax.rsqrt(jnp.mean(hidden * hidden, axis=-1, keepdims=True) + EPSILON)
    return hidden * inverse * gain


def rotate(heads, cosine_table, sine_table):
    half_size = heads.shape[-1] // 2
    turned = jnp.concatenate([-heads[..., half_size:], heads[..., :half_size]], axis=-1)
    return heads * cosine_table + turned * sine_table


def rope_tables(positions, head_size):
    frequency = jnp.exp(
        jnp.arange(head_size // 2, dtype=jnp.float32) * (-2.0 * math.log(THETA_BASE) / head_size)
    )
    angles = positions[..., None] * frequency
    angles = jnp.concatenate([angles, angles], axis=-1)
    return (jnp.cos(angles)[..., None, :], jnp.sin(angles)[..., None, :])


def swiglu(gate_proj, up_proj):
    return jax.nn.silu(gate_proj) * up_proj


def route_weights(logits, routes):
    one_hot = (routes[..., None] == jnp.arange(logits.shape[-1], dtype=jnp.int32)).astype(
        jnp.float32
    )
    chosen = jnp.sum(one_hot * logits[..., None, :], axis=-1)
    weights = jax.nn.softmax(chosen, axis=-1)
    return jnp.sum(weights[..., None] * one_hot, axis=-2)


def keep_same(running):
    return running


def blockwise(block_step, running, arrays, offset):
    key_count = arrays[0].shape[1]
    block_width = math.gcd(key_count, 512)

    def one_block(block_index, inner_carry):
        pieces = tuple(
            (
                lax.dynamic_slice_in_dim(array_item, block_index * block_width, block_width, 1)
                for array_item in arrays
            )
        )
        return block_step(inner_carry, pieces, offset + block_index * block_width)

    return lax.fori_loop(0, key_count // block_width, one_block, running)


def masked_scores(queries, key_piece, key_start, query_seg, query_index, seg_all):
    batch_row_list, key_count = (key_piece.shape[0], key_piece.shape[1])
    key_heads = key_piece.reshape(batch_row_list, key_count, queries.shape[2], queries.shape[4])
    scores = (
        jnp.einsum("rskgd,rnkd->rkgsn", queries, key_heads, preferred_element_type=jnp.float32)
        * SOFT_SCALE
    )
    key_seg = lax.dynamic_slice_in_dim(seg_all, key_start, key_count, 1)
    key_index = key_start + jnp.arange(key_count, dtype=jnp.int32)
    allowed = (key_seg[:, None, :] == query_seg[:, :, None]) & (
        key_index[None, None, :] <= query_index[None, :, None]
    )
    allowed = allowed[:, None, None]
    return (jnp.where(allowed, scores, NEG_FILL), allowed, key_heads)


def shards(
    tokens,
    cotangent,
    segment,
    routes,
    attn_gain,
    w_query,
    w_key,
    w_value,
    w_output,
    expert_norm_gain,
    w_router,
    w_gate,
    w_up,
    w_down,
):
    batch_row_list, local_len, model_width = tokens.shape
    kv_heads = w_key.shape[1] // HD
    group_size = w_query.shape[1] // w_key.shape[1]
    expert_count = w_gate.shape[0]
    seq_count = lax.axis_size("seq")
    seq_len = local_len * seq_count
    my_place = lax.axis_index("seq")
    seg_all = collect(segment, "seq", 1)
    query_index = my_place * local_len + jnp.arange(local_len, dtype=jnp.int32)
    last_index = query_index[local_len - 1]
    starts = jnp.sum((seg_all[:, None, :] < segment[:, :, None]).astype(jnp.int32), axis=-1)
    positions = (query_index[None, :] - starts).astype(jnp.float32)
    cosine_table, sine_table = rope_tables(positions, HD)
    inputs = tokens.astype(jnp.float32)
    normed, attn_norm_back = jax.vjp(rms_apply, inputs, attn_gain.astype(jnp.float32))
    normed_low = normed.astype(jnp.bfloat16)
    queries_raw = jnp.einsum(
        "rsd,de->rse", normed_low, w_query, preferred_element_type=jnp.float32
    ).reshape(batch_row_list, local_len, kv_heads * group_size, HD)
    keys_raw = jnp.einsum(
        "rsd,de->rse", normed_low, w_key, preferred_element_type=jnp.float32
    ).reshape(batch_row_list, local_len, kv_heads, HD)
    values_low = jnp.einsum(
        "rsd,de->rse", normed_low, w_value, preferred_element_type=jnp.float32
    ).astype(jnp.bfloat16)

    def turn_heads(heads):
        return rotate(heads, cosine_table, sine_table)

    queries_rot, query_rope_back = jax.vjp(turn_heads, queries_raw)
    keys_rot, key_rope_back = jax.vjp(turn_heads, keys_raw)
    queries_low = queries_rot.astype(jnp.bfloat16).reshape(
        batch_row_list, local_len, kv_heads, group_size, HD
    )
    keys_low = keys_rot.astype(jnp.bfloat16).reshape(batch_row_list, local_len, kv_heads * HD)

    def stats_step(running, pieces, key_start):

        def stats_compute(inner_carry):
            top_score, exp_total = inner_carry
            scores, allowed, key_heads = masked_scores(
                queries_low, pieces[0], key_start, segment, query_index, seg_all
            )
            new_top = jnp.maximum(top_score, jnp.max(scores, axis=-1))
            weights = jnp.where(allowed, jnp.exp(scores - new_top[..., None]), 0.0)
            return (new_top, exp_total * jnp.exp(top_score - new_top) + jnp.sum(weights, axis=-1))

        return lax.cond(key_start <= last_index, stats_compute, keep_same, running)

    def out_step(running, pieces, key_start):

        def out_compute(partial_out):
            scores, allowed, key_heads = masked_scores(
                queries_low, pieces[0], key_start, segment, query_index, seg_all
            )
            weights_low = jnp.where(allowed, jnp.exp(scores - log_total[..., None]), 0.0).astype(
                jnp.bfloat16
            )
            value_heads = pieces[1].reshape(key_heads.shape)
            return partial_out + jnp.einsum(
                "rkgsn,rnkd->rskgd", weights_low, value_heads, preferred_element_type=jnp.float32
            )

        return lax.cond(key_start <= last_index, out_compute, keep_same, running)

    def make_grad_step(acc_base):

        def grad_step(running, pieces, key_start):

            def grad_compute(inner_carry):
                query_grad, key_grads, value_grads = inner_carry
                scores, allowed, key_heads = masked_scores(
                    queries_low, pieces[0], key_start, segment, query_index, seg_all
                )
                key_count = key_heads.shape[1]
                value_heads = pieces[1].reshape(key_heads.shape)
                weights = jnp.where(allowed, jnp.exp(scores - log_total[..., None]), 0.0)
                weight_grad = jnp.einsum(
                    "rskgd,rnkd->rkgsn",
                    grad_attended,
                    value_heads,
                    preferred_element_type=jnp.float32,
                )
                score_grad = (weights * (weight_grad - delta[..., None])).astype(jnp.bfloat16)
                query_grad = query_grad + SOFT_SCALE * jnp.einsum(
                    "rkgsn,rnkd->rskgd", score_grad, key_heads, preferred_element_type=jnp.float32
                )
                key_part = SOFT_SCALE * jnp.einsum(
                    "rkgsn,rskgd->rnkd", score_grad, queries_low, preferred_element_type=jnp.float32
                )
                value_part = jnp.einsum(
                    "rkgsn,rskgd->rnkd",
                    weights.astype(jnp.bfloat16),
                    grad_attended,
                    preferred_element_type=jnp.float32,
                )
                key_part = key_part.reshape(batch_row_list, key_count, -1)
                value_part = value_part.reshape(batch_row_list, key_count, -1)
                place = key_start - acc_base
                key_grads = lax.dynamic_update_slice_in_dim(
                    key_grads,
                    lax.dynamic_slice_in_dim(key_grads, place, key_count, 1) + key_part,
                    place,
                    1,
                )
                value_grads = lax.dynamic_update_slice_in_dim(
                    value_grads,
                    lax.dynamic_slice_in_dim(value_grads, place, key_count, 1) + value_part,
                    place,
                    1,
                )
                return (query_grad, key_grads, value_grads)

            return lax.cond(key_start <= last_index, grad_compute, keep_same, running)

        return grad_step

    top_init = jnp.full((batch_row_list, kv_heads, group_size, local_len), NEG_FILL, jnp.float32)
    total_init = jnp.zeros((batch_row_list, kv_heads, group_size, local_len), jnp.float32)
    keys_all, values_all = side_by_side((keys_low, values_low), "seq", 1, 0)
    top_score, exp_total = blockwise(stats_step, (top_init, total_init), (keys_all,), 0)
    log_total = top_score + jnp.log(exp_total)
    out_init = jnp.zeros((batch_row_list, local_len, kv_heads, group_size, HD), jnp.float32)
    attended = blockwise(out_step, out_init, (keys_all, values_all), 0)
    attended_low = attended.reshape(batch_row_list, local_len, -1).astype(jnp.bfloat16)
    resid = inputs + jnp.einsum(
        "rse,ed->rsd", attended_low, w_output, preferred_element_type=jnp.float32
    )
    moe_normed, moe_norm_back = jax.vjp(rms_apply, resid, expert_norm_gain.astype(jnp.float32))
    moe_low = moe_normed.astype(jnp.bfloat16)
    logits = jnp.einsum("rsd,de->rse", moe_low, w_router, preferred_element_type=jnp.float32)

    def combine_of(logit_values):
        return route_weights(logit_values, routes)

    combine, combine_back = jax.vjp(combine_of, logits)
    grad_out = cotangent.astype(jnp.float32)
    mixture = resid
    combine_parts = []
    for expert in range(expert_count):
        gate_proj = jnp.einsum(
            "rsd,df->rsf", moe_low, w_gate[expert], preferred_element_type=jnp.float32
        )
        up_proj = jnp.einsum(
            "rsd,df->rsf", moe_low, w_up[expert], preferred_element_type=jnp.float32
        )
        act_low = swiglu(gate_proj, up_proj).astype(jnp.bfloat16)
        expert_out = jnp.einsum(
            "rsf,fd->rsd", act_low, w_down[expert], preferred_element_type=jnp.float32
        )
        mixture = mixture + combine[..., expert : expert + 1] * expert_out
        combine_parts.append(jnp.sum(grad_out * expert_out, axis=-1))
    output = mixture.astype(jnp.bfloat16)
    moe_grad = jnp.zeros_like(resid)
    gate_parts = []
    up_parts = []
    down_parts = []
    for expert in range(expert_count):
        gate_proj = jnp.einsum(
            "rsd,df->rsf", moe_low, w_gate[expert], preferred_element_type=jnp.float32
        )
        up_proj = jnp.einsum(
            "rsd,df->rsf", moe_low, w_up[expert], preferred_element_type=jnp.float32
        )
        act_value, act_back = jax.vjp(swiglu, gate_proj, up_proj)
        act_low = act_value.astype(jnp.bfloat16)
        expert_grad = (combine[..., expert : expert + 1] * grad_out).astype(jnp.bfloat16)
        down_parts.append(
            jnp.einsum("rsf,rsd->fd", act_low, expert_grad, preferred_element_type=jnp.float32)
        )
        act_grad = jnp.einsum(
            "rsd,fd->rsf", expert_grad, w_down[expert], preferred_element_type=jnp.float32
        )
        gate_grad_value, up_grad_value = act_back(act_grad)
        gate_low = gate_grad_value.astype(jnp.bfloat16)
        up_low = up_grad_value.astype(jnp.bfloat16)
        gate_parts.append(
            jnp.einsum("rsd,rsf->df", moe_low, gate_low, preferred_element_type=jnp.float32)
        )
        up_parts.append(
            jnp.einsum("rsd,rsf->df", moe_low, up_low, preferred_element_type=jnp.float32)
        )
        moe_grad = moe_grad + jnp.einsum(
            "rsf,df->rsd", gate_low, w_gate[expert], preferred_element_type=jnp.float32
        )
        moe_grad = moe_grad + jnp.einsum(
            "rsf,df->rsd", up_low, w_up[expert], preferred_element_type=jnp.float32
        )
    logit_grad = combine_back(jnp.stack(combine_parts, axis=-1))[0].astype(jnp.bfloat16)
    router_local = jnp.einsum(
        "rsd,rse->de", moe_low, logit_grad, preferred_element_type=jnp.float32
    )
    moe_grad = moe_grad + jnp.einsum(
        "rse,de->rsd", logit_grad, w_router, preferred_element_type=jnp.float32
    )
    resid_part, moe_gain_local = moe_norm_back(moe_grad)
    resid_grad = grad_out + resid_part
    gate_local = jnp.stack(gate_parts, axis=0)
    up_local = jnp.stack(up_parts, axis=0)
    down_local = jnp.stack(down_parts, axis=0)
    attn_grad_low = resid_grad.astype(jnp.bfloat16)
    output_local = jnp.einsum(
        "rse,rsd->ed", attended_low, attn_grad_low, preferred_element_type=jnp.float32
    )
    grad_attended = jnp.einsum(
        "rsd,ed->rse", attn_grad_low, w_output, preferred_element_type=jnp.float32
    ).astype(jnp.bfloat16)
    grad_attended = grad_attended.reshape(batch_row_list, local_len, kv_heads, group_size, HD)
    delta = jnp.einsum("rskgd,rskgd->rkgs", grad_attended.astype(jnp.float32), attended)
    grad_init = (
        jnp.zeros_like(attended),
        jnp.zeros((batch_row_list, seq_len, kv_heads * HD), jnp.float32),
        jnp.zeros((batch_row_list, seq_len, kv_heads * HD), jnp.float32),
    )
    query_grad, key_grads, value_grads = blockwise(
        make_grad_step(0), grad_init, (keys_all, values_all), 0
    )
    key_sum, value_sum = tuple(
        (
            part.astype(jnp.float32)
            for part in side_by_side_2(
                (key_grads.astype(jnp.bfloat16), value_grads.astype(jnp.bfloat16)), "seq", 1, 0
            )
        )
    )
    query_low_grad = query_rope_back(
        query_grad.reshape(batch_row_list, local_len, kv_heads * group_size, HD)
    )[0]
    query_low_grad = query_low_grad.reshape(batch_row_list, local_len, -1).astype(jnp.bfloat16)
    key_low_grad = key_rope_back(key_sum.reshape(batch_row_list, local_len, kv_heads, HD))[0]
    key_low_grad = key_low_grad.reshape(batch_row_list, local_len, -1).astype(jnp.bfloat16)
    value_low_grad = value_sum.astype(jnp.bfloat16)
    query_local = jnp.einsum(
        "rsd,rse->de", normed_low, query_low_grad, preferred_element_type=jnp.float32
    )
    key_local = jnp.einsum(
        "rsd,rse->de", normed_low, key_low_grad, preferred_element_type=jnp.float32
    )
    value_local = jnp.einsum(
        "rsd,rse->de", normed_low, value_low_grad, preferred_element_type=jnp.float32
    )
    normed_grad = jnp.einsum(
        "rse,de->rsd", query_low_grad, w_query, preferred_element_type=jnp.float32
    )
    normed_grad = normed_grad + jnp.einsum(
        "rse,de->rsd", key_low_grad, w_key, preferred_element_type=jnp.float32
    )
    normed_grad = normed_grad + jnp.einsum(
        "rse,de->rsd", value_low_grad, w_value, preferred_element_type=jnp.float32
    )
    input_part, attn_gain_local = attn_norm_back(normed_grad)
    token_grad = (resid_grad + input_part).astype(jnp.bfloat16)
    all_sums = lax.psum(
        (
            attn_gain_local,
            query_local,
            key_local,
            value_local,
            output_local,
            moe_gain_local,
            router_local,
            gate_local,
            up_local,
            down_local,
        ),
        ("rows", "seq"),
    )
    return (
        output,
        token_grad,
        all_sums[0],
        all_sums[1],
        all_sums[2],
        all_sums[3],
        all_sums[4],
        all_sums[5],
        all_sums[6],
        all_sums[7],
        all_sums[8],
        all_sums[9],
    )


def solution(mesh):
    return jax.shard_map(
        shards,
        mesh=mesh,
        in_specs=(
            P("rows", "seq", None),
            P("rows", "seq", None),
            P("rows", "seq"),
            P("rows", "seq", None),
            P(),
            P(),
            P(),
            P(),
            P(),
            P(),
            P(),
            P(),
            P(),
            P(),
        ),
        out_specs=(
            P("rows", "seq", None),
            P("rows", "seq", None),
            P(),
            P(),
            P(),
            P(),
            P(),
            P(),
            P(),
            P(),
            P(),
            P(),
        ),
        check_vma=False,
    )
```

profile of v0, /device:TPU:1, one launch (start us, length us, event | category | flops | bytes accessed | tf_op | source)
XLA Modules:
  0.0 572.3 jit_solution(16975333111661812859)
XLA Ops:
  8.6 7.8 %all-to-all-start = ((s32[16,1,128]{2,1,0:T(1,128)}), s32[16,1,128]{2,1,0:T(1,128)S(1)}, u32[]{:S(2)}, u32[]{:S(2)}) async-start(s32[16,1,128]{2,1,0:T(1,128)} %broadcast_in_dim.143), calls=%async_computation | async-start | bytes 16384 | tf_op jit(solution)/shard_map/all_to_all | solution.py:25
  26.8 2.6 fusion.183
  30.1 35.5 %all-gather.2.cloned.1.call-done = bf16[2,2048,512]{2,1,0:T(8,128)(2,1)} async-done(((bf16[2,128,512]{2,1,0:T(8,128)(2,1)}), bf16[2,2048,512]{2,1,0:T(8,128)(2,1)}) %all-gather.2.cloned.1.call-update) | async-done | bytes 4194320 | tf_op jit(solution)/shard_map/all_gather | solution.py:36
  65.7 4.5 fusion.188
  70.2 3.9 copy.96
  74.1 6.0 %while.51 = (s32[]{:T(128)}, f32[1,8,2,128]{3,2,1,0:T(2,128)S(1)}, f32[1,8,2,128]{3,2,1,0:T(2,128)S(1)}, s32[]{:T(128)}, s32[1,2048]{1,0:T(1,128)S(1)}, /*index=...) while((s32[]{:T(128)}, f32[1,8,2,128]{3,2,1,0:T(2,128)S(1)}, ...), condition=%wide.region_7.8_spmd.clone, body=%wide.region_2.7_spmd.clone.sunk | while | flops 142807680 | bytes 10539817 | solution.py:104
  74.8 3.2 conditional.9
  80.1 3.9 copy.95
  84.9 8.7 %while.52 = (s32[]{:T(128)}, f32[1,128,8,2,64]{1,4,3,2,0:T(8,128)}, s32[]{:T(128)}, bf16[1,2048,512]{1,2,0:T(8,128)(2,1)}, s32[1,2048]{1,0:T(1,128)S(1)}, /*inde...) while((s32[]{:T(128)}, f32[1,128,8,2,64]{1,4,3,2,0:T(8,128)}, ...), condition=%wide.region_11.12_spmd.clone, body=%wide.region_8.11_spmd.clone.sunk | while | flops 274006656 | bytes 4608793 | solution.py:104
  85.6 5.8 %conditional.10 = (f32[1,128,8,2,64]{1,4,3,2,0:T(8,128)}) conditional(s32[]{:T(128)} %convert_element_type.411, f32[1,128,8,2,64]{1,4,3,2,0:T(8,128)} %get-tuple-element.1555, (s32[]{:T(128)}, bf16[1,2048,512]{1,2,0:T(8,128)(2,1)}, s32[1,2048]{1,0:T(1,128)S(1)}, s32[1,128]{1,0:T(1,128)S(1)}, s32[]{:T(128)}, ...), branch_computations={%region_9.9_spmd, %region_10.10_spmd} | conditional | flops 274006656 | bytes 4608058 | solution.py:202
  87.9 3.5 fusion.18
  118.8 2.5 broadcast.708.clone
  121.4 2.5 broadcast.708
  123.9 13.4 %while.53 = (s32[]{:T(128)}, f32[1,128,8,2,64]{1,4,3,2,0:T(8,128)S(1)}, f32[1,2048,512]{1,2,0:T(8,128)}, f32[1,2048,512]{1,2,0:T(8,128)}, s32[]{:T(128)}, /*inde...) while((s32[]{:T(128)}, ...), condition=%wide.region_27.28_spmd.clone, body=%wide.region_24.27_spmd.clone.sunk | while | flops 684917376 | bytes 34313136 | solution.py:104
  124.6 10.7 %conditional.11 = ((f32[1,128,8,2,64]{1,4,3,2,0:T(8,128)S(1)}, f32[1,2048,512]{1,2,0:T(8,128)}, f32[1,2048,512]{1,2,0:T(8,128)})) conditional(s32[]{:T(128)} %convert_element_type.412, (f32[1,128,8,2,64]{1,4,3,2,0:T(8,128)S(1)}, f32[1,2048,512]{1,2,0:T(8,128)}, f32[1,2048,512]{1,2,0:T(8,128)}) %tuple.195, (s32[]{:T(128)}, ...), branch_computations={%region_25.25_spmd, %region_26.26_spmd} | conditional | flops 684917376 | bytes 34312312 | solution.py:252
  131.9 3.3 fusion.55
  137.3 2.7 convert_element_type.254
  141.1 2.4 pad_maximum_fusion.3
  143.5 11.1 %copy.121 = bf16[2,2048,512]{2,0,1:T(2,128)(2,1)} copy(bf16[2,2048,512]{1,2,0:T(8,128)(2,1)} %pad_maximum_fusion.3) | data formatting | bytes 8388608
  154.6 5.4 copy.126
  165.5 3.3 pad_maximum_fusion.2
  168.7 3.4 pad_maximum_fusion.1
  172.2 3.4 pad_maximum_fusion
  175.6 2.8 fusion.181
  178.4 2.7 fusion.152
  181.1 104.2 %reduce-scatter.4.cloned.1.call-done = bf16[128,1024]{1,0:T(8,128)(2,1)} async-done(((bf16[2048,1024]{1,0:T(8,128)(2,1)}), bf16[128,1024]{1,0:T(8,128)(2,1)}) %reduce-scatter.4.cloned.1.call-update) | async-done | bytes 262160
  294.6 69.5 %all-reduce.4 = (f32[1024]{0:T(1024)}, f32[1024]{0:T(1024)}, f32[1024,3]{0,1:T(4,128)}) all-reduce(f32[1024]{0:T(1024)S(1)} %get-tuple-element.1157, f32[1024]{0:T(1024)S(1)} %get-tuple-element.1155, f32[1024,3]{0,1:T(4,128)S(1)} %copy-done.56), channel_id=1, replica_groups=mesh['rows'=8,'seq'=16] {'rows','seq'}, use_global_device_ids=true, to_apply=%region_31.32 | all-reduce | flops 5120 | bytes 40960 | tf_op jit(solution)/shard_map/psum | solution.py:391
  365.0 178.4 %all-reduce.8.cloned.1.call-done = (f32[1024,1024]{1,0:T(8,128)}, f32[1024,512]{1,0:T(8,128)}, f32[1024,512]{1,0:T(8,128)}, f32[1024,1024]{1,0:T(8,128)}, f32[3,...) async-done(((f32[1024,1024]{1,0:T(8,128)}, f32[1024,512]{1,0:T(8,128)}, f32[1024,512]{1,0:T(8,128)}, f32[1024,1024]{1,0:T(8,128)}, ...) | async-done | bytes 31457296 | tf_op jit(solution)/shard_map/psum | solution.py:391
  543.4 5.1 copy.177
  554.5 3.2 copy.181
  559.0 2.9 copy.182
  562.6 2.8 copy.183
  (311 shorter events, 75.4 us)
Async XLA Ops:
  7.2 87.7 %copy-start = (bf16[1024,1024]{1,0:T(8,128)(2,1)S(1)}, bf16[1024,1024]{1,0:T(8,128)(2,1)}, u32[]{:S(2)}) copy-start(bf16[1024,1024]{1,0:T(8,128)(2,1)} %param.34) | copy-start | bytes 6291460
  7.2 15.4 %copy-start.55 = (s32[1,128]{1,0:T(1,128)S(1)}, s32[1,128]{1,0:T(1,128)}, u32[]{:S(2)}) copy-start(s32[1,128]{1,0:T(1,128)} %param.28) | copy-start | bytes 1540
  8.6 14.0 %all-to-all-start = ((s32[16,1,128]{2,1,0:T(1,128)}), s32[16,1,128]{2,1,0:T(1,128)S(1)}, u32[]{:S(2)}, u32[]{:S(2)}) async-start(s32[16,1,128]{2,1,0:T(1,128)} %broadcast_in_dim.143), calls=%async_computation | async-start | bytes 16384 | tf_op jit(solution)/shard_map/all_to_all | solution.py:25
  16.4 49.3 %all-gather.2.cloned.1.call-start = ((), (), s32[]{:S(2)}) async-start(), calls=%async_computation.2 | async-start | bytes 4456448 | tf_op jit(solution)/shard_map/all_gather | solution.py:36
  22.2 4.6 copy-start.59
  22.2 4.6 copy-start.3
  23.0 142.2 %copy-start.33 = (f32[128,64]{0,1:T(8,128)}, f32[128,64]{0,1:T(8,128)S(1)}, u32[]{:S(2)}) copy-start(f32[128,64]{0,1:T(8,128)S(1)} %get-tuple-element.1269) | copy-start | bytes 98308
  23.0 142.3 %copy-start.35 = (f32[128,64]{0,1:T(8,128)}, f32[128,64]{0,1:T(8,128)S(1)}, u32[]{:S(2)}) copy-start(f32[128,64]{0,1:T(8,128)S(1)} %get-tuple-element.1268) | copy-start | bytes 98308
  26.7 258.5 %reduce-scatter.4.cloned.1.call-start = ((), (), s32[]{:S(2)}) async-start(), calls=%async_computation.3 | async-start | bytes 4456448
  95.5 3.5 copy-start.62
  95.5 16.8 %copy-start.5 = (f32[1,128,1024]{2,1,0:T(8,128)}, f32[1,128,1024]{2,1,0:T(8,128)S(1)}, u32[]{:S(2)}) copy-start(f32[1,128,1024]{2,1,0:T(8,128)S(1)} %get-tuple-element.1276) | copy-start | bytes 1572868
  96.1 3.9 copy-start.64
  96.4 3.6 copy-start.66
  103.0 4.2 copy-start.7
  103.0 4.2 copy-start.19
  103.0 4.1 copy-start.67
  103.0 4.1 copy-start.70
  108.3 3.5 copy-start.45
  160.0 383.4 %all-reduce.8.cloned.1.call-start = ((), (), s32[]{:S(2)}) async-start(), calls=%async_computation.4 | async-start | bytes 62914560 | tf_op jit(solution)/shard_map/psum | solution.py:391
  165.4 10.1 %copy-start.24 = (bf16[1,128,16,64]{1,3,2,0:T(8,128)(2,1)}, bf16[1,128,16,64]{1,3,2,0:T(8,128)(2,1)S(1)}, u32[]{:S(2)}) copy-start(bf16[1,128,16,64]{1,3,2,0:T(8,128)(2,1)S(1)} %add_convert_fusion) | copy-start | bytes 786436
  178.4 108.8 %copy-start.34 = (f32[128,64]{0,1:T(8,128)S(1)}, f32[128,64]{0,1:T(8,128)}, u32[]{:S(2)}) copy-start(f32[128,64]{0,1:T(8,128)} %copy-done.33) | copy-start | bytes 98308
  181.1 108.0 %copy-start.36 = (f32[128,64]{0,1:T(8,128)S(1)}, f32[128,64]{0,1:T(8,128)}, u32[]{:S(2)}) copy-start(f32[128,64]{0,1:T(8,128)} %copy-done.35) | copy-start | bytes 98308
  292.6 71.5 %copy-start.61 = (f32[128]{0:T(128)S(1)}, f32[128]{0:T(128)}, u32[]{:S(2)}) copy-start(f32[128]{0:T(128)} %copy-done.60) | copy-start | bytes 1540
  543.4 5.1 copy-start.27
  543.4 6.4 %copy-start.26 = (f32[1024,512]{1,0:T(8,128)S(1)}, f32[1024,512]{1,0:T(8,128)}, u32[]{:S(2)}) copy-start(f32[1024,512]{1,0:T(8,128)} %get-tuple-element.1631) | copy-start | bytes 6291460
  543.4 11.1 %slice-start.4 = ((s8[6291456]{0:T(1024)(128)(4,1)}), s8[4194304]{0:T(1024)(128)(4,1)S(1)}, s32[]{:S(2)}) async-start(s8[6291456]{0:T(1024)(128)(4,1)} %bitcast.458), calls=%async_computation.9 | async-start | bytes 8388608
  548.5 3.9 copy-start.13
  549.8 4.7 slice-start.5
  552.3 5.4 slice-start.2
  554.5 4.6 slice-start.3
  554.5 7.5 %slice-start = ((s8[6291456]{0:T(1024)(128)(4,1)}), s8[4194304]{0:T(1024)(128)(4,1)S(1)}, s32[]{:S(2)}) async-start(s8[6291456]{0:T(1024)(128)(4,1)} %bitcast.454), calls=%async_computation.5 | async-start | bytes 8388608
  559.0 3.6 slice-start.1
  (49 other events, 94.3 us)
Sparse Core Ops, SparseCore 0:
  26.9 38.7 all-gather.1
  160.1 125.0 reduce-scatter.3
  292.8 250.4 all-reduce.7
where the time goes:
time: 574 us; the launch traced here: 572 us
  waiting for transfers between devices  318 us (55%)
  local copies, waits for them, and re-layouts  73.8 us (13%)
  blocking collectives  69.5 us (12%)
  matrix products  47.6 us (8%)
  other arithmetic  31.4 us (5%)
  between operations  15 us (3%)
  loops' own time  8.69 us (2%)
  starting transfers between devices  8.14 us (1%)
    psum x1, waiting for transfers between devices, shards(): lax.psum((attn_gain_local, query_local, key_local, value_local, output_lo...  178 us
    unnamed x4, waiting for transfers between devices  104 us
    psum x1, blocking collectives, shards(): lax.psum((attn_gain_local, query_local, key_local, value_local, output_lo...  69.5 us
    unnamed x166, local copies, waits for them, and re-layouts  53.2 us
    all_gather x1, waiting for transfers between devices, side_by_side(): lax.all_gather(both, axis, axis=dim, tiled=True)  35.5 us
  transfers between devices with their start and end apart: 4, of which 3 were waited for; matrix products, arithmetic and copies ran while one was open for 6% of the time, Pallas kernels for 0%

commit v1 on v0

v1 whole, which is shorter than its diff:
```python
import math

import jax
import jax.numpy as jnp
from jax import lax
from jax.experimental import pallas as pl
from jax.experimental.pallas import tpu as pltpu
from jax.sharding import Mesh
from jax.sharding import PartitionSpec as P

BF = jnp.bfloat16
F32 = jnp.float32
D = 1024
HQ = 16
HK = 8
HD = 64
FF = 512
EXPERTS = 3
T = 128
S = 2048
BLK = 256
NB = S // BLK
HALF = HD // 2
PAY = 3 * HD + 16
FC = 256
NF = FF // FC

EPSILON = 1e-06
THETA_BASE = 10000.0
SOFT_SCALE = 0.125
NEG_FILL = -1e30

AXES = ("y", "xh", "z", "xl", "core")
ROWS = ("y", "xh")
SEQ = ("z", "xl", "core")

NN = (((1,), (0,)), ((), ()))
NT = (((1,), (1,)), ((), ()))
TN = (((0,), (0,)), ((), ()))


def dot(a, b, dims=NN):
    return lax.dot_general(a, b, dims, preferred_element_type=F32)


def swap(a):
    return jnp.transpose(a, (1, 0))


def project_kernel(tok_ref, seg_ref, gain_ref, wq_ref, wk_ref, wv_ref, out_ref):
    x = tok_ref[...].astype(F32)
    inverse = lax.rsqrt(jnp.mean(x * x, axis=1, keepdims=True) + EPSILON)
    normed = (x * inverse * gain_ref[...].astype(F32)).astype(BF)
    ids = jnp.broadcast_to(seg_ref[...].astype(F32), (16, T)).astype(BF)
    for h in range(HQ):
        out_ref[h, 3 * HD :, :] = ids
    for j in range(4):
        q = swap(dot(normed, wq_ref[:, 256 * j : 256 * (j + 1)])).astype(BF)
        for i in range(4):
            out_ref[4 * j + i, 0:HD, :] = q[HD * i : HD * (i + 1)]
    for w_ref, at in ((wk_ref, HD), (wv_ref, 2 * HD)):
        for j in range(2):
            a = swap(dot(normed, w_ref[:, 256 * j : 256 * (j + 1)])).astype(BF)
            for i in range(4):
                part = a[HD * i : HD * (i + 1)]
                head = 2 * (4 * j + i)
                out_ref[head, at : at + HD, :] = part
                out_ref[head + 1, at : at + HD, :] = part


def project(tokens, segment, gain, w_query, w_key, w_value):
    return pl.pallas_call(
        project_kernel,
        out_shape=jax.ShapeDtypeStruct((HQ, PAY, T), BF),
        name="project",
    )(tokens, segment, gain, w_query, w_key, w_value)


def starts_of(x_ref):
    ids = x_ref[:, 3 * HD :, :].astype(F32)
    counts = [
        (jnp.sum(jnp.where(ids == float(s), 1.0, 0.0)) * (1.0 / 16)).astype(jnp.int32)
        for s in range(3)
    ]
    first = counts[0]
    second = first + counts[1]
    return first, second, second + counts[2]


def start_at(index, bounds):
    b1, b2, b3 = bounds
    return jnp.where(index >= b3, b3, jnp.where(index >= b2, b2, jnp.where(index >= b1, b1, 0)))


def joined(ref, i, at):
    return jnp.concatenate([ref[2 * i, at : at + HD, :], ref[2 * i + 1, at : at + HD, :]], axis=1)


def allowed_of(i, j, bounds):
    query = i * BLK + lax.broadcasted_iota(jnp.int32, (1, BLK), 1)
    start = start_at(query, bounds)
    key = j * BLK + lax.broadcasted_iota(jnp.int32, (BLK, BLK), 0)
    return (key >= start) & (key <= query)


def attend_kernel(x_ref, att_ref, full_ref, log_ref, q_ref, k_ref, cos_ref, sin_ref, kt_ref, v_ref):
    bounds = starts_of(x_ref)
    frequency = jnp.exp(
        lax.broadcasted_iota(jnp.int32, (HALF, 1), 0).astype(F32)
        * (-2.0 * math.log(THETA_BASE) / HD)
    )

    def turn_block(i, carry):
        index = i * BLK + lax.broadcasted_iota(jnp.int32, (1, BLK), 1)
        positions = (index - start_at(index, bounds)).astype(F32)
        angles = positions * frequency
        cosine, sine = jnp.cos(angles), jnp.sin(angles)
        cos_ref[i] = cosine
        sin_ref[i] = sine

        def turned(at):
            a = joined(x_ref, i, at).astype(F32)
            low, high = a[:HALF], a[HALF:]
            return jnp.concatenate(
                [low * cosine - high * sine, high * cosine + low * sine], axis=0
            )

        q_ref[i] = (turned(0).astype(BF).astype(F32) * SOFT_SCALE).astype(BF)
        k = turned(HD)
        k_ref[i] = k.astype(BF)
        kt_ref[i] = swap(k).astype(BF)
        v_ref[i] = joined(x_ref, i, 2 * HD)
        return carry

    lax.fori_loop(0, NB, turn_block, 0)

    def query_block(i, carry):
        first = start_at(i * BLK, bounds) // BLK
        q = q_ref[i]

        def key_block(j, running):
            top, total, acc = running
            scores = jnp.where(allowed_of(i, j, bounds), dot(kt_ref[j], q), NEG_FILL)
            new_top = jnp.maximum(top, jnp.max(scores, axis=0, keepdims=True))
            weights = jnp.exp(scores - new_top)
            scale = jnp.exp(top - new_top)
            total = total * scale + jnp.sum(weights, axis=0, keepdims=True)
            acc = acc * scale + dot(v_ref[j], weights.astype(BF))
            return new_top, total, acc

        begin = (
            jnp.full((1, BLK), NEG_FILL, F32),
            jnp.zeros((1, BLK), F32),
            jnp.zeros((HD, BLK), F32),
        )
        begin = key_block(i, begin)
        top, total, acc = lax.fori_loop(first, i, key_block, begin)
        attended = acc / total
        log_ref[i] = top + jnp.log(total)
        full_ref[i] = attended
        low = attended.astype(BF)
        att_ref[2 * i] = low[:, :T]
        att_ref[2 * i + 1] = low[:, T:]
        return carry

    lax.fori_loop(0, NB, query_block, 0)


def attend(received):
    return pl.pallas_call(
        attend_kernel,
        out_shape=(
            jax.ShapeDtypeStruct((HQ, HD, T), BF),
            jax.ShapeDtypeStruct((NB, HD, BLK), F32),
            jax.ShapeDtypeStruct((NB, 1, BLK), F32),
            jax.ShapeDtypeStruct((NB, HD, BLK), BF),
            jax.ShapeDtypeStruct((NB, HD, BLK), BF),
            jax.ShapeDtypeStruct((NB, HALF, BLK), F32),
            jax.ShapeDtypeStruct((NB, HALF, BLK), F32),
        ),
        scratch_shapes=[pltpu.VMEM((NB, BLK, HD), BF), pltpu.VMEM((NB, HD, BLK), BF)],
        name="attend",
    )(received)


def attend_back_kernel(
    x_ref, g_ref, full_ref, log_ref, q_ref, k_ref, cos_ref, sin_ref, out_ref,
    kt_ref, vt_ref, dk_ref, dv_ref,
):
    bounds = starts_of(x_ref)

    def prepare(i, carry):
        kt_ref[i] = swap(k_ref[i].astype(F32)).astype(BF)
        vt_ref[i] = swap(joined(x_ref, i, 2 * HD).astype(F32)).astype(BF)
        dk_ref[i] = jnp.zeros((HD, BLK), F32)
        dv_ref[i] = jnp.zeros((HD, BLK), F32)
        return carry

    lax.fori_loop(0, NB, prepare, 0)

    def turn_back(i, a):
        cosine, sine = cos_ref[i], sin_ref[i]
        low, high = a[:HALF], a[HALF:]
        return jnp.concatenate([low * cosine + high * sine, high * cosine - low * sine], axis=0)

    def put(i, at, a):
        low = a.astype(BF)
        out_ref[2 * i, at : at + HD, :] = low[:, :T]
        out_ref[2 * i + 1, at : at + HD, :] = low[:, T:]

    def query_block(i, carry):
        first = start_at(i * BLK, bounds) // BLK
        q = q_ref[i]
        grad = joined(g_ref, i, 0)
        delta = jnp.sum(grad.astype(F32) * full_ref[i], axis=0, keepdims=True)
        log_total = log_ref[i]

        def key_block(j, dq):
            scores = dot(kt_ref[j], q)
            p = jnp.where(allowed_of(i, j, bounds), jnp.exp(scores - log_total), 0.0)
            dp = dot(vt_ref[j], grad)
            ds = (p * (dp - delta)).astype(BF)
            dv_ref[j] += dot(grad, p.astype(BF), NT)
            dk_ref[j] += dot(q, ds, NT)
            return dq + dot(k_ref[j], ds)

        dq = lax.fori_loop(first, i + 1, key_block, jnp.zeros((HD, BLK), F32))
        put(i, 0, turn_back(i, dq * SOFT_SCALE))
        return carry

    lax.fori_loop(0, NB, query_block, 0)

    def finish(i, carry):
        put(i, HD, turn_back(i, dk_ref[i]))
        put(i, 2 * HD, dv_ref[i])
        return carry

    lax.fori_loop(0, NB, finish, 0)


def attend_back(received, grad, full, log_total, q, k, cosine, sine):
    return pl.pallas_call(
        attend_back_kernel,
        out_shape=jax.ShapeDtypeStruct((HQ, 3 * HD, T), BF),
        scratch_shapes=[
            pltpu.VMEM((NB, BLK, HD), BF),
            pltpu.VMEM((NB, BLK, HD), BF),
            pltpu.VMEM((NB, HD, BLK), F32),
            pltpu.VMEM((NB, HD, BLK), F32),
        ],
        name="attend_back",
    )(received, grad, full, log_total, q, k, cosine, sine)


def experts_kernel(
    att_ref, tok_ref, cot_ref, routes_ref, gain_ref, wr_ref, wo_ref, wg_ref, wu_ref, wd_ref,
    out_ref, resid_grad_ref, grad_att_ref, dwo_ref, dwg_ref, dwu_ref, dwd_ref, small_ref,
    moe_ref, moe_t_ref, resid_ref, combine_ref, mix_ref, moe_grad_ref, cgrad_ref,
):
    e, f = pl.program_id(0), pl.program_id(1)
    lane = lax.broadcasted_iota(jnp.int32, (T, T), 1)

    @pl.when((e == 0) & (f == 0))
    def _():
        attended = swap(att_ref[...].astype(F32)).astype(BF)
        resid = tok_ref[...].astype(F32) + dot(attended, wo_ref[...])
        inverse = lax.rsqrt(jnp.mean(resid * resid, axis=1, keepdims=True) + EPSILON)
        normed = resid * inverse * gain_ref[...].astype(F32)
        moe_low = normed.astype(BF)
        resid_ref[...] = resid
        mix_ref[...] = resid
        moe_ref[...] = moe_low
        moe_t_ref[...] = swap(normed).astype(BF)
        logits = dot(moe_low, wr_ref[...], NT)
        r0, r1 = routes_ref[:, 0:1], routes_ref[:, 1:2]
        l0 = jnp.sum(jnp.where(lane[:, :8] == r0, logits, 0.0), axis=1, keepdims=True)
        l1 = jnp.sum(jnp.where(lane[:, :8] == r1, logits, 0.0), axis=1, keepdims=True)
        top = jnp.maximum(l0, l1)
        e0, e1 = jnp.exp(l0 - top), jnp.exp(l1 - top)
        total = e0 + e1
        combine_ref[...] = jnp.where(lane == r0, e0 / total, 0.0) + jnp.where(
            lane == r1, e1 / total, 0.0
        )
        moe_grad_ref[...] = jnp.zeros_like(moe_grad_ref)
        cgrad_ref[...] = jnp.zeros_like(cgrad_ref)

    moe_low = moe_ref[...]
    grad_out = cot_ref[...].astype(F32)
    combine = jnp.sum(jnp.where(lane == e, combine_ref[...], 0.0), axis=1, keepdims=True)
    expert_grad = (combine * grad_out).astype(BF)
    gate = dot(moe_low, wg_ref[0])
    up = dot(moe_low, wu_ref[0])
    sig = 1.0 / (1.0 + jnp.exp(-gate))
    silu = gate * sig
    act = silu * up
    act_low = act.astype(BF)
    down = dot(act_low, wd_ref[0])
    mix_ref[...] += combine * down
    cgrad_ref[...] += jnp.where(lane == e, jnp.sum(grad_out * down, axis=1, keepdims=True), 0.0)
    dwd_ref[0] = dot(swap(act).astype(BF), expert_grad).astype(BF)
    act_grad = dot(expert_grad, wd_ref[0], NT)
    gate_low = (act_grad * up * (sig * (1.0 + gate * (1.0 - sig)))).astype(BF)
    up_low = (act_grad * silu).astype(BF)
    moe_t = moe_t_ref[...]
    dwg_ref[0] = dot(moe_t, gate_low).astype(BF)
    dwu_ref[0] = dot(moe_t, up_low).astype(BF)
    moe_grad_ref[...] += dot(gate_low, wg_ref[0], NT) + dot(up_low, wu_ref[0], NT)

    @pl.when((e == EXPERTS - 1) & (f == NF - 1))
    def _():
        out_ref[...] = mix_ref[...].astype(BF)
        weights, cgrad = combine_ref[...], cgrad_ref[...]
        mean = jnp.sum(weights * cgrad, axis=1, keepdims=True)
        logit_grad = (weights * (cgrad - mean)).astype(BF)
        small_ref[0:8, :] = dot(logit_grad, moe_ref[...], TN)[0:8]
        moe_grad = moe_grad_ref[...] + dot(logit_grad[:, 0:8], wr_ref[...])
        resid = resid_ref[...]
        inverse = lax.rsqrt(jnp.mean(resid * resid, axis=1, keepdims=True) + EPSILON)
        n = resid * inverse
        small_ref[8:16, :] = jnp.broadcast_to(jnp.sum(moe_grad * n, axis=0, keepdims=True), (8, D))
        scaled = moe_grad * gain_ref[...].astype(F32)
        resid_grad = cot_ref[...].astype(F32) + inverse * (
            scaled - n * jnp.mean(n * scaled, axis=1, keepdims=True)
        )
        resid_grad_ref[...] = resid_grad
        low = resid_grad.astype(BF)
        dwo_ref[...] = dot(att_ref[...], low).astype(BF)
        grad_att_ref[...] = dot(wo_ref[...], low, NT).astype(BF)


def experts(attended, tokens, cotangent, routes, gain, w_router, w_output, w_gate, w_up, w_down):
    def whole(*shape):
        return pl.BlockSpec(shape, lambda e, f: (0,) * len(shape))

    def columns():
        return pl.BlockSpec((1, D, FC), lambda e, f: (e, 0, f))

    def rows():
        return pl.BlockSpec((1, FC, D), lambda e, f: (e, f, 0))

    return pl.pallas_call(
        experts_kernel,
        grid=(EXPERTS, NF),
        in_specs=[
            whole(D, T), whole(T, D), whole(T, D), whole(T, 2), whole(1, D), whole(8, D),
            whole(D, D), columns(), columns(), rows(),
        ],
        out_specs=(
            whole(T, D), whole(T, D), whole(D, T), whole(D, D), columns(), columns(), rows(),
            whole(16, D),
        ),
        out_shape=(
            jax.ShapeDtypeStruct((T, D), BF),
            jax.ShapeDtypeStruct((T, D), F32),
            jax.ShapeDtypeStruct((D, T), BF),
            jax.ShapeDtypeStruct((D, D), BF),
            jax.ShapeDtypeStruct((EXPERTS, D, FF), BF),
            jax.ShapeDtypeStruct((EXPERTS, D, FF), BF),
            jax.ShapeDtypeStruct((EXPERTS, FF, D), BF),
            jax.ShapeDtypeStruct((16, D), F32),
        ),
        scratch_shapes=[
            pltpu.VMEM((T, D), BF),
            pltpu.VMEM((D, T), BF),
            pltpu.VMEM((T, D), F32),
            pltpu.VMEM((T, T), F32),
            pltpu.VMEM((T, D), F32),
            pltpu.VMEM((T, D), F32),
            pltpu.VMEM((T, T), F32),
        ],
        name="experts",
    )(attended, tokens, cotangent, routes, gain, w_router, w_output, w_gate, w_up, w_down)


def project_back_kernel(
    g_ref, tok_ref, gain_ref, wq_ref, wk_ref, wv_ref, resid_grad_ref,
    out_ref, dwq_ref, dwk_ref, dwv_ref, small_ref,
):
    x = tok_ref[...].astype(F32)
    gain = gain_ref[...].astype(F32)
    inverse = lax.rsqrt(jnp.mean(x * x, axis=1, keepdims=True) + EPSILON)
    n = x * inverse
    normed_t = swap(n * gain).astype(BF)
    normed_grad = jnp.zeros((T, D), F32)
    dq = g_ref[:, 0:HD, :].reshape(D, T)
    dwq_ref[...] = dot(normed_t, dq, NT).astype(BF)
    normed_grad += dot(swap(dq.astype(F32)).astype(BF), wq_ref[...], NT)
    for at, w_ref, dw_ref in ((HD, wk_ref, dwk_ref), (2 * HD, wv_ref, dwv_ref)):
        parts = g_ref[:, at : at + HD, :].astype(F32).reshape(HK, 2, HD, T)
        summed = (parts[:, 0] + parts[:, 1]).reshape(HK * HD, T)
        low = summed.astype(BF)
        dw_ref[...] = dot(normed_t, low, NT).astype(BF)
        normed_grad += dot(swap(summed).astype(BF), w_ref[...], NT)
    scaled = normed_grad * gain
    out_ref[...] = (
        resid_grad_ref[...] + inverse * (scaled - n * jnp.mean(n * scaled, axis=1, keepdims=True))
    ).astype(BF)
    small_ref[...] = jnp.broadcast_to(jnp.sum(normed_grad * n, axis=0, keepdims=True), (16, D))


def project_back(grads, tokens, gain, w_query, w_key, w_value, resid_grad):
    return pl.pallas_call(
        project_back_kernel,
        out_shape=(
            jax.ShapeDtypeStruct((T, D), BF),
            jax.ShapeDtypeStruct((D, HQ * HD), BF),
            jax.ShapeDtypeStruct((D, HK * HD), BF),
            jax.ShapeDtypeStruct((D, HK * HD), BF),
            jax.ShapeDtypeStruct((16, D), F32),
        ),
        name="project_back",
    )(grads, tokens, gain, w_query, w_key, w_value, resid_grad)


def exchange(array):
    return lax.all_to_all(array, SEQ, 0, 0, tiled=True)


def shards(
    tokens, cotangent, segment, routes, attn_gain, w_query, w_key, w_value, w_output,
    expert_norm_gain, w_router, w_gate, w_up, w_down,
):
    tokens, cotangent = tokens[0], cotangent[0]
    attn_gain = attn_gain.reshape(1, D)
    expert_norm_gain = expert_norm_gain.reshape(1, D)
    router_rows = jnp.pad(w_router.T, ((0, 8 - EXPERTS), (0, 0)))

    received = exchange(project(tokens, segment, attn_gain, w_query, w_key, w_value))
    attended, full, log_total, q, k, cosine, sine = attend(received)
    attended = exchange(attended).reshape(D, T)
    output, resid_grad, grad_att, dwo, dwg, dwu, dwd, small_moe = experts(
        attended, tokens, cotangent, routes[0], expert_norm_gain, router_rows, w_output,
        w_gate, w_up, w_down,
    )
    grad_att = exchange(grad_att.reshape(HQ, HD, T))
    grads = exchange(
        attend_back(received, grad_att, full, log_total, q, k, cosine, sine)
    )
    token_grad, dwq, dwk, dwv, small_attn = project_back(
        grads, tokens, attn_gain, w_query, w_key, w_value, resid_grad
    )
    small = jnp.concatenate([small_moe[:9], small_attn[:7]], axis=0).astype(BF)
    dwq, dwk, dwv, dwo, dwg, dwu, dwd, small = (
        a.astype(F32) for a in lax.psum((dwq, dwk, dwv, dwo, dwg, dwu, dwd, small), AXES)
    )
    return (
        output[None], token_grad[None], small[9], dwq, dwk, dwv, dwo, small[8],
        small[:EXPERTS].T, dwg, dwu, dwd,
    )


def solution(mesh):
    fine = Mesh(mesh.devices.reshape(4, 2, 4, 2, 2), AXES)
    by_token = P(ROWS, SEQ, None)
    return jax.shard_map(
        shards,
        mesh=fine,
        in_specs=(by_token, by_token, P(ROWS, SEQ), by_token) + (P(),) * 10,
        out_specs=(by_token, by_token) + (P(),) * 10,
        check_vma=False,
    )
```

time: 574 us -> 333 us (0.58)
  waiting for transfers between devices: 318 us -> 114 us
  local copies, waits for them, and re-layouts: 73.8 us -> 6.75 us
  Pallas kernels: 0 us -> 51.5 us
  blocking collectives: 69.5 us -> 121 us
  matrix products: 47.6 us -> 0 us
  other arithmetic: 31.4 us -> 20.9 us
  loops' own time: 8.69 us -> 0 us
    unnamed x4 -> x1, waiting for transfers between devices: 104 us -> 0.02 us
    psum x1, waiting for transfers between devices: 178 us -> 109 us  [shards(): lax.psum((dwq, dwk, dwv, dwo, dwg, dwu, dwd, small), AXES)]
    pallas_call x0 -> x5, Pallas kernels: none -> 51.5 us  [the longest x1 18.4 us: experts(): pl.pallas_call(experts_kernel, grid=(EXPERTS, NF), in_specs=[whole(D, T),...]
    all_to_all x0 -> x3, blocking collectives: none -> 51.4 us  [exchange(): return lax.all_to_all(array, SEQ, 0, 0, tiled=True)]
    unnamed x166 -> x23, local copies, waits for them, and re-layouts: 53.2 us -> 2.29 us
    dot_general x49 -> x0, matrix products: 47.6 us -> none  [the longest x1 3.46 us: out_compute(): jnp.einsum('rkgsn,rnkd->rskgd', weights_low, value_heads, preferred_eleme...]
    all_gather x1 -> x0, waiting for transfers between devices: 35.5 us -> none  [side_by_side(): lax.all_gather(both, axis, axis=dim, tiled=True)]
    convert_element_type x11 -> x8, other arithmetic: 7.01 us -> 20.9 us  [shards(): a.astype(F32)]
  transfers between devices with their start and end apart: 4 -> 2, of which waited for: 3 -> 2; matrix products, arithmetic and copies ran while one was open for 6% -> 1% of each run, Pallas kernels for 0% -> 0%
where the time goes in v1:
time: 333 us; the launch traced here: 332 us
  blocking collectives  121 us (36%)
  waiting for transfers between devices  114 us (34%)
  Pallas kernels  51.5 us (15%)
  other arithmetic  20.9 us (6%)
  between operations  14.1 us (4%)
  local copies, waits for them, and re-layouts  6.75 us (2%)
  starting transfers between devices  4.52 us (1%)
    psum x1, waiting for transfers between devices, shards(): lax.psum((dwq, dwk, dwv, dwo, dwg, dwu, dwd, small), AXES)  109 us
    psum x1, blocking collectives, shards(): lax.psum((dwq, dwk, dwv, dwo, dwg, dwu, dwd, small), AXES)  69.2 us
    all_to_all x3, blocking collectives, exchange(): return lax.all_to_all(array, SEQ, 0, 0, tiled=True)  51.4 us
    convert_element_type x8, other arithmetic, shards(): a.astype(F32)  20.9 us
    pallas_call x1, Pallas kernels, experts(): pl.pallas_call(experts_kernel, grid=(EXPERTS, NF), in_specs=[whole(D, T),...  18.4 us
    pallas_call x1, Pallas kernels, attend(): pl.pallas_call(attend_kernel, out_shape=(jax.ShapeDtypeStruct((HQ, HD, T)...  11.8 us
    pallas_call x1, Pallas kernels, attend_back(): pl.pallas_call(attend_back_kernel, out_shape=jax.ShapeDtypeStruct((HQ, 3...  11.1 us
  transfers between devices with their start and end apart: 2, of which 2 were waited for; matrix products, arithmetic and copies ran while one was open for 1% of the time, Pallas kernels for 0%

profile of v1, /device:TPU:1, one launch (start us, length us, event | category | flops | bytes accessed | tf_op | source)
XLA Modules:
  0.0 332.2 jit_solution(4658763536424552290)
XLA Ops:
  7.2 1.3 reshape.36.gain_ref
  8.5 4.1 %project.1 = bf16[16,208,128]{2,1,0:T(8,128)(2,1)} custom-call(bf16[128,1024]{1,0:T(8,128)(2,1)} %bitcast.12, s32[1,128]{1,0:T(1,128)} %seg_ref.1, bf16[1,1024]{1,0:T(2,128)(2,1)} %reshape.36.gain_ref, bf16[1024,1024]{1,0:T(8,128)(2,1)} %wq_ref.3, bf16[1024,512]{1,0:T(8,128)(2,1)} %wk_ref.3, bf16[1024,512]{1,0:T(8,128)(2,1)} %wv_ref.3), custom_call_target="tpu_custom_call" | custom-call | tf_op jit(solution)/shard_map/project/pallas_call | solution.py:72
  12.6 21.2 %all_to_all.20.x_ref = bf16[16,208,128]{2,1,0:T(8,128)(2,1)} all-to-all(bf16[16,208,128]{2,1,0:T(8,128)(2,1)} %project.1), channel_id=1, replica_groups=mesh['y'=4,'xh'=2,'z'=4,'xl'=2,'core'=2] {'z','xl','core'}, dimensions={0} | all-to-all | bytes 1703936 | tf_op jit(solution)/shard_map/all_to_all | solution.py:416
  33.7 11.8 %attend.1 = (bf16[16,64,128]{2,1,0:T(8,128)(2,1)}, f32[8,64,256]{2,1,0:T(8,128)}, f32[8,1,256]{2,1,0:T(1,128)}, bf16[8,64,256]{2,1,0:T(8,128)(2,1)}, bf16[8,64,2...) custom-call(bf16[16,208,128]{2,1,0:T(8,128)(2,1)} %all_to_all.20.x_ref), custom_call_target="tpu_custom_call" | custom-call | tf_op jit(solution)/shard_map/attend/pallas_call | solution.py:170
  45.5 4.5 %all-to-all-start.1 = ((bf16[16,64,128]{2,1,0:T(8,128)(2,1)}), bf16[16,64,128]{2,1,0:T(8,128)(2,1)S(1)}, u32[]{:S(2)}, u32[]{:S(2)}) async-start(bf16[16,64,128]{2,1,0:T(8,128)(2,1)} %get-tuple-element.32), calls=%async_computation.1 | async-start | bytes 524288 | tf_op jit(solution)/shard_map/all_to_all | solution.py:416
  50.0 0.0 all-reduce.4.cloned.1.call-start
  50.1 0.7 copy.26
  50.8 0.0 copy-done.9
  50.8 0.6 reshape.38.gain_ref
  51.4 0.6 pad.4.wr_ref
  52.0 5.2 %all-to-all-done.1 = bf16[16,64,128]{2,1,0:T(8,128)(2,1)S(1)} async-done(((bf16[16,64,128]{2,1,0:T(8,128)(2,1)}), bf16[16,64,128]{2,1,0:T(8,128)(2,1)S(1)}, u32[]{:S(2)}, u32[]{:S(2)}) %all-to-all-start.1) | async-done | bytes 262176 | tf_op jit(solution)/shard_map/all_to_all | solution.py:416
  57.3 0.7 copy-done.6
  58.0 18.4 %experts.1 = (bf16[128,1024]{1,0:T(8,128)(2,1)}, f32[128,1024]{1,0:T(8,128)}, bf16[1024,128]{1,0:T(8,128)(2,1)}, bf16[1024,1024]{1,0:T(8,128)(2,1)}, bf16[3,1024...) custom-call(bf16[1024,128]{1,0:T(8,128)(2,1)} %bitcast.15, ...), custom_call_target="tpu_custom_call" | custom-call | tf_op jit(solution)/shard_map/experts/pallas_call | solution.py:341
  76.3 12.2 %all_to_all.21.g_ref = bf16[16,64,128]{2,1,0:T(8,128)(2,1)} all-to-all(bf16[16,64,128]{2,1,0:T(8,128)(2,1)} %bitcast.18), channel_id=1, replica_groups=mesh['y'=4,'xh'=2,'z'=4,'xl'=2,'core'=2] {'z','xl','core'}, dimensions={0} | all-to-all | bytes 524288 | tf_op jit(solution)/shard_map/all_to_all | solution.py:416
  88.6 11.1 %attend_back.1 = bf16[16,192,128]{2,1,0:T(8,128)(2,1)} custom-call(bf16[16,208,128]{2,1,0:T(8,128)(2,1)} %all_to_all.20.x_ref, bf16[16,64,128]{2,1,0:T(8,128)(2,1)} %all_to_all.21.g_ref, f32[8,64,256]{2,1,0:T(8,128)} %get-tuple-element.35.full_ref, f32[8,1,256]{2,1,0:T(1,128)} %get-tuple-element.36.log_ref, bf16[8,64,256]{2,1,0:T(8,128)(2,1)} %get-tuple-element.37.q_ref, ...), custom_call_target="tpu_custom_call" | custom-call | tf_op jit(solution)/shard_map/attend_back/pallas_call | solution.py:242
  99.7 17.9 %all_to_all.22.g_ref = bf16[16,192,128]{2,1,0:T(8,128)(2,1)} all-to-all(bf16[16,192,128]{2,1,0:T(8,128)(2,1)} %attend_back.1), channel_id=1, replica_groups=mesh['y'=4,'xh'=2,'z'=4,'xl'=2,'core'=2] {'z','xl','core'}, dimensions={0} | all-to-all | bytes 1572864 | tf_op jit(solution)/shard_map/all_to_all | solution.py:416
  117.6 6.2 %project_back.1 = (bf16[128,1024]{1,0:T(8,128)(2,1)}, bf16[1024,1024]{1,0:T(8,128)(2,1)}, bf16[1024,512]{1,0:T(8,128)(2,1)}, bf16[1024,512]{1,0:T(8,128)(2,1)}, f32[16,1024]{1,0:T(8,128)}) custom-call(bf16[16,192,128]{2,1,0:T(8,128)(2,1)} %all_to_all.22.g_ref, bf16[128,1024]{1,0:T(8,128)(2,1)} %bitcast.14, bf16[1,1024]{1,0:T(2,128)(2,1)} %reshape.36.gain_ref, ...), custom_call_target="tpu_custom_call" | custom-call | tf_op jit(solution)/shard_map/project_back/pallas_call | solution.py:402
  123.8 0.0 all-reduce.4.cloned.1.call-update
  123.8 0.8 copy-done.7
  124.6 0.8 slice.31
  125.4 69.2 %psum.56 = bf16[16,1024]{1,0:T(8,128)(2,1)S(1)} all-reduce(bf16[16,1024]{1,0:T(8,128)(2,1)S(1)} %pad_maximum_fusion), channel_id=1, replica_groups=mesh['y'=4,'xh'=2,'z'=4,'xl'=2,'core'=2] {'y','xh','z','xl','core'}, use_global_device_ids=true, to_apply=%region_0.1 | all-reduce | flops 16384 | bytes 65536 | tf_op jit(solution)/shard_map/psum | solution.py:444
  194.6 0.6 fusion
  195.2 0.6 slice_bitcast_fusion
  195.8 108.6 %all-reduce.4.cloned.1.call-done = (bf16[1024,1024]{1,0:T(8,128)(2,1)}, bf16[1024,512]{1,0:T(8,128)(2,1)}, bf16[1024,512]{1,0:T(8,128)(2,1)}, bf16[1024,1024]{1,...) async-done(((bf16[1024,1024]{1,0:T(8,128)(2,1)}, bf16[1024,512]{1,0:T(8,128)(2,1)}, ...) | async-done | bytes 15728656 | tf_op jit(solution)/shard_map/psum | solution.py:444
  304.5 5.6 %convert_element_type.32 = f32[3,1024,512]{2,1,0:T(8,128)} convert(bf16[3,1024,512]{2,1,0:T(8,128)(2,1)} %get-tuple-element.56) | non-fusion elementwise | flops 1572864 | bytes 9437184 | tf_op jit(solution)/shard_map/convert_element_type | solution.py:444
  310.1 3.6 %convert_element_type.33 = f32[3,1024,512]{2,1,0:T(8,128)} convert(bf16[3,1024,512]{2,1,0:T(8,128)(2,1)S(1)} %copy-done.1) | non-fusion elementwise | flops 1572864 | bytes 9437184 | tf_op jit(solution)/shard_map/convert_element_type | solution.py:444
  313.7 3.5 %convert_element_type.34 = f32[3,512,1024]{2,1,0:T(8,128)} convert(bf16[3,512,1024]{2,1,0:T(8,128)(2,1)S(1)} %copy-done) | non-fusion elementwise | flops 1572864 | bytes 9437184 | tf_op jit(solution)/shard_map/convert_element_type | solution.py:444
  317.2 2.5 convert_element_type.28
  319.7 2.5 convert_element_type.31
  322.2 0.0 copy-done.5
  322.2 1.6 convert_element_type.29
  323.8 1.6 convert_element_type.30
  (21 shorter events, 0.1 us)
Async XLA Ops:
  8.5 41.6 %copy-start.10 = (s32[1,128,2]{1,2,0:T(2,128)S(1)}, s32[1,128,2]{1,2,0:T(2,128)}, u32[]{:S(2)}) copy-start(s32[1,128,2]{1,2,0:T(2,128)} %param.17) | copy-start | bytes 3076
  8.5 42.4 %copy-start.9 = (bf16[1024]{0:T(1024)(128)(2,1)S(1)}, bf16[1024]{0:T(1024)(128)(2,1)}, u32[]{:S(2)}) copy-start(bf16[1024]{0:T(1024)(128)(2,1)} %param.23) | copy-start | bytes 6148
  8.5 43.0 %copy-start.8 = (bf16[1024,3]{0,1:T(4,128)(2,1)S(1)}, bf16[1024,3]{0,1:T(4,128)(2,1)}, u32[]{:S(2)}) copy-start(bf16[1024,3]{0,1:T(4,128)(2,1)} %param.24) | copy-start | bytes 18436
  45.5 11.7 %all-to-all-start.1 = ((bf16[16,64,128]{2,1,0:T(8,128)(2,1)}), bf16[16,64,128]{2,1,0:T(8,128)(2,1)S(1)}, u32[]{:S(2)}, u32[]{:S(2)}) async-start(bf16[16,64,128]{2,1,0:T(8,128)(2,1)} %get-tuple-element.32), calls=%async_computation.1 | async-start | bytes 524288 | tf_op jit(solution)/shard_map/all_to_all | solution.py:416
  50.0 254.5 %all-reduce.4.cloned.1.call-start = ((), (), s32[]{:S(2)}) async-start(), calls=%async_computation.4 | async-start | bytes 31457280 | tf_op jit(solution)/shard_map/psum | solution.py:444
  57.3 0.7 copy-start.6
  123.8 0.8 copy-start.7
  304.5 5.6 %copy-start.1 = (bf16[3,1024,512]{2,1,0:T(8,128)(2,1)S(1)}, bf16[3,1024,512]{2,1,0:T(8,128)(2,1)}, u32[]{:S(2)}) copy-start(bf16[3,1024,512]{2,1,0:T(8,128)(2,1)} %get-tuple-element.57) | copy-start | bytes 9437188
  310.1 3.6 %copy-start = (bf16[3,512,1024]{2,1,0:T(8,128)(2,1)S(1)}, bf16[3,512,1024]{2,1,0:T(8,128)(2,1)}, u32[]{:S(2)}) copy-start(bf16[3,512,1024]{2,1,0:T(8,128)(2,1)} %get-tuple-element.58) | copy-start | bytes 9437188
  313.7 3.5 %copy-start.3 = (bf16[1024,1024]{1,0:T(8,128)(2,1)S(1)}, bf16[1024,1024]{1,0:T(8,128)(2,1)}, u32[]{:S(2)}) copy-start(bf16[1024,1024]{1,0:T(8,128)(2,1)} %get-tuple-element.52) | copy-start | bytes 6291460
  317.2 2.5 copy-start.2
  319.7 2.5 copy-start.5
  322.2 1.6 copy-start.4
Sparse Core Ops, SparseCore 0:
  123.9 180.5 all-reduce.3

commit v2 on v1

v2 whole, which is shorter than its diff:
```python
import math

import jax
import jax.numpy as jnp
from jax import lax
from jax.experimental import pallas as pl
from jax.experimental.pallas import tpu as pltpu
from jax.sharding import Mesh
from jax.sharding import PartitionSpec as P

BF = jnp.bfloat16
F32 = jnp.float32
D = 1024
HQ = 16
HK = 8
HD = 64
FF = 512
EXPERTS = 3
T = 128
S = 2048
BLK = 256
NB = S // BLK
HALF = HD // 2
PAY = 3 * HD + 16
FC = 256
NF = FF // FC
NC = 8
NR = 16
FS = FF // NC
GU = 2 * FS * EXPERTS
ACTS = 3 * FS * EXPERTS
PIECE = 96
PART = 3 * PIECE
MINE = 2 * PIECE

EPSILON = 1e-06
THETA_BASE = 10000.0
SOFT_SCALE = 0.125
NEG_FILL = -1e30

AXES = ("y", "xh", "z", "xl", "core")
ROWS = ("y", "xh")
SEQ = ("z", "xl", "core")
CHIPS = ("z", "xl")
REST = ("y", "xh", "core")
RING = ("y", "core")
PLANE = ("z", "xh", "xl")
ALL = ("y", "z", "xh", "xl", "core")

NN = (((1,), (0,)), ((), ()))
NT = (((1,), (1,)), ((), ()))
TN = (((0,), (0,)), ((), ()))


def dot(a, b, dims=NN):
    return lax.dot_general(a, b, dims, preferred_element_type=F32)


def cost(us):
    return pl.CostEstimate(flops=int(us * 1e9), bytes_accessed=1 << 20, transcendentals=0)


def swap(a):
    return jnp.transpose(a, (1, 0))


def project_kernel(tok_ref, seg_ref, gain_ref, wq_ref, wk_ref, wv_ref, out_ref):
    x = tok_ref[...].astype(F32)
    inverse = lax.rsqrt(jnp.mean(x * x, axis=1, keepdims=True) + EPSILON)
    normed = (x * inverse * gain_ref[...].astype(F32)).astype(BF)
    ids = jnp.broadcast_to(seg_ref[...].astype(F32), (16, T)).astype(BF)
    for h in range(HQ):
        out_ref[h, 3 * HD :, :] = ids
    for j in range(4):
        q = swap(dot(normed, wq_ref[:, 256 * j : 256 * (j + 1)])).astype(BF)
        for i in range(4):
            out_ref[4 * j + i, 0:HD, :] = q[HD * i : HD * (i + 1)]
    for w_ref, at in ((wk_ref, HD), (wv_ref, 2 * HD)):
        for j in range(2):
            a = swap(dot(normed, w_ref[:, 256 * j : 256 * (j + 1)])).astype(BF)
            for i in range(4):
                part = a[HD * i : HD * (i + 1)]
                head = 2 * (4 * j + i)
                out_ref[head, at : at + HD, :] = part
                out_ref[head + 1, at : at + HD, :] = part


def project(tokens, segment, gain, w_query, w_key, w_value):
    return pl.pallas_call(
        project_kernel,
        out_shape=jax.ShapeDtypeStruct((HQ, PAY, T), BF),
        cost_estimate=cost(4),
        name="project",
    )(tokens, segment, gain, w_query, w_key, w_value)


def starts_of(x_ref):
    ids = x_ref[:, 3 * HD :, :].astype(F32)
    counts = [
        (jnp.sum(jnp.where(ids == float(s), 1.0, 0.0)) * (1.0 / 16)).astype(jnp.int32)
        for s in range(3)
    ]
    first = counts[0]
    second = first + counts[1]
    return first, second, second + counts[2]


def start_at(index, bounds):
    b1, b2, b3 = bounds
    return jnp.where(index >= b3, b3, jnp.where(index >= b2, b2, jnp.where(index >= b1, b1, 0)))


def joined(ref, i, at):
    return jnp.concatenate([ref[2 * i, at : at + HD, :], ref[2 * i + 1, at : at + HD, :]], axis=1)


def by_core(place_ref, a):
    even = place_ref[0] == 0
    low, high = a[:, :T], a[:, T:]
    return jnp.where(even, low, high).astype(BF), jnp.where(even, high, low).astype(BF)


def allowed_of(i, j, bounds):
    query = i * BLK + lax.broadcasted_iota(jnp.int32, (1, BLK), 1)
    start = start_at(query, bounds)
    key = j * BLK + lax.broadcasted_iota(jnp.int32, (BLK, BLK), 0)
    return (key >= start) & (key <= query)


def attend_kernel(place_ref, x_ref, att_ref, keep_ref, send_ref, full_ref, log_ref, q_ref, k_ref, cos_ref, sin_ref, kt_ref, v_ref):
    bounds = starts_of(x_ref)
    frequency = jnp.exp(
        lax.broadcasted_iota(jnp.int32, (HALF, 1), 0).astype(F32)
        * (-2.0 * math.log(THETA_BASE) / HD)
    )

    def turn_block(i, carry):
        index = i * BLK + lax.broadcasted_iota(jnp.int32, (1, BLK), 1)
        positions = (index - start_at(index, bounds)).astype(F32)
        angles = positions * frequency
        cosine, sine = jnp.cos(angles), jnp.sin(angles)
        cos_ref[i] = cosine
        sin_ref[i] = sine

        def turned(at):
            a = joined(x_ref, i, at).astype(F32)
            low, high = a[:HALF], a[HALF:]
            return jnp.concatenate(
                [low * cosine - high * sine, high * cosine + low * sine], axis=0
            )

        q_ref[i] = (turned(0).astype(BF).astype(F32) * SOFT_SCALE).astype(BF)
        k = turned(HD)
        k_ref[i] = k.astype(BF)
        kt_ref[i] = swap(k).astype(BF)
        v_ref[i] = joined(x_ref, i, 2 * HD)
        return carry

    lax.fori_loop(0, NB, turn_block, 0)

    def query_block(i, carry):
        first = start_at(i * BLK, bounds) // BLK
        q = q_ref[i]

        def key_block(j, running):
            top, total, acc = running
            scores = jnp.where(allowed_of(i, j, bounds), dot(kt_ref[j], q), NEG_FILL)
            new_top = jnp.maximum(top, jnp.max(scores, axis=0, keepdims=True))
            weights = jnp.exp(scores - new_top)
            scale = jnp.exp(top - new_top)
            total = total * scale + jnp.sum(weights, axis=0, keepdims=True)
            acc = acc * scale + dot(v_ref[j], weights.astype(BF))
            return new_top, total, acc

        begin = (
            jnp.full((1, BLK), NEG_FILL, F32),
            jnp.zeros((1, BLK), F32),
            jnp.zeros((HD, BLK), F32),
        )
        begin = key_block(i, begin)
        top, total, acc = lax.fori_loop(first, i, key_block, begin)
        attended = acc / total
        log_ref[i] = top + jnp.log(total)
        full_ref[i] = attended
        low = attended.astype(BF)
        att_ref[2 * i] = low[:, :T]
        att_ref[2 * i + 1] = low[:, T:]
        keep_ref[i], send_ref[i] = by_core(place_ref, attended)
        return carry

    lax.fori_loop(0, NB, query_block, 0)


PLACE = pl.BlockSpec(memory_space=pltpu.SMEM)


def in_vmem(count):
    return [pl.BlockSpec(memory_space=pltpu.VMEM)] * count


def attend(place, received):
    return pl.pallas_call(
        attend_kernel,
        in_specs=[PLACE] + in_vmem(1),
        out_shape=(
            jax.ShapeDtypeStruct((HQ, HD, T), BF),
            jax.ShapeDtypeStruct((NC, HD, T), BF),
            jax.ShapeDtypeStruct((NC, HD, T), BF),
            jax.ShapeDtypeStruct((NB, HD, BLK), F32),
            jax.ShapeDtypeStruct((NB, 1, BLK), F32),
            jax.ShapeDtypeStruct((NB, HD, BLK), BF),
            jax.ShapeDtypeStruct((NB, HD, BLK), BF),
            jax.ShapeDtypeStruct((NB, HALF, BLK), F32),
            jax.ShapeDtypeStruct((NB, HALF, BLK), F32),
        ),
        scratch_shapes=[pltpu.VMEM((NB, BLK, HD), BF), pltpu.VMEM((NB, HD, BLK), BF)],
        cost_estimate=cost(13),
        name="attend",
    )(place, received)


def attend_back_kernel(
    place_ref, x_ref, g_ref, full_ref, log_ref, q_ref, k_ref, cos_ref, sin_ref, keep_ref, send_ref,
    kt_ref, vt_ref, dk_ref, dv_ref,
):
    bounds = starts_of(x_ref)

    def prepare(i, carry):
        kt_ref[i] = swap(k_ref[i].astype(F32)).astype(BF)
        vt_ref[i] = swap(joined(x_ref, i, 2 * HD).astype(F32)).astype(BF)
        dk_ref[i] = jnp.zeros((HD, BLK), F32)
        dv_ref[i] = jnp.zeros((HD, BLK), F32)
        return carry

    lax.fori_loop(0, NB, prepare, 0)

    def turn_back(i, a):
        cosine, sine = cos_ref[i], sin_ref[i]
        low, high = a[:HALF], a[HALF:]
        return jnp.concatenate([low * cosine + high * sine, high * cosine - low * sine], axis=0)

    def put(i, at, a):
        rows = slice(at, at + HD)
        keep_ref[i, rows, :], send_ref[i, rows, :] = by_core(place_ref, a)

    def query_block(i, carry):
        first = start_at(i * BLK, bounds) // BLK
        q = q_ref[i]
        grad = joined(g_ref, i, 0)
        delta = jnp.sum(grad.astype(F32) * full_ref[i], axis=0, keepdims=True)
        log_total = log_ref[i]

        def key_block(j, dq):
            scores = dot(kt_ref[j], q)
            p = jnp.where(allowed_of(i, j, bounds), jnp.exp(scores - log_total), 0.0)
            dp = dot(vt_ref[j], grad)
            ds = (p * (dp - delta)).astype(BF)
            dv_ref[j] += dot(grad, p.astype(BF), NT)
            dk_ref[j] += dot(q, ds, NT)
            return dq + dot(k_ref[j], ds)

        dq = lax.fori_loop(first, i + 1, key_block, jnp.zeros((HD, BLK), F32))
        put(i, 0, turn_back(i, dq * SOFT_SCALE))
        return carry

    lax.fori_loop(0, NB, query_block, 0)

    def finish(i, carry):
        put(i, HD, turn_back(i, dk_ref[i]))
        put(i, 2 * HD, dv_ref[i])
        return carry

    lax.fori_loop(0, NB, finish, 0)


def attend_back(place, received, grad, full, log_total, q, k, cosine, sine):
    return pl.pallas_call(
        attend_back_kernel,
        in_specs=[PLACE] + in_vmem(8),
        out_shape=(
            jax.ShapeDtypeStruct((NC, 3 * HD, T), BF),
            jax.ShapeDtypeStruct((NC, 3 * HD, T), BF),
        ),
        scratch_shapes=[
            pltpu.VMEM((NB, BLK, HD), BF),
            pltpu.VMEM((NB, BLK, HD), BF),
            pltpu.VMEM((NB, HD, BLK), F32),
            pltpu.VMEM((NB, HD, BLK), F32),
        ],
        cost_estimate=cost(13),
        name="attend_back",
    )(place, received, grad, full, log_total, q, k, cosine, sine)


def normed_kernel(tok_ref, gain_ref, out_ref):
    x = tok_ref[...].astype(F32)
    inverse = lax.rsqrt(jnp.mean(x * x, axis=1, keepdims=True) + EPSILON)
    out_ref[...] = swap(x * inverse * gain_ref[...].astype(F32)).astype(BF)


def normed_columns(tokens, gain):
    return pl.pallas_call(
        normed_kernel, out_shape=jax.ShapeDtypeStruct((D, T), BF), cost_estimate=cost(2), name="normed_columns"
    )(tokens, gain)


def resid_kernel(
    att_ref, tok_ref, routes_ref, gain_ref, wr_ref, wo_ref, resid_ref, moe_ref, moe_t_ref, combine_ref
):
    attended = swap(att_ref[...].astype(F32)).astype(BF)
    resid = tok_ref[...].astype(F32) + dot(attended, wo_ref[...])
    inverse = lax.rsqrt(jnp.mean(resid * resid, axis=1, keepdims=True) + EPSILON)
    normed = resid * inverse * gain_ref[...].astype(F32)
    moe_low = normed.astype(BF)
    resid_ref[...] = resid
    moe_ref[...] = moe_low
    moe_t_ref[...] = swap(normed).astype(BF)
    logits = dot(moe_low, wr_ref[...], NT)
    lane = lax.broadcasted_iota(jnp.int32, (T, T), 1)
    r0, r1 = routes_ref[:, 0:1], routes_ref[:, 1:2]
    l0 = jnp.sum(jnp.where(lane[:, :8] == r0, logits, 0.0), axis=1, keepdims=True)
    l1 = jnp.sum(jnp.where(lane[:, :8] == r1, logits, 0.0), axis=1, keepdims=True)
    top = jnp.maximum(l0, l1)
    e0, e1 = jnp.exp(l0 - top), jnp.exp(l1 - top)
    total = e0 + e1
    combine_ref[...] = jnp.where(lane == r0, e0 / total, 0.0) + jnp.where(
        lane == r1, e1 / total, 0.0
    )


def residual(attended, tokens, routes, gain, w_router, w_output):
    return pl.pallas_call(
        resid_kernel,
        out_shape=(
            jax.ShapeDtypeStruct((T, D), F32),
            jax.ShapeDtypeStruct((T, D), BF),
            jax.ShapeDtypeStruct((D, T), BF),
            jax.ShapeDtypeStruct((T, T), F32),
        ),
        cost_estimate=cost(4),
        name="residual",
    )(attended, tokens, routes, gain, w_router, w_output)


def experts_kernel(
    resid_ref, moe_ref, combine_ref, cot_ref, gain_ref, wr_ref, wo_ref, wg_ref, wu_ref, wd_ref,
    out_ref, resid_grad_ref, grad_att_ref, grad_t_ref, acts_ref, small_ref,
    mix_ref, moe_grad_ref, cgrad_ref,
):
    e, f = pl.program_id(0), pl.program_id(1)
    lane = lax.broadcasted_iota(jnp.int32, (T, T), 1)

    @pl.when((e == 0) & (f == 0))
    def _():
        mix_ref[...] = resid_ref[...]
        moe_grad_ref[...] = jnp.zeros_like(moe_grad_ref)
        cgrad_ref[...] = jnp.zeros_like(cgrad_ref)

    moe_low = moe_ref[...]
    grad_out = cot_ref[...].astype(F32)
    combine = jnp.sum(jnp.where(lane == e, combine_ref[...], 0.0), axis=1, keepdims=True)
    expert_grad = (combine * grad_out).astype(BF)
    gate = dot(moe_low, wg_ref[0])
    up = dot(moe_low, wu_ref[0])
    act_grad = dot(expert_grad, wd_ref[0], NT)
    sig = 1.0 / (1.0 + jnp.exp(-gate))
    silu = gate * sig
    act_low = (silu * up).astype(BF)
    down = dot(act_low, wd_ref[0])
    mix_ref[...] += combine * down
    cgrad_ref[...] += jnp.where(lane == e, jnp.sum(grad_out * down, axis=1, keepdims=True), 0.0)
    gate_grad = act_grad * up * (sig * (1.0 + gate * (1.0 - sig)))
    up_grad = act_grad * silu
    moe_grad_ref[...] += dot(gate_grad.astype(BF), wg_ref[0], NT) + dot(
        up_grad.astype(BF), wu_ref[0], NT
    )
    gate_t = swap(gate_grad).astype(BF)
    up_t = swap(up_grad).astype(BF)
    act_t = swap(combine * act_low.astype(F32)).astype(BF)
    at_gu = pl.multiple_of(2 * FS * e, FS)
    at_down = pl.multiple_of(GU + FS * e, FS)
    for i in range(FC // FS):
        j = f * (FC // FS) + i
        acts_ref[j, pl.ds(at_gu, FS), :] = gate_t[FS * i : FS * (i + 1)]
        acts_ref[j, pl.ds(at_gu + FS, FS), :] = up_t[FS * i : FS * (i + 1)]
        acts_ref[j, pl.ds(at_down, FS), :] = act_t[FS * i : FS * (i + 1)]

    @pl.when((e == EXPERTS - 1) & (f == NF - 1))
    def _():
        out_ref[...] = mix_ref[...].astype(BF)
        weights, cgrad = combine_ref[...], cgrad_ref[...]
        mean = jnp.sum(weights * cgrad, axis=1, keepdims=True)
        logit_grad = (weights * (cgrad - mean)).astype(BF)
        small_ref[0:8, :] = dot(logit_grad, moe_low, TN)[0:8]
        moe_grad = moe_grad_ref[...] + dot(logit_grad[:, 0:8], wr_ref[...])
        resid = resid_ref[...]
        inverse = lax.rsqrt(jnp.mean(resid * resid, axis=1, keepdims=True) + EPSILON)
        n = resid * inverse
        small_ref[8:16, :] = jnp.broadcast_to(jnp.sum(moe_grad * n, axis=0, keepdims=True), (8, D))
        scaled = moe_grad * gain_ref[...].astype(F32)
        resid_grad = grad_out + inverse * (
            scaled - n * jnp.mean(n * scaled, axis=1, keepdims=True)
        )
        resid_grad_ref[...] = resid_grad
        grad_t_ref[...] = swap(resid_grad).astype(BF)
        grad_att_ref[...] = dot(wo_ref[...], resid_grad.astype(BF), NT).astype(BF)


def experts(resid, moe_low, combine, cotangent, gain, w_router, w_output, w_gate, w_up, w_down):
    def whole(*shape):
        return pl.BlockSpec(shape, lambda e, f: (0,) * len(shape))

    def columns():
        return pl.BlockSpec((1, D, FC), lambda e, f: (e, 0, f))

    def rows():
        return pl.BlockSpec((1, FC, D), lambda e, f: (e, f, 0))

    return pl.pallas_call(
        experts_kernel,
        grid=(EXPERTS, NF),
        in_specs=[
            whole(T, D), whole(T, D), whole(T, T), whole(T, D), whole(1, D), whole(8, D),
            whole(D, D), columns(), columns(), rows(),
        ],
        out_specs=(
            whole(T, D), whole(T, D), whole(D, T), whole(D, T), whole(NC, ACTS, T), whole(16, D),
        ),
        out_shape=(
            jax.ShapeDtypeStruct((T, D), BF),
            jax.ShapeDtypeStruct((T, D), F32),
            jax.ShapeDtypeStruct((D, T), BF),
            jax.ShapeDtypeStruct((D, T), BF),
            jax.ShapeDtypeStruct((NC, ACTS, T), BF),
            jax.ShapeDtypeStruct((16, D), F32),
        ),
        scratch_shapes=[
            pltpu.VMEM((T, D), F32),
            pltpu.VMEM((T, D), F32),
            pltpu.VMEM((T, T), F32),
        ],
        cost_estimate=cost(13),
        name="experts",
    )(resid, moe_low, combine, cotangent, gain, w_router, w_output, w_gate, w_up, w_down)


def side_by_side(ref, i, j):
    return jnp.concatenate([ref[i], ref[j]], axis=1)


def expert_weights_kernel(acts_ref, moe_ref, cot_ref, out_ref, wide_ref, down_ref):
    for b in range(0, NC, 2):
        acts = side_by_side(acts_ref, b, b + 1)
        wide = dot(side_by_side(moe_ref, b, b + 1), acts[0:GU], NT)
        down = dot(acts[GU:], jnp.concatenate([cot_ref[b], cot_ref[b + 1]], axis=0))
        if b == 0:
            wide_ref[...] = wide
            down_ref[...] = down
        else:
            wide_ref[...] += wide
            down_ref[...] += down
    for i in range(NR):
        for e in range(EXPERTS):
            out_ref[i, 64 * e : 64 * (e + 1), :] = wide_ref[
                64 * i : 64 * (i + 1), 128 * e : 128 * (e + 1)
            ].astype(BF)
        half, lanes = 96 * (i % 2), 128 * (i // 2)
        out_ref[i, 192:288, :] = down_ref[half : half + 96, lanes : lanes + 128].astype(BF)


def expert_weights(acts, moe, cotangent):
    return pl.pallas_call(
        expert_weights_kernel,
        out_shape=jax.ShapeDtypeStruct((NR, PART, T), BF),
        scratch_shapes=[pltpu.VMEM((D, GU), F32), pltpu.VMEM((FS * EXPERTS, D), F32)],
        cost_estimate=cost(5),
        name="expert_weights",
    )(acts, moe, cotangent)


def project_weights_kernel(
    place_ref, mine_ref, theirs_ref, att_ref, att_other_ref,
    normed0_ref, normed1_ref, normed2_ref, normed3_ref, grad_ref,
    back_ref, out_ref, heads_ref,
):
    core, z, xl = place_ref[0], place_ref[1], place_ref[2]
    own = pl.ds(pl.multiple_of(HD * core, HD), HD)
    partner = pl.ds(pl.multiple_of(HD * (1 - core), HD), HD)
    for b in range(NC):
        back_ref[b, own, :] = mine_ref[b, 0:HD, :]
        back_ref[b, partner, :] = theirs_ref[b, 0:HD, :]
        back_ref[b, 2 * HD :, :] = (
            mine_ref[b, HD:, :].astype(F32) + theirs_ref[b, HD:, :].astype(F32)
        ).astype(BF)
        heads_ref[b, own, :] = att_ref[b]
        heads_ref[b, partner, :] = att_other_ref[b]
    total = jnp.zeros((D, 4 * HD), F32)
    o = jnp.zeros((2 * HD, D), F32)
    for back, normed_ref in enumerate((normed0_ref, normed1_ref, normed2_ref, normed3_ref)):
        chip = 2 * ((z - back) & 3)
        near, far = chip + xl, chip + 1 - xl
        total += dot(side_by_side(normed_ref, 0, 1), side_by_side(back_ref, near, far), NT)
    for b in range(0, NC, 2):
        mine, later = 2 * b + core, 2 * b + 2 + core
        o += dot(side_by_side(heads_ref, b, b + 1), side_by_side(grad_ref, mine, later), NT)
    low, o_low = total.astype(BF), o.astype(BF)
    for i in range(NR):
        out_ref[i, 0:64, :] = low[64 * i : 64 * (i + 1), 0:128]
        out_ref[i, 64:128, :] = low[64 * i : 64 * (i + 1), 128:256]
        half, lanes = 64 * (i % 2), 128 * (i // 2)
        out_ref[i, 128:192, :] = o_low[half : half + 64, lanes : lanes + 128]


def project_weights(place, mine, theirs, attended, attended_other, normed, grad):
    return pl.pallas_call(
        project_weights_kernel,
        in_specs=[PLACE] + in_vmem(9),
        out_shape=(
            jax.ShapeDtypeStruct((NC, 4 * HD, T), BF),
            jax.ShapeDtypeStruct((NR, MINE, T), BF),
        ),
        scratch_shapes=[pltpu.VMEM((NC, 2 * HD, T), BF)],
        cost_estimate=cost(5),
        name="project_weights",
    )(place, mine, theirs, attended, attended_other, *normed, grad)


def project_back_kernel(
    g_ref, tok_ref, gain_ref, wq_ref, wk_ref, wv_ref, resid_grad_ref, small_ref, out_ref, sums_ref
):
    x = tok_ref[...].astype(F32)
    gain = gain_ref[...].astype(F32)
    inverse = lax.rsqrt(jnp.mean(x * x, axis=1, keepdims=True) + EPSILON)
    n = x * inverse

    def rows(first, last):
        a = g_ref[:, first:last, :]
        return swap(a.reshape(NC * (last - first), T).astype(F32)).astype(BF)

    normed_grad = dot(rows(0, 2 * HD), wq_ref[...], NT)
    normed_grad += dot(rows(2 * HD, 3 * HD), wk_ref[...], NT)
    normed_grad += dot(rows(3 * HD, 4 * HD), wv_ref[...], NT)
    scaled = normed_grad * gain
    out_ref[...] = (
        resid_grad_ref[...] + inverse * (scaled - n * jnp.mean(n * scaled, axis=1, keepdims=True))
    ).astype(BF)
    gain_grad = jnp.sum(normed_grad * n, axis=0, keepdims=True)
    row = lax.broadcasted_iota(jnp.int32, (8, D), 0)
    sums_ref[...] = jnp.where(
        row < EXPERTS, small_ref[0:8], jnp.where(row == EXPERTS, small_ref[8:16], gain_grad)
    )


def project_back(grads, tokens, gain, w_query, w_key, w_value, resid_grad, small):
    return pl.pallas_call(
        project_back_kernel,
        out_shape=(jax.ShapeDtypeStruct((T, D), BF), jax.ShapeDtypeStruct((8, D), F32)),
        cost_estimate=cost(5),
        name="project_back",
    )(grads, tokens, gain, w_query, w_key, w_value, resid_grad, small)


def assemble_kernel(
    g0_ref, g1_ref, g2_ref, p0_ref, p1_ref,
    q_ref, k_ref, v_ref, o_ref, g_ref, u_ref, d_ref,
):
    core = pl.program_id(2)
    low_half = lax.broadcasted_iota(jnp.int32, (64, T), 1) < 64

    def rows(refs, pick, first, last):
        found = []
        for at, ref in enumerate(refs):
            begin, end = max(first - PIECE * at, 0), min(last - PIECE * at, PIECE)
            if begin < end:
                found.append(pick(ref)[begin:end])
        whole = found[0] if len(found) == 1 else jnp.concatenate(found, axis=0)
        return whole.astype(F32)

    def expert_rows(j, first, last):
        refs = (g0_ref, g1_ref, g2_ref)
        return rows(refs, lambda ref: ref[j // 2, 0, 0, 0, j % 2], first, last)

    def project_rows(j, first, last):
        return rows((p0_ref, p1_ref), lambda ref: ref[0, j // 2, 0, j % 2, 0], first, last)

    def turned(a):
        return pltpu.roll(a, 64, 1)

    for m in range(NC // 2):
        tile = slice(T * m, T * (m + 1))
        for e in range(EXPERTS):
            a, b = (expert_rows(2 * m + i, 64 * e, 64 * (e + 1)) for i in range(2))
            g_ref[e, :, tile] = jnp.where(low_half, a, turned(b))
            u_ref[e, :, tile] = jnp.where(low_half, turned(a), b)
        a, b = (project_rows(2 * m + i, 64, 128) for i in range(2))
        k_ref[:, tile] = jnp.where(low_half, a, turned(b))
        v_ref[:, tile] = jnp.where(low_half, turned(a), b)
    for j in range(NC):
        q_ref[:, T * j : T * (j + 1)] = project_rows(j, 0, 64)
        o_ref[j, core] = project_rows(j, 128, 192)

    @pl.when(core == 0)
    def _():
        for j in range(NC):
            a = expert_rows(j, 192, 288)
            d_ref[0, j] = a[0:64]
            d_ref[1, j, 0:32] = a[64:96]

    @pl.when(core == 1)
    def _():
        for j in range(NC):
            a = expert_rows(j, 192, 288)
            d_ref[1, j, 32:64] = a[0:32]
            d_ref[2, j] = a[32:96]


def assemble(gathered):
    def experts_of(at):
        return pl.BlockSpec((4, 1, 1, 1, 2, PIECE, T), lambda a, b, c: (0, a, b, c, 0, at, 0))

    def project_of(at):
        return pl.BlockSpec((1, 4, 1, 2, 1, PIECE, T), lambda a, b, c: (a, 0, b, 0, c, at, 0))

    def rows(width):
        return pl.BlockSpec((64, width), lambda a, b, c: (4 * a + 2 * b + c, 0))

    def stack():
        return pl.BlockSpec((EXPERTS, 64, FF), lambda a, b, c: (0, 4 * a + 2 * b + c, 0))

    return pl.pallas_call(
        assemble_kernel,
        grid=(4, 2, 2),
        in_specs=[experts_of(0), experts_of(1), experts_of(2), project_of(3), project_of(4)],
        out_specs=(
            rows(D), rows(FF), rows(FF),
            pl.BlockSpec((NC, 2, HD, T), lambda a, b, c: (0, 0, 0, 2 * a + b)),
            stack(), stack(),
            pl.BlockSpec((EXPERTS, NC, FS, T), lambda a, b, c: (0, 0, 0, 2 * a + b)),
        ),
        out_shape=(
            jax.ShapeDtypeStruct((D, D), F32),
            jax.ShapeDtypeStruct((D, FF), F32),
            jax.ShapeDtypeStruct((D, FF), F32),
            jax.ShapeDtypeStruct((NC, 2, HD, D), F32),
            jax.ShapeDtypeStruct((EXPERTS, D, FF), F32),
            jax.ShapeDtypeStruct((EXPERTS, D, FF), F32),
            jax.ShapeDtypeStruct((EXPERTS, NC, FS, D), F32),
        ),
        cost_estimate=cost(20),
        name="assemble",
    )(*(gathered,) * 5)


def exchange(array, axes=SEQ):
    return lax.all_to_all(array, axes, 0, 0, tiled=True)


def swapped(array, axis):
    return lax.ppermute(array, axis, [(0, 1), (1, 0)])


def gather(array, axes):
    return lax.all_gather(array, axes, axis=0)


def spread_sum(part, axes, count):
    return jnp.sum(exchange(jnp.broadcast_to(part[None], (count, *part.shape)), axes), axis=0)


def part_sum(parts, axes):
    return jnp.sum(exchange(parts, axes).astype(F32), axis=0).astype(BF)


def after(array, *others):
    return lax.optimization_barrier((array, *others))


def shards(
    tokens, cotangent, segment, routes, attn_gain, w_query, w_key, w_value, w_output,
    expert_norm_gain, w_router, w_gate, w_up, w_down,
):
    tokens, cotangent = tokens[0], cotangent[0]
    attn_gain = attn_gain.reshape(1, D)
    expert_norm_gain = expert_norm_gain.reshape(1, D)
    router_rows = jnp.pad(w_router.T, ((0, 8 - EXPERTS), (0, 0)))
    place = jnp.stack([lax.axis_index(a) for a in ("core", "z", "xl")]).astype(jnp.int32)

    cot_all = gather(cotangent, RING)
    received = exchange(project(tokens, segment, attn_gain, w_query, w_key, w_value))
    normed = normed_columns(tokens, attn_gain)
    normed = jnp.stack([normed, swapped(normed, "xl")])
    received, normed = after(received, normed)
    normed_all = [normed] + [
        lax.ppermute(normed, "z", [(i, (i + back) % 4) for i in range(4)]) for back in (1, 2, 3)
    ]
    attended, att_mine, att_sent, full, log_total, q, k, cosine, sine = attend(place, received)
    attended, cot_all = after(attended, cot_all)
    attended = exchange(attended).reshape(D, T)
    att_theirs = swapped(att_sent, "core")
    resid, moe_low, moe_columns, combine = residual(
        attended, tokens, routes[0], expert_norm_gain, router_rows, w_output
    )
    moe_all = gather(moe_columns, RING)
    output, resid_grad, grad_att, grad_columns, acts, small = experts(
        resid, moe_low, combine, cotangent, expert_norm_gain, router_rows, w_output,
        w_gate, w_up, w_down,
    )
    acts = exchange(acts, RING)
    grad_all = gather(grad_columns, SEQ)
    grad_att, acts, moe_all = after(grad_att, acts, moe_all)
    grad_att = exchange(grad_att.reshape(HQ, HD, T))
    parts = expert_weights(acts, moe_all, cot_all)
    mine, sent = attend_back(place, received, grad_att, full, log_total, q, k, cosine, sine)
    expert_part = part_sum(parts, PLANE)
    grads, weights = project_weights(
        place, mine, swapped(sent, "core"), att_mine, att_theirs, normed_all, grad_all
    )
    project_part = part_sum(weights, REST)
    gathered = gather(jnp.concatenate([expert_part, project_part], axis=0), ALL)
    grads, project_part = after(grads, project_part)
    token_grad, small = project_back(
        exchange(grads, CHIPS), tokens, attn_gain, w_query, w_key, w_value, resid_grad, small
    )
    small = spread_sum(spread_sum(small, REST, NR), CHIPS, NC)
    dwq, dwk, dwv, dwo, dwg, dwu, dwd = assemble(
        gathered.reshape(4, 4, 2, 2, 2, PART + MINE, T)
    )
    return (
        output[None], token_grad[None], small[4], dwq, dwk, dwv, dwo.reshape(D, D), small[3],
        small[:EXPERTS].T, dwg, dwu, dwd.reshape(EXPERTS, FF, D),
    )


def solution(mesh):
    fine = Mesh(mesh.devices.reshape(4, 2, 4, 2, 2), AXES)
    by_token = P(ROWS, SEQ, None)
    return jax.shard_map(
        shards,
        mesh=fine,
        in_specs=(by_token, by_token, P(ROWS, SEQ), by_token) + (P(),) * 10,
        out_specs=(by_token, by_token) + (P(),) * 10,
        check_vma=False,
    )
```

time: 333 us -> 289 us (0.87)
  blocking collectives: 121 us -> 39.5 us
  starting transfers between devices: 4.52 us -> 40.5 us
  Pallas kernels: 51.5 us -> 81.7 us
  other arithmetic: 20.9 us -> 2.58 us
  waiting for transfers between devices: 114 us -> 102 us
    psum x1 -> x0, waiting for transfers between devices: 109 us -> none  [shards(): lax.psum((dwq, dwk, dwv, dwo, dwg, dwu, dwd, small), AXES)]
    psum x1 -> x0, blocking collectives: 69.2 us -> none  [shards(): lax.psum((dwq, dwk, dwv, dwo, dwg, dwu, dwd, small), AXES)]
    all_gather x0 -> x4, waiting for transfers between devices: none -> 47.6 us  [gather(): return lax.all_gather(array, axes, axis=0)]
    all_to_all x1 -> x6, waiting for transfers between devices: 5.22 us -> 38.7 us  [exchange(): return lax.all_to_all(array, axes, 0, 0, tiled=True)]
    all_to_all x1 -> x6, starting transfers between devices: 4.49 us -> 37 us  [exchange(): return lax.all_to_all(array, axes, 0, 0, tiled=True)]
    pallas_call x3 -> x8, Pallas kernels: 41.3 us -> 72.7 us  [the longest x1 20.7 us: assemble(): pl.pallas_call(assemble_kernel, grid=(4, 2, 2), in_specs=[experts_of(0),...]
    convert_element_type x8 -> x0, other arithmetic: 20.9 us -> none  [shards(): a.astype(F32)]
    ppermute x0 -> x6, waiting for transfers between devices: none -> 15 us  [the longest x3 14.9 us: swapped(): return lax.ppermute(array, axis, [(0, 1), (1, 0)])]
  transfers between devices with their start and end apart: 2 -> 16, of which waited for: 2 -> 9; matrix products, arithmetic and copies ran while one was open for 1% -> 2% of each run, Pallas kernels for 0% -> 20%
where the time goes in v2:
time: 289 us; the launch traced here: 287 us
  waiting for transfers between devices  102 us (35%)
  Pallas kernels  81.7 us (28%)
  starting transfers between devices  40.5 us (14%)
  blocking collectives  39.5 us (14%)
  between operations  13.9 us (5%)
  local copies, waits for them, and re-layouts  6.91 us (2%)
    all_gather x4, waiting for transfers between devices, gather(): return lax.all_gather(array, axes, axis=0)  47.6 us
    all_to_all x3, blocking collectives, exchange(): return lax.all_to_all(array, axes, 0, 0, tiled=True)  39.5 us
    all_to_all x6, waiting for transfers between devices, exchange(): return lax.all_to_all(array, axes, 0, 0, tiled=True)  38.7 us
    all_to_all x6, starting transfers between devices, exchange(): return lax.all_to_all(array, axes, 0, 0, tiled=True)  37 us
    pallas_call x1, Pallas kernels, assemble(): pl.pallas_call(assemble_kernel, grid=(4, 2, 2), in_specs=[experts_of(0),...  20.7 us
    ppermute x3, waiting for transfers between devices, swapped(): return lax.ppermute(array, axis, [(0, 1), (1, 0)])  14.9 us
    pallas_call x1, Pallas kernels, experts(): pl.pallas_call(experts_kernel, grid=(EXPERTS, NF), in_specs=[whole(T, D),...  12.6 us
    pallas_call x1, Pallas kernels, attend(): pl.pallas_call(attend_kernel, in_specs=[PLACE] + in_vmem(1), out_shape=(j...  11.9 us
  transfers between devices with their start and end apart: 16, of which 9 were waited for; matrix products, arithmetic and copies ran while one was open for 2% of the time, Pallas kernels for 20%

profile of v2, /device:TPU:1, one launch (start us, length us, event | category | flops | bytes accessed | tf_op | source)
XLA Modules:
  0.0 287.2 jit_solution(13399280146309404124)
XLA Ops:
  7.9 1.3 reshape.47.gain_ref
  9.2 4.1 %project.1 = bf16[16,208,128]{2,1,0:T(8,128)(2,1)} custom-call(bf16[128,1024]{1,0:T(8,128)(2,1)} %bitcast.40, s32[1,128]{1,0:T(1,128)} %seg_ref.1, bf16[1,1024]{1,0:T(2,128)(2,1)} %reshape.47.gain_ref, bf16[1024,1024]{1,0:T(8,128)(2,1)} %wq_ref.3, bf16[1024,512]{1,0:T(8,128)(2,1)} %wk_ref.3, bf16[1024,512]{1,0:T(8,128)(2,1)} %wv_ref.3), custom_call_target="tpu_custom_call" | custom-call | flops 4000000000 | bytes 1048576 | tf_op jit(solution)/shard_map/project/pallas_call | solution.py:89
  13.3 7.8 %all-to-all-start = ((bf16[16,208,128]{2,1,0:T(8,128)(2,1)}), bf16[16,208,128]{2,1,0:T(8,128)(2,1)S(1)}, u32[]{:S(2)}, u32[]{:S(2)}) async-start(bf16[16,208,128]{2,1,0:T(8,128)(2,1)} %project.1), calls=%async_computation | async-start | bytes 1703936 | tf_op jit(solution)/shard_map/all_to_all | solution.py:655
  21.0 1.9 normed_columns.1
  22.9 1.4 collective-permute-start
  24.9 13.3 %collective-permute-done = bf16[1024,128]{1,0:T(8,128)(2,1)S(1)} collective-permute-done((bf16[1024,128]{1,0:T(8,128)(2,1)}, bf16[1024,128]{1,0:T(8,128)(2,1)S(1)}, u32[]{:S(2)}, u32[]{:S(2)}) %collective-permute-start) | collective-permute-done | bytes 262176 | tf_op jit(solution)/shard_map/ppermute | solution.py:659
  38.2 1.0 pad_maximum_fusion.normed0_ref
  39.2 0.9 copy-done.1
  40.1 11.9 %attend.1 = (bf16[16,64,128]{2,1,0:T(8,128)(2,1)}, bf16[8,64,128]{2,1,0:T(8,128)(2,1)}, bf16[8,64,128]{2,1,0:T(8,128)(2,1)}, f32[8,64,256]{2,1,0:T(8,128)}, f32[...) custom-call(s32[3]{0:T(128)} %pad_add_fusion.place_ref, ...), custom_call_target="tpu_custom_call" | custom-call | flops 12999999488 | bytes 1048576 | tf_op jit(solution)/shard_map/attend/pallas_call | solution.py:202
  52.0 5.2 %all-to-all-start.1 = ((bf16[16,64,128]{2,1,0:T(8,128)(2,1)}), bf16[16,64,128]{2,1,0:T(8,128)(2,1)S(1)}, u32[]{:S(2)}, u32[]{:S(2)}) async-start(bf16[16,64,128]{2,1,0:T(8,128)(2,1)} %get-tuple-element.54), calls=%async_computation.1 | async-start | bytes 524288 | tf_op jit(solution)/shard_map/all_to_all | solution.py:655
  59.2 5.2 %all-to-all-done.1 = bf16[16,64,128]{2,1,0:T(8,128)(2,1)S(1)} async-done(((bf16[16,64,128]{2,1,0:T(8,128)(2,1)}), bf16[16,64,128]{2,1,0:T(8,128)(2,1)S(1)}, u32[]{:S(2)}, u32[]{:S(2)}) %all-to-all-start.1) | async-done | bytes 262176 | tf_op jit(solution)/shard_map/all_to_all | solution.py:655
  65.1 3.4 %residual.1 = (f32[128,1024]{1,0:T(8,128)}, bf16[128,1024]{1,0:T(8,128)(2,1)}, bf16[1024,128]{1,0:T(8,128)(2,1)}, f32[128,128]{1,0:T(8,128)}) custom-call(bf16[1024,128]{1,0:T(8,128)(2,1)} %bitcast.29, bf16[128,1024]{1,0:T(8,128)(2,1)} %bitcast.42, s32[128,2]{1,0:T(8,128)} %bitcast.32, bf16[1,1024]{1,0:T(2,128)(2,1)} %reshape.49.gain_ref, ...), custom_call_target="tpu_custom_call" | custom-call | flops 4000000000 | bytes 1048576 | tf_op jit(solution)/shard_map/residual/pallas_call | solution.py:332
  68.6 12.6 %experts.1 = (bf16[128,1024]{1,0:T(8,128)(2,1)}, f32[128,1024]{1,0:T(8,128)}, bf16[1024,128]{1,0:T(8,128)(2,1)}, bf16[1024,128]{1,0:T(8,128)(2,1)}, bf16[8,576,128]{2,1,0:T(8,128)(2,1)}, /*index=5*/f32[16,1024]{1,0:T(8,128)}) custom-call(f32[128,1024]{1,0:T(8,128)} %get-tuple-element.55.resid_ref, bf16[128,1024]{1,0:T(8,128)(2,1)} %get-tuple-element.56.moe_ref, ...), custom_call_target="tpu_custom_call" | custom-call | flops 12999999488 | bytes 1048576 | tf_op jit(solution)/shard_map/experts/pallas_call | solution.py:419
  81.2 7.1 %all-to-all-start.2 = ((bf16[8,576,128]{2,1,0:T(8,128)(2,1)}), bf16[8,576,128]{2,1,0:T(8,128)(2,1)S(1)}, u32[]{:S(2)}, u32[]{:S(2)}) async-start(bf16[8,576,128]{2,1,0:T(8,128)(2,1)} %get-tuple-element.60), calls=%async_computation.2 | async-start | bytes 2359296 | tf_op jit(solution)/shard_map/all_to_all | solution.py:655
  89.8 15.2 %all-to-all-done.2.acts_ref = bf16[8,576,128]{2,1,0:T(8,128)(2,1)S(1)} async-done(((bf16[8,576,128]{2,1,0:T(8,128)(2,1)}), bf16[8,576,128]{2,1,0:T(8,128)(2,1)S(1)}, u32[]{:S(2)}, u32[]{:S(2)}) %all-to-all-start.2) | async-done | bytes 1179680 | tf_op jit(solution)/shard_map/all_to_all | solution.py:655
  105.0 5.2 %all-to-all-start.3 = ((bf16[16,64,128]{2,1,0:T(8,128)(2,1)}), bf16[16,64,128]{2,1,0:T(8,128)(2,1)S(1)}, u32[]{:S(2)}, u32[]{:S(2)}) async-start(bf16[16,64,128]{2,1,0:T(8,128)(2,1)} %bitcast.28), calls=%async_computation.3 | async-start | bytes 524288 | tf_op jit(solution)/shard_map/all_to_all | solution.py:655
  110.2 5.5 %expert_weights.1 = bf16[16,288,128]{2,1,0:T(8,128)(2,1)} custom-call(bf16[8,576,128]{2,1,0:T(8,128)(2,1)} %copy-done, bf16[8,1024,128]{2,1,0:T(8,128)(2,1)} %bitcast.39, bf16[8,128,1024]{2,1,0:T(8,128)(2,1)} %all-gather.8.cloned.1.call-done.cot_ref), custom_call_target="tpu_custom_call" | custom-call | flops 5000000000 | bytes 1048576 | tf_op jit(solution)/shard_map/expert_weights/pallas_call | solution.py:472
  115.7 4.1 %all-to-all-done.3.g_ref = bf16[16,64,128]{2,1,0:T(8,128)(2,1)S(1)} async-done(((bf16[16,64,128]{2,1,0:T(8,128)(2,1)}), bf16[16,64,128]{2,1,0:T(8,128)(2,1)S(1)}, u32[]{:S(2)}, u32[]{:S(2)}) %all-to-all-start.3) | async-done | bytes 262176 | tf_op jit(solution)/shard_map/all_to_all | solution.py:655
  119.8 4.5 %all-to-all-start.8 = ((bf16[16,288,128]{2,1,0:T(8,128)(2,1)}), bf16[16,288,128]{2,1,0:T(8,128)(2,1)S(1)}, u32[]{:S(2)}, u32[]{:S(2)}) async-start(bf16[16,288,128]{2,1,0:T(8,128)(2,1)} %expert_weights.1), calls=%async_computation.8 | async-start | bytes 2359296 | tf_op jit(solution)/shard_map/all_to_all | solution.py:655
  124.4 11.2 %attend_back.1 = (bf16[8,192,128]{2,1,0:T(8,128)(2,1)}, bf16[8,192,128]{2,1,0:T(8,128)(2,1)}) custom-call(s32[3]{0:T(128)} %pad_add_fusion.place_ref, bf16[16,208,128]{2,1,0:T(8,128)(2,1)} %copy-done.1, bf16[16,64,128]{2,1,0:T(8,128)(2,1)} %copy-done.4, f32[8,64,256]{2,1,0:T(8,128)} %get-tuple-element.63.full_ref, f32[8,1,256]{2,1,0:T(1,128)} %get-tuple-element.64.log_ref, ...), custom_call_target="tpu_custom_call" | custom-call | flops 12999999488 | bytes 1048576 | tf_op jit(solution)/shard_map/attend_back/pallas_call | solution.py:277
  136.1 1.5 collective-permute-done.2.att_other_ref
  137.8 16.3 %all-gather.12.cloned.1.call-done = bf16[16384,128]{1,0:T(8,128)(2,1)} async-done(((bf16[1024,128]{1,0:T(8,128)(2,1)}), bf16[16384,128]{1,0:T(8,128)(2,1)}) %all-gather.12.cloned.1.call-update) | async-done | bytes 4194320 | tf_op jit(solution)/shard_map/all_gather | solution.py:663
  154.2 5.5 %project_weights.1 = (bf16[8,256,128]{2,1,0:T(8,128)(2,1)}, bf16[16,192,128]{2,1,0:T(8,128)(2,1)}) custom-call(s32[3]{0:T(128)} %pad_add_fusion.place_ref, bf16[8,192,128]{2,1,0:T(8,128)(2,1)} %get-tuple-element.69.mine_ref, bf16[8,192,128]{2,1,0:T(8,128)(2,1)} %collective-permute-done.1.theirs_ref, bf16[8,64,128]{2,1,0:T(8,128)(2,1)} %get-tuple-element.71.att_ref, ...), custom_call_target="tpu_custom_call" | custom-call | flops 5000000000 | bytes 1048576 | tf_op jit(solution)/shard_map/project_weights/pallas_call | solution.py:515
  159.7 7.2 %all-to-all-start.4 = ((bf16[16,192,128]{2,1,0:T(8,128)(2,1)}), bf16[16,192,128]{2,1,0:T(8,128)(2,1)S(1)}, u32[]{:S(2)}, u32[]{:S(2)}) async-start(bf16[16,192,128]{2,1,0:T(8,128)(2,1)} %get-tuple-element.76), calls=%async_computation.4 | async-start | bytes 1572864 | tf_op jit(solution)/shard_map/all_to_all | solution.py:655
  167.1 14.2 %all-to-all-done.4 = bf16[16,192,128]{2,1,0:T(8,128)(2,1)S(1)} async-done(((bf16[16,192,128]{2,1,0:T(8,128)(2,1)}), bf16[16,192,128]{2,1,0:T(8,128)(2,1)S(1)}, u32[]{:S(2)}, u32[]{:S(2)}) %all-to-all-start.4) | async-done | bytes 786464 | tf_op jit(solution)/shard_map/all_to_all | solution.py:655
  182.1 12.4 %all_to_all.45.g_ref = bf16[8,256,128]{2,1,0:T(8,128)(2,1)} all-to-all(bf16[8,256,128]{2,1,0:T(8,128)(2,1)S(1)} %copy-done.3), channel_id=1, replica_groups=mesh['y'=4,'xh'=2,'z'=4,'xl'=2,'core'=2] {'z','xl'}, dimensions={0} | all-to-all | bytes 1048576 | tf_op jit(solution)/shard_map/all_to_all | solution.py:655
  194.4 5.0 %project_back.1 = (bf16[128,1024]{1,0:T(8,128)(2,1)}, f32[8,1024]{1,0:T(8,128)}) custom-call(bf16[8,256,128]{2,1,0:T(8,128)(2,1)} %all_to_all.45.g_ref, bf16[128,1024]{1,0:T(8,128)(2,1)} %bitcast.43, bf16[1,1024]{1,0:T(2,128)(2,1)} %reshape.47.gain_ref, bf16[1024,1024]{1,0:T(8,128)(2,1)} %wq_ref.3, bf16[1024,512]{1,0:T(8,128)(2,1)} %wk_ref.3, ...), custom_call_target="tpu_custom_call" | custom-call | flops 5000000000 | bytes 1048576 | tf_op jit(solution)/shard_map/project_back/pallas_call | solution.py:555
  199.4 0.8 broadcast_in_dim.20
  200.2 18.5 %all_to_all.46 = f32[16,8,1024]{2,1,0:T(8,128)S(1)} all-to-all(f32[16,8,1024]{2,1,0:T(8,128)S(1)} %broadcast_in_dim.20), channel_id=1, replica_groups=mesh['y'=4,'xh'=2,'z'=4,'xl'=2,'core'=2] {'y','xh','core'}, dimensions={0} | all-to-all | bytes 1048576 | tf_op jit(solution)/shard_map/all_to_all | solution.py:655
  218.8 8.6 %all_to_all.47 = f32[8,8,1024]{2,1,0:T(8,128)S(1)} all-to-all(f32[8,8,1024]{2,1,0:T(8,128)S(1)} %broadcast_in_dim.21), channel_id=1, replica_groups=mesh['y'=4,'xh'=2,'z'=4,'xl'=2,'core'=2] {'z','xl'}, dimensions={0} | all-to-all | bytes 524288 | tf_op jit(solution)/shard_map/all_to_all | solution.py:655
  228.6 31.3 %all-gather.14.cloned.1.call-done = bf16[61440,128]{1,0:T(8,128)(2,1)} async-done(((bf16[480,128]{1,0:T(8,128)(2,1)}), bf16[61440,128]{1,0:T(8,128)(2,1)}) %all-gather.14.cloned.1.call-update) | async-done | bytes 15728656 | tf_op jit(solution)/shard_map/all_gather | solution.py:663
  259.9 20.7 %assemble.1 = (f32[1024,1024]{1,0:T(8,128)}, f32[1024,512]{1,0:T(8,128)}, f32[1024,512]{1,0:T(8,128)}, f32[8,2,64,1024]{3,2,1,0:T(8,128)}, f32[3,1024,512]{2,1,0...) custom-call(bf16[4,4,2,2,2,480,128]{6,5,4,3,2,1,0:T(8,128)(2,1)} %bitcast.22, ...), custom_call_target="tpu_custom_call" | custom-call | flops 20000000000 | bytes 1048576 | tf_op jit(solution)/shard_map/assemble/pallas_call | solution.py:630
  (58 shorter events, 8.6 us)
Async XLA Ops:
  7.2 44.9 %all-gather.8.cloned.1.call-start = ((), (), s32[]{:S(2)}) async-start(), calls=%async_computation.9 | async-start | bytes 2359296 | tf_op jit(solution)/shard_map/all_gather | solution.py:663
  13.3 26.0 %all-to-all-start = ((bf16[16,208,128]{2,1,0:T(8,128)(2,1)}), bf16[16,208,128]{2,1,0:T(8,128)(2,1)S(1)}, u32[]{:S(2)}, u32[]{:S(2)}) async-start(bf16[16,208,128]{2,1,0:T(8,128)(2,1)} %project.1), calls=%async_computation | async-start | bytes 1703936 | tf_op jit(solution)/shard_map/all_to_all | solution.py:655
  22.9 15.2 %collective-permute-start = (bf16[1024,128]{1,0:T(8,128)(2,1)}, bf16[1024,128]{1,0:T(8,128)(2,1)S(1)}, u32[]{:S(2)}, u32[]{:S(2)}) collective-permute-start(bf16[1024,128]{1,0:T(8,128)(2,1)} %normed_columns.1), channel_id=1, source_target_pairs={{0,2},{2,0},{1,3},{3,1},{4,6},{6,4},{5,7},{7,5},{8,10},{10,8},{9,1... | collective-permute-start | bytes 786440 | tf_op jit(solution)/shard_map/ppermute | solution.py:659
  39.2 50.3 %copy-start.2 = (bf16[2,1024,128]{2,1,0:T(8,128)(2,1)}, bf16[2,1024,128]{2,1,0:T(8,128)(2,1)S(1)}, u32[]{:S(2)}) copy-start(bf16[2,1024,128]{2,1,0:T(8,128)(2,1)S(1)} %pad_maximum_fusion.normed0_ref) | copy-start | bytes 1572868
  39.2 18.1 %copy-start.7 = (bf16[1024]{0:T(1024)(128)(2,1)S(1)}, bf16[1024]{0:T(1024)(128)(2,1)}, u32[]{:S(2)}) copy-start(bf16[1024]{0:T(1024)(128)(2,1)} %param.23) | copy-start | bytes 6148
  39.2 18.7 %copy-start.8 = (s32[1,128,2]{1,2,0:T(2,128)S(1)}, s32[1,128,2]{1,2,0:T(2,128)}, u32[]{:S(2)}) copy-start(s32[1,128,2]{1,2,0:T(2,128)} %param.17) | copy-start | bytes 3076
  39.2 19.4 %copy-start.6 = (bf16[1024,3]{0,1:T(4,128)(2,1)S(1)}, bf16[1024,3]{0,1:T(4,128)(2,1)}, u32[]{:S(2)}) copy-start(bf16[1024,3]{0,1:T(4,128)(2,1)} %param.24) | copy-start | bytes 18436
  39.2 0.9 copy-start.1
  52.0 12.3 %all-to-all-start.1 = ((bf16[16,64,128]{2,1,0:T(8,128)(2,1)}), bf16[16,64,128]{2,1,0:T(8,128)(2,1)S(1)}, u32[]{:S(2)}, u32[]{:S(2)}) async-start(bf16[16,64,128]{2,1,0:T(8,128)(2,1)} %get-tuple-element.54), calls=%async_computation.1 | async-start | bytes 524288 | tf_op jit(solution)/shard_map/all_to_all | solution.py:655
  57.2 47.8 %all-gather.10.cloned.1.call-start = ((), (), s32[]{:S(2)}) async-start(), calls=%async_computation.10 | async-start | bytes 2359296 | tf_op jit(solution)/shard_map/all_gather | solution.py:663
  64.4 0.7 copy-start.5
  68.5 85.6 %all-gather.12.cloned.1.call-start = ((), (), s32[]{:S(2)}) async-start(), calls=%async_computation.11 | async-start | bytes 4456448 | tf_op jit(solution)/shard_map/all_gather | solution.py:663
  81.2 23.8 %all-to-all-start.2 = ((bf16[8,576,128]{2,1,0:T(8,128)(2,1)}), bf16[8,576,128]{2,1,0:T(8,128)(2,1)S(1)}, u32[]{:S(2)}, u32[]{:S(2)}) async-start(bf16[8,576,128]{2,1,0:T(8,128)(2,1)} %get-tuple-element.60), calls=%async_computation.2 | async-start | bytes 2359296 | tf_op jit(solution)/shard_map/all_to_all | solution.py:655
  88.3 49.3 %collective-permute-start.5 = (bf16[2,1024,128]{2,1,0:T(8,128)(2,1)S(1)}, bf16[2,1024,128]{2,1,0:T(8,128)(2,1)S(1)}, u32[]{:S(2)}, u32[]{:S(2)}) collective-permute-start(bf16[2,1024,128]{2,1,0:T(8,128)(2,1)S(1)} %pad_maximum_fusion.normed0_ref), channel_id=1, source_target_pairs={{0,12},{4,0},{8,4},{12,8},{1,13},{5,1},{9,5},{13,9},{2,14},{6,2},{... | collective-permute-start | bytes 1572872 | tf_op jit(solution)/shard_map/ppermute | solution.py:694
  88.8 48.8 %collective-permute-start.4 = (bf16[2,1024,128]{2,1,0:T(8,128)(2,1)S(1)}, bf16[2,1024,128]{2,1,0:T(8,128)(2,1)S(1)}, u32[]{:S(2)}, u32[]{:S(2)}) collective-permute-start(bf16[2,1024,128]{2,1,0:T(8,128)(2,1)S(1)} %pad_maximum_fusion.normed0_ref), channel_id=1, source_target_pairs={{0,8},{4,12},{8,0},{12,4},{1,9},{5,13},{9,1},{13,5},{2,10},{6,14},... | collective-permute-start | bytes 1572872 | tf_op jit(solution)/shard_map/ppermute | solution.py:694
  89.4 48.2 %collective-permute-start.3 = (bf16[2,1024,128]{2,1,0:T(8,128)(2,1)S(1)}, bf16[2,1024,128]{2,1,0:T(8,128)(2,1)S(1)}, u32[]{:S(2)}, u32[]{:S(2)}) collective-permute-start(bf16[2,1024,128]{2,1,0:T(8,128)(2,1)S(1)} %pad_maximum_fusion.normed0_ref), channel_id=1, source_target_pairs={{0,4},{4,8},{8,12},{12,0},{1,5},{5,9},{9,13},{13,1},{2,6},{6,10},{... | collective-permute-start | bytes 1572872 | tf_op jit(solution)/shard_map/ppermute | solution.py:694
  105.0 5.2 %copy-start = (bf16[8,576,128]{2,1,0:T(8,128)(2,1)}, bf16[8,576,128]{2,1,0:T(8,128)(2,1)S(1)}, u32[]{:S(2)}) copy-start(bf16[8,576,128]{2,1,0:T(8,128)(2,1)S(1)} %all-to-all-done.2.acts_ref) | copy-start | bytes 3538948
  105.0 14.9 %all-to-all-start.3 = ((bf16[16,64,128]{2,1,0:T(8,128)(2,1)}), bf16[16,64,128]{2,1,0:T(8,128)(2,1)S(1)}, u32[]{:S(2)}, u32[]{:S(2)}) async-start(bf16[16,64,128]{2,1,0:T(8,128)(2,1)} %bitcast.28), calls=%async_computation.3 | async-start | bytes 524288 | tf_op jit(solution)/shard_map/all_to_all | solution.py:655
  119.8 4.5 %copy-start.4 = (bf16[16,64,128]{2,1,0:T(8,128)(2,1)}, bf16[16,64,128]{2,1,0:T(8,128)(2,1)S(1)}, u32[]{:S(2)}) copy-start(bf16[16,64,128]{2,1,0:T(8,128)(2,1)S(1)} %all-to-all-done.3.g_ref) | copy-start | bytes 786436
  119.8 39.8 %all-to-all-start.8 = ((bf16[16,288,128]{2,1,0:T(8,128)(2,1)}), bf16[16,288,128]{2,1,0:T(8,128)(2,1)S(1)}, u32[]{:S(2)}, u32[]{:S(2)}) async-start(bf16[16,288,128]{2,1,0:T(8,128)(2,1)} %expert_weights.1), calls=%async_computation.8 | async-start | bytes 2359296 | tf_op jit(solution)/shard_map/all_to_all | solution.py:655
  135.6 2.3 collective-permute-start.1
  135.6 2.0 collective-permute-start.2
  137.6 16.5 %copy-start.12 = (bf16[8,64,128]{2,1,0:T(8,128)(2,1)}, bf16[8,64,128]{2,1,0:T(8,128)(2,1)S(1)}, u32[]{:S(2)}) copy-start(bf16[8,64,128]{2,1,0:T(8,128)(2,1)S(1)} %collective-permute-done.2.att_other_ref) | copy-start | bytes 393220
  137.6 16.5 %copy-start.9 = (bf16[2,1024,128]{2,1,0:T(8,128)(2,1)}, bf16[2,1024,128]{2,1,0:T(8,128)(2,1)S(1)}, u32[]{:S(2)}) copy-start(bf16[2,1024,128]{2,1,0:T(8,128)(2,1)S(1)} %collective-permute-done.5.normed3_ref) | copy-start | bytes 1572868
  137.6 16.5 %copy-start.10 = (bf16[2,1024,128]{2,1,0:T(8,128)(2,1)}, bf16[2,1024,128]{2,1,0:T(8,128)(2,1)S(1)}, u32[]{:S(2)}) copy-start(bf16[2,1024,128]{2,1,0:T(8,128)(2,1)S(1)} %collective-permute-done.4.normed2_ref) | copy-start | bytes 1572868
  137.7 16.5 %copy-start.11 = (bf16[2,1024,128]{2,1,0:T(8,128)(2,1)}, bf16[2,1024,128]{2,1,0:T(8,128)(2,1)S(1)}, u32[]{:S(2)}) copy-start(bf16[2,1024,128]{2,1,0:T(8,128)(2,1)S(1)} %collective-permute-done.3.normed1_ref) | copy-start | bytes 1572868
  159.7 22.4 %copy-start.3 = (bf16[8,256,128]{2,1,0:T(8,128)(2,1)S(1)}, bf16[8,256,128]{2,1,0:T(8,128)(2,1)}, u32[]{:S(2)}) copy-start(bf16[8,256,128]{2,1,0:T(8,128)(2,1)} %get-tuple-element.77) | copy-start | bytes 1572868
  159.7 21.6 %all-to-all-start.4 = ((bf16[16,192,128]{2,1,0:T(8,128)(2,1)}), bf16[16,192,128]{2,1,0:T(8,128)(2,1)S(1)}, u32[]{:S(2)}, u32[]{:S(2)}) async-start(bf16[16,192,128]{2,1,0:T(8,128)(2,1)} %get-tuple-element.76), calls=%async_computation.4 | async-start | bytes 1572864 | tf_op jit(solution)/shard_map/all_to_all | solution.py:655
  166.9 93.0 %all-gather.14.cloned.1.call-start = ((), (), s32[]{:S(2)}) async-start(), calls=%async_computation.12 | async-start | bytes 15851520 | tf_op jit(solution)/shard_map/all_gather | solution.py:663
Sparse Core Ops, SparseCore 0:
  9.7 28.7 all-gather.7
  68.6 28.7 all-gather.9
  99.2 54.9 all-gather.11
  182.2 77.6 all-gather.13

commit v3 on v2

--- a/solution.py
+++ b/solution.py
@@ -1,3 +1,4 @@
+import functools
 import math
 
 import jax
@@ -20,9 +21,10 @@
 S = 2048
 BLK = 256
 NB = S // BLK
+WINDOW = 1024 // BLK + 1
 HALF = HD // 2
 PAY = 3 * HD + 16
-FC = 256
+FC = 512
 NF = FF // FC
 NC = 8
 NR = 16
@@ -41,8 +43,8 @@
 AXES = ("y", "xh", "z", "xl", "core")
 ROWS = ("y", "xh")
 SEQ = ("z", "xl", "core")
-CHIPS = ("z", "xl")
-REST = ("y", "xh", "core")
+COLUMN = ("z", "core")
+REST = ("y", "xh", "xl")
 RING = ("y", "core")
 PLANE = ("z", "xh", "xl")
 ALL = ("y", "z", "xh", "xl", "core")
@@ -50,6 +52,10 @@
 NN = (((1,), (0,)), ((), ()))
 NT = (((1,), (1,)), ((), ()))
 TN = (((0,), (0,)), ((), ()))
+
+
+def device_of(head):
+    return head // 4 * 4 + head % 2 * 2 + head // 2 % 2
 
 
 def dot(a, b, dims=NN):
@@ -74,15 +80,15 @@
     for j in range(4):
         q = swap(dot(normed, wq_ref[:, 256 * j : 256 * (j + 1)])).astype(BF)
         for i in range(4):
-            out_ref[4 * j + i, 0:HD, :] = q[HD * i : HD * (i + 1)]
+            out_ref[device_of(4 * j + i), 0:HD, :] = q[HD * i : HD * (i + 1)]
     for w_ref, at in ((wk_ref, HD), (wv_ref, 2 * HD)):
         for j in range(2):
             a = swap(dot(normed, w_ref[:, 256 * j : 256 * (j + 1)])).astype(BF)
             for i in range(4):
                 part = a[HD * i : HD * (i + 1)]
                 head = 2 * (4 * j + i)
-                out_ref[head, at : at + HD, :] = part
-                out_ref[head + 1, at : at + HD, :] = part
+                out_ref[device_of(head), at : at + HD, :] = part
+                out_ref[device_of(head + 1), at : at + HD, :] = part
 
 
 def project(tokens, segment, gain, w_query, w_key, w_value):
@@ -114,17 +120,32 @@
     return jnp.concatenate([ref[2 * i, at : at + HD, :], ref[2 * i + 1, at : at + HD, :]], axis=1)
 
 
-def by_core(place_ref, a):
-    even = place_ref[0] == 0
-    low, high = a[:, :T], a[:, T:]
-    return jnp.where(even, low, high).astype(BF), jnp.where(even, high, low).astype(BF)
-
-
-def allowed_of(i, j, bounds):
+def put_pair(place_ref, keep_ref, send_ref, i, rows, a):
+    low = a.astype(BF)
+    for ref, half in ((keep_ref, place_ref[2]), (send_ref, 1 - place_ref[2])):
+
+        @pl.when((i & 1) == half)
+        def _(ref=ref):
+            ref[2 * (i // 2), rows, :] = low[:, :T]
+            ref[2 * (i // 2) + 1, rows, :] = low[:, T:]
+
+
+def windowed(i, bounds, body):
+    blocks = i + 1 - start_at(i * BLK, bounds) // BLK
+    for window in range(1, WINDOW + 1):
+        pl.when(blocks == window)(functools.partial(body, window))
+
+
+def masks_of(i, bounds):
     query = i * BLK + lax.broadcasted_iota(jnp.int32, (1, BLK), 1)
-    start = start_at(query, bounds)
-    key = j * BLK + lax.broadcasted_iota(jnp.int32, (BLK, BLK), 0)
-    return (key >= start) & (key <= query)
+    first = start_at(query, bounds) - i * BLK
+    key = lax.broadcasted_iota(jnp.int32, (BLK, BLK), 0)
+
+    def allowed(back):
+        inside = key >= first + back * BLK
+        return inside & (key <= query - i * BLK) if back == 0 else inside
+
+    return allowed
 
 
 def attend_kernel(place_ref, x_ref, att_ref, keep_ref, send_ref, full_ref, log_ref, q_ref, k_ref, cos_ref, sin_ref, kt_ref, v_ref):
@@ -156,36 +177,32 @@
         v_ref[i] = joined(x_ref, i, 2 * HD)
         return carry
 
-    lax.fori_loop(0, NB, turn_block, 0)
+    lax.fori_loop(0, NB, turn_block, 0, unroll=True)
 
     def query_block(i, carry):
-        first = start_at(i * BLK, bounds) // BLK
         q = q_ref[i]
-
-        def key_block(j, running):
-            top, total, acc = running
-            scores = jnp.where(allowed_of(i, j, bounds), dot(kt_ref[j], q), NEG_FILL)
-            new_top = jnp.maximum(top, jnp.max(scores, axis=0, keepdims=True))
-            weights = jnp.exp(scores - new_top)
-            scale = jnp.exp(top - new_top)
-            total = total * scale + jnp.sum(weights, axis=0, keepdims=True)
-            acc = acc * scale + dot(v_ref[j], weights.astype(BF))
-            return new_top, total, acc
-
-        begin = (
-            jnp.full((1, BLK), NEG_FILL, F32),
-            jnp.zeros((1, BLK), F32),
-            jnp.zeros((HD, BLK), F32),
-        )
-        begin = key_block(i, begin)
-        top, total, acc = lax.fori_loop(first, i, key_block, begin)
-        attended = acc / total
-        log_ref[i] = top + jnp.log(total)
-        full_ref[i] = attended
-        low = attended.astype(BF)
-        att_ref[2 * i] = low[:, :T]
-        att_ref[2 * i + 1] = low[:, T:]
-        keep_ref[i], send_ref[i] = by_core(place_ref, attended)
+        allowed = masks_of(i, bounds)
+
+        def attend_window(window):
+            scores = [
+                jnp.where(allowed(back), dot(kt_ref[i - back], q), NEG_FILL)
+                for back in range(window)
+            ]
+            top = jnp.max(functools.reduce(jnp.maximum, scores), axis=0, keepdims=True)
+            weights = [jnp.exp(a - top) for a in scores]
+            total = jnp.sum(functools.reduce(jnp.add, weights), axis=0, keepdims=True)
+            acc = functools.reduce(
+                jnp.add, [dot(v_ref[i - back], weights[back].astype(BF)) for back in range(window)]
+            )
+            attended = acc / total
+            log_ref[i] = top + jnp.log(total)
+            full_ref[i] = attended
+            low = attended.astype(BF)
+            att_ref[2 * i] = low[:, :T]
+            att_ref[2 * i + 1] = low[:, T:]
+            put_pair(place_ref, keep_ref, send_ref, i, slice(0, HD), attended)
+
+        windowed(i, bounds, attend_window)
         return carry
 
     lax.fori_loop(0, NB, query_block, 0)
@@ -232,7 +249,7 @@
         dv_ref[i] = jnp.zeros((HD, BLK), F32)
         return carry
 
-    lax.fori_loop(0, NB, prepare, 0)
+    lax.fori_loop(0, NB, prepare, 0, unroll=True)
 
     def turn_back(i, a):
         cosine, sine = cos_ref[i], sin_ref[i]
@@ -240,27 +257,29 @@
         return jnp.concatenate([low * cosine + high * sine, high * cosine - low * sine], axis=0)
 
     def put(i, at, a):
-        rows = slice(at, at + HD)
-        keep_ref[i, rows, :], send_ref[i, rows, :] = by_core(place_ref, a)
+        put_pair(place_ref, keep_ref, send_ref, i, slice(at, at + HD), a)
 
     def query_block(i, carry):
-        first = start_at(i * BLK, bounds) // BLK
         q = q_ref[i]
+        allowed = masks_of(i, bounds)
         grad = joined(g_ref, i, 0)
         delta = jnp.sum(grad.astype(F32) * full_ref[i], axis=0, keepdims=True)
         log_total = log_ref[i]
 
-        def key_block(j, dq):
-            scores = dot(kt_ref[j], q)
-            p = jnp.where(allowed_of(i, j, bounds), jnp.exp(scores - log_total), 0.0)
-            dp = dot(vt_ref[j], grad)
-            ds = (p * (dp - delta)).astype(BF)
-            dv_ref[j] += dot(grad, p.astype(BF), NT)
-            dk_ref[j] += dot(q, ds, NT)
-            return dq + dot(k_ref[j], ds)
-
-        dq = lax.fori_loop(first, i + 1, key_block, jnp.zeros((HD, BLK), F32))
-        put(i, 0, turn_back(i, dq * SOFT_SCALE))
+        def back_window(window):
+            dq = jnp.zeros((HD, BLK), F32)
+            for back in range(window):
+                j = i - back
+                scores = dot(kt_ref[j], q)
+                p = jnp.where(allowed(back), jnp.exp(scores - log_total), 0.0)
+                dp = dot(vt_ref[j], grad)
+                ds = (p * (dp - delta)).astype(BF)
+                dv_ref[j] += dot(grad, p.astype(BF), NT)
+                dk_ref[j] += dot(q, ds, NT)
+                dq += dot(k_ref[j], ds)
+            put(i, 0, turn_back(i, dq * SOFT_SCALE))
+
+        windowed(i, bounds, back_window)
         return carry
 
     lax.fori_loop(0, NB, query_block, 0)
@@ -270,7 +289,7 @@
         put(i, 2 * HD, dv_ref[i])
         return carry
 
-    lax.fori_loop(0, NB, finish, 0)
+    lax.fori_loop(0, NB, finish, 0, unroll=True)
 
 
 def attend_back(place, received, grad, full, log_total, q, k, cosine, sine):
@@ -307,7 +326,8 @@
 def resid_kernel(
     att_ref, tok_ref, routes_ref, gain_ref, wr_ref, wo_ref, resid_ref, moe_ref, moe_t_ref, combine_ref
 ):
-    attended = swap(att_ref[...].astype(F32)).astype(BF)
+    heads = [att_ref[device_of(h)] for h in range(HQ)]
+    attended = swap(jnp.concatenate(heads, axis=0).astype(F32)).astype(BF)
     resid = tok_ref[...].astype(F32) + dot(attended, wo_ref[...])
     inverse = lax.rsqrt(jnp.mean(resid * resid, axis=1, keepdims=True) + EPSILON)
     normed = resid * inverse * gain_ref[...].astype(F32)
@@ -343,7 +363,7 @@
 
 
 def experts_kernel(
-    resid_ref, moe_ref, combine_ref, cot_ref, gain_ref, wr_ref, wo_ref, wg_ref, wu_ref, wd_ref,
+    place_ref, resid_ref, moe_ref, combine_ref, cot_ref, gain_ref, wr_ref, wo_ref, wg_ref, wu_ref, wd_ref,
     out_ref, resid_grad_ref, grad_att_ref, grad_t_ref, acts_ref, small_ref,
     mix_ref, moe_grad_ref, cgrad_ref,
 ):
@@ -379,8 +399,10 @@
     act_t = swap(combine * act_low.astype(F32)).astype(BF)
     at_gu = pl.multiple_of(2 * FS * e, FS)
     at_down = pl.multiple_of(GU + FS * e, FS)
+    core, y = place_ref[0], place_ref[3]
     for i in range(FC // FS):
         j = f * (FC // FS) + i
+        j = 2 * ((j // 2 - y) & 3) + ((j & 1) ^ core)
         acts_ref[j, pl.ds(at_gu, FS), :] = gate_t[FS * i : FS * (i + 1)]
         acts_ref[j, pl.ds(at_gu + FS, FS), :] = up_t[FS * i : FS * (i + 1)]
         acts_ref[j, pl.ds(at_down, FS), :] = act_t[FS * i : FS * (i + 1)]
@@ -403,10 +425,12 @@
         )
         resid_grad_ref[...] = resid_grad
         grad_t_ref[...] = swap(resid_grad).astype(BF)
-        grad_att_ref[...] = dot(wo_ref[...], resid_grad.astype(BF), NT).astype(BF)
-
-
-def experts(resid, moe_low, combine, cotangent, gain, w_router, w_output, w_gate, w_up, w_down):
+        grad_att = dot(wo_ref[...], resid_grad.astype(BF), NT).astype(BF)
+        for h in range(HQ):
+            grad_att_ref[device_of(h)] = grad_att[HD * h : HD * (h + 1)]
+
+
+def experts(place, resid, moe_low, combine, cotangent, gain, w_router, w_output, w_gate, w_up, w_down):
     def whole(*shape):
         return pl.BlockSpec(shape, lambda e, f: (0,) * len(shape))
 
@@ -420,16 +444,17 @@
         experts_kernel,
         grid=(EXPERTS, NF),
         in_specs=[
-            whole(T, D), whole(T, D), whole(T, T), whole(T, D), whole(1, D), whole(8, D),
+            PLACE, whole(T, D), whole(T, D), whole(T, T), whole(T, D), whole(1, D), whole(8, D),
             whole(D, D), columns(), columns(), rows(),
         ],
         out_specs=(
-            whole(T, D), whole(T, D), whole(D, T), whole(D, T), whole(NC, ACTS, T), whole(16, D),
+            whole(T, D), whole(T, D), whole(HQ, HD, T), whole(D, T), whole(NC, ACTS, T),
+            whole(16, D),
         ),
         out_shape=(
             jax.ShapeDtypeStruct((T, D), BF),
             jax.ShapeDtypeStruct((T, D), F32),
-            jax.ShapeDtypeStruct((D, T), BF),
+            jax.ShapeDtypeStruct((HQ, HD, T), BF),
             jax.ShapeDtypeStruct((D, T), BF),
             jax.ShapeDtypeStruct((NC, ACTS, T), BF),
             jax.ShapeDtypeStruct((16, D), F32),
@@ -441,19 +466,25 @@
         ],
         cost_estimate=cost(13),
         name="experts",
-    )(resid, moe_low, combine, cotangent, gain, w_router, w_output, w_gate, w_up, w_down)
+    )(place, resid, moe_low, combine, cotangent, gain, w_router, w_output, w_gate, w_up, w_down)
 
 
 def side_by_side(ref, i, j):
     return jnp.concatenate([ref[i], ref[j]], axis=1)
 
 
-def expert_weights_kernel(acts_ref, moe_ref, cot_ref, out_ref, wide_ref, down_ref):
-    for b in range(0, NC, 2):
-        acts = side_by_side(acts_ref, b, b + 1)
-        wide = dot(side_by_side(moe_ref, b, b + 1), acts[0:GU], NT)
-        down = dot(acts[GU:], jnp.concatenate([cot_ref[b], cot_ref[b + 1]], axis=0))
-        if b == 0:
+def expert_weights_kernel(
+    place_ref, acts0_ref, acts1_ref, acts2_ref, acts3_ref, other_ref, moe_ref, cot_ref,
+    out_ref, wide_ref, down_ref,
+):
+    core, y = place_ref[0], place_ref[3]
+    for back, acts_ref in enumerate((acts0_ref, acts1_ref, acts2_ref, acts3_ref)):
+        chip = 2 * ((y - back) & 3)
+        near, far = chip + core, chip + 1 - core
+        acts = jnp.concatenate([acts_ref[...], other_ref[back]], axis=1)
+        wide = dot(side_by_side(moe_ref, near, far), acts[0:GU], NT)
+        down = dot(acts[GU:], jnp.concatenate([cot_ref[near], cot_ref[far]], axis=0))
+        if back == 0:
             wide_ref[...] = wide
             down_ref[...] = down
         else:
@@ -468,61 +499,79 @@
         out_ref[i, 192:288, :] = down_ref[half : half + 96, lanes : lanes + 128].astype(BF)
 
 
-def expert_weights(acts, moe, cotangent):
+def expert_weights(place, acts, others, moe, cotangent):
     return pl.pallas_call(
         expert_weights_kernel,
+        in_specs=[PLACE] + in_vmem(7),
         out_shape=jax.ShapeDtypeStruct((NR, PART, T), BF),
         scratch_shapes=[pltpu.VMEM((D, GU), F32), pltpu.VMEM((FS * EXPERTS, D), F32)],
         cost_estimate=cost(5),
         name="expert_weights",
-    )(acts, moe, cotangent)
+    )(place, *acts, others, moe, cotangent)
+
+
+def own_rows(half):
+    return pl.ds(pl.multiple_of(HD * half, HD), HD), pl.ds(pl.multiple_of(HD * (1 - half), HD), HD)
 
 
 def project_weights_kernel(
-    place_ref, mine_ref, theirs_ref, att_ref, att_other_ref,
-    normed0_ref, normed1_ref, normed2_ref, normed3_ref, grad_ref,
-    back_ref, out_ref, heads_ref,
-):
-    core, z, xl = place_ref[0], place_ref[1], place_ref[2]
-    own = pl.ds(pl.multiple_of(HD * core, HD), HD)
-    partner = pl.ds(pl.multiple_of(HD * (1 - core), HD), HD)
+    place_ref, mine_ref, theirs_ref, normed_ref, back_ref, out_ref
+):
+    own, partner = own_rows(place_ref[2])
     for b in range(NC):
         back_ref[b, own, :] = mine_ref[b, 0:HD, :]
         back_ref[b, partner, :] = theirs_ref[b, 0:HD, :]
         back_ref[b, 2 * HD :, :] = (
             mine_ref[b, HD:, :].astype(F32) + theirs_ref[b, HD:, :].astype(F32)
         ).astype(BF)
-        heads_ref[b, own, :] = att_ref[b]
-        heads_ref[b, partner, :] = att_other_ref[b]
     total = jnp.zeros((D, 4 * HD), F32)
-    o = jnp.zeros((2 * HD, D), F32)
-    for back, normed_ref in enumerate((normed0_ref, normed1_ref, normed2_ref, normed3_ref)):
-        chip = 2 * ((z - back) & 3)
-        near, far = chip + xl, chip + 1 - xl
-        total += dot(side_by_side(normed_ref, 0, 1), side_by_side(back_ref, near, far), NT)
     for b in range(0, NC, 2):
-        mine, later = 2 * b + core, 2 * b + 2 + core
-        o += dot(side_by_side(heads_ref, b, b + 1), side_by_side(grad_ref, mine, later), NT)
-    low, o_low = total.astype(BF), o.astype(BF)
+        total += dot(side_by_side(normed_ref, b, b + 1), side_by_side(back_ref, b, b + 1), NT)
+    low = total.astype(BF)
     for i in range(NR):
         out_ref[i, 0:64, :] = low[64 * i : 64 * (i + 1), 0:128]
         out_ref[i, 64:128, :] = low[64 * i : 64 * (i + 1), 128:256]
-        half, lanes = 64 * (i % 2), 128 * (i // 2)
-        out_ref[i, 128:192, :] = o_low[half : half + 64, lanes : lanes + 128]
-
-
-def project_weights(place, mine, theirs, attended, attended_other, normed, grad):
+
+
+def project_weights(place, mine, theirs, normed):
     return pl.pallas_call(
         project_weights_kernel,
-        in_specs=[PLACE] + in_vmem(9),
+        in_specs=[PLACE] + in_vmem(3),
         out_shape=(
             jax.ShapeDtypeStruct((NC, 4 * HD, T), BF),
             jax.ShapeDtypeStruct((NR, MINE, T), BF),
         ),
+        cost_estimate=cost(4),
+        name="project_weights",
+    )(place, mine, theirs, normed)
+
+
+def output_weights_kernel(
+    place_ref, att_ref, att_other_ref, grad_ref, parts_ref, out_ref, heads_ref
+):
+    own, partner = own_rows(place_ref[2])
+    o = jnp.zeros((2 * HD, D), F32)
+    for b in range(NC):
+        heads_ref[b, own, :] = att_ref[b]
+        heads_ref[b, partner, :] = att_other_ref[b]
+    for b in range(0, NC, 2):
+        o += dot(side_by_side(heads_ref, b, b + 1), side_by_side(grad_ref, b, b + 1), NT)
+    low = o.astype(BF)
+    for i in range(NR):
+        half, lanes = 64 * (i % 2), 128 * (i // 2)
+        out_ref[i, 0:128, :] = parts_ref[i, 0:128, :]
+        out_ref[i, 128:192, :] = low[half : half + 64, lanes : lanes + 128]
+
+
+def output_weights(place, attended, attended_other, grad, parts):
+    return pl.pallas_call(
+        output_weights_kernel,
+        in_specs=[PLACE] + in_vmem(4),
+        out_shape=jax.ShapeDtypeStruct((NR, MINE, T), BF),
         scratch_shapes=[pltpu.VMEM((NC, 2 * HD, T), BF)],
-        cost_estimate=cost(5),
-        name="project_weights",
-    )(place, mine, theirs, attended, attended_other, *normed, grad)
+        cost_estimate=cost(3),
+        name="output_weights",
+    )(place, attended, attended_other, grad, parts)
 
 
 def project_back_kernel(
@@ -564,7 +613,6 @@
     g0_ref, g1_ref, g2_ref, p0_ref, p1_ref,
     q_ref, k_ref, v_ref, o_ref, g_ref, u_ref, d_ref,
 ):
-    core = pl.program_id(2)
     low_half = lax.broadcasted_iota(jnp.int32, (64, T), 1) < 64
 
     def rows(refs, pick, first, last):
@@ -576,66 +624,62 @@
         whole = found[0] if len(found) == 1 else jnp.concatenate(found, axis=0)
         return whole.astype(F32)
 
-    def expert_rows(j, first, last):
-        refs = (g0_ref, g1_ref, g2_ref)
-        return rows(refs, lambda ref: ref[j // 2, 0, 0, 0, j % 2], first, last)
-
-    def project_rows(j, first, last):
-        return rows((p0_ref, p1_ref), lambda ref: ref[0, j // 2, 0, j % 2, 0], first, last)
-
     def turned(a):
         return pltpu.roll(a, 64, 1)
 
-    for m in range(NC // 2):
-        tile = slice(T * m, T * (m + 1))
-        for e in range(EXPERTS):
-            a, b = (expert_rows(2 * m + i, 64 * e, 64 * (e + 1)) for i in range(2))
-            g_ref[e, :, tile] = jnp.where(low_half, a, turned(b))
-            u_ref[e, :, tile] = jnp.where(low_half, turned(a), b)
-        a, b = (project_rows(2 * m + i, 64, 128) for i in range(2))
-        k_ref[:, tile] = jnp.where(low_half, a, turned(b))
-        v_ref[:, tile] = jnp.where(low_half, turned(a), b)
-    for j in range(NC):
-        q_ref[:, T * j : T * (j + 1)] = project_rows(j, 0, 64)
-        o_ref[j, core] = project_rows(j, 128, 192)
-
-    @pl.when(core == 0)
-    def _():
+    for c in range(2):
+        here = slice(64 * c, 64 * (c + 1))
+
+        def expert_rows(j, first, last, c=c):
+            refs = (g0_ref, g1_ref, g2_ref)
+            return rows(refs, lambda ref: ref[j // 2, 0, 0, c, j % 2], first, last)
+
+        def project_rows(j, first, last, c=c):
+            return rows((p0_ref, p1_ref), lambda ref: ref[0, j // 2, 0, c, j % 2], first, last)
+
+        for m in range(NC // 2):
+            tile = slice(T * m, T * (m + 1))
+            for e in range(EXPERTS):
+                a, b = (expert_rows(2 * m + i, 64 * e, 64 * (e + 1)) for i in range(2))
+                g_ref[e, here, tile] = jnp.where(low_half, a, turned(b))
+                u_ref[e, here, tile] = jnp.where(low_half, turned(a), b)
+            a, b = (project_rows(2 * m + i, 64, 128) for i in range(2))
+            k_ref[here, tile] = jnp.where(low_half, a, turned(b))
+            v_ref[here, tile] = jnp.where(low_half, turned(a), b)
         for j in range(NC):
+            q_ref[here, T * j : T * (j + 1)] = project_rows(j, 0, 64)
+            o_ref[j, c] = project_rows(j, 128, 192)
             a = expert_rows(j, 192, 288)
-            d_ref[0, j] = a[0:64]
-            d_ref[1, j, 0:32] = a[64:96]
-
-    @pl.when(core == 1)
-    def _():
-        for j in range(NC):
-            a = expert_rows(j, 192, 288)
-            d_ref[1, j, 32:64] = a[0:32]
-            d_ref[2, j] = a[32:96]
+            if c == 0:
+                d_ref[0, j] = a[0:64]
+                d_ref[1, j, 0:32] = a[64:96]
+            else:
+                d_ref[1, j, 32:64] = a[0:32]
+                d_ref[2, j] = a[32:96]
 
 
 def assemble(gathered):
     def experts_of(at):
-        return pl.BlockSpec((4, 1, 1, 1, 2, PIECE, T), lambda a, b, c: (0, a, b, c, 0, at, 0))
+        return pl.BlockSpec((4, 1, 1, 2, 2, PIECE, T), lambda a, b: (0, a, b, 0, 0, at, 0))
 
     def project_of(at):
-        return pl.BlockSpec((1, 4, 1, 2, 1, PIECE, T), lambda a, b, c: (a, 0, b, 0, c, at, 0))
+        return pl.BlockSpec((1, 4, 1, 2, 2, PIECE, T), lambda a, b: (a, 0, b, 0, 0, at, 0))
 
     def rows(width):
-        return pl.BlockSpec((64, width), lambda a, b, c: (4 * a + 2 * b + c, 0))
+        return pl.BlockSpec((T, width), lambda a, b: (2 * a + b, 0))
 
     def stack():
-        return pl.BlockSpec((EXPERTS, 64, FF), lambda a, b, c: (0, 4 * a + 2 * b + c, 0))
+        return pl.BlockSpec((EXPERTS, T, FF), lambda a, b: (0, 2 * a + b, 0))
 
     return pl.pallas_call(
         assemble_kernel,
-        grid=(4, 2, 2),
+        grid=(4, 2),
         in_specs=[experts_of(0), experts_of(1), experts_of(2), project_of(3), project_of(4)],
         out_specs=(
             rows(D), rows(FF), rows(FF),
-            pl.BlockSpec((NC, 2, HD, T), lambda a, b, c: (0, 0, 0, 2 * a + b)),
+            pl.BlockSpec((NC, 2, HD, T), lambda a, b: (0, 0, 0, 2 * a + b)),
             stack(), stack(),
-            pl.BlockSpec((EXPERTS, NC, FS, T), lambda a, b, c: (0, 0, 0, 2 * a + b)),
+            pl.BlockSpec((EXPERTS, NC, FS, T), lambda a, b: (0, 0, 0, 2 * a + b)),
         ),
         out_shape=(
             jax.ShapeDtypeStruct((D, D), F32),
@@ -683,45 +727,50 @@
     attn_gain = attn_gain.reshape(1, D)
     expert_norm_gain = expert_norm_gain.reshape(1, D)
     router_rows = jnp.pad(w_router.T, ((0, 8 - EXPERTS), (0, 0)))
-    place = jnp.stack([lax.axis_index(a) for a in ("core", "z", "xl")]).astype(jnp.int32)
+    place = jnp.stack([lax.axis_index(a) for a in ("core", "z", "xl", "y")]).astype(jnp.int32)
 
     cot_all = gather(cotangent, RING)
     received = exchange(project(tokens, segment, attn_gain, w_query, w_key, w_value))
-    normed = normed_columns(tokens, attn_gain)
-    normed = jnp.stack([normed, swapped(normed, "xl")])
-    received, normed = after(received, normed)
-    normed_all = [normed] + [
-        lax.ppermute(normed, "z", [(i, (i + back) % 4) for i in range(4)]) for back in (1, 2, 3)
-    ]
+    received, normed = after(received, normed_columns(tokens, attn_gain))
+    normed_all = gather(normed, COLUMN)
     attended, att_mine, att_sent, full, log_total, q, k, cosine, sine = attend(place, received)
     attended, cot_all = after(attended, cot_all)
-    attended = exchange(attended).reshape(D, T)
-    att_theirs = swapped(att_sent, "core")
+    attended = exchange(attended)
+    att_theirs = swapped(att_sent, "xl")
     resid, moe_low, moe_columns, combine = residual(
         attended, tokens, routes[0], expert_norm_gain, router_rows, w_output
     )
     moe_all = gather(moe_columns, RING)
     output, resid_grad, grad_att, grad_columns, acts, small = experts(
-        resid, moe_low, combine, cotangent, expert_norm_gain, router_rows, w_output,
+        place, resid, moe_low, combine, cotangent, expert_norm_gain, router_rows, w_output,
         w_gate, w_up, w_down,
     )
-    acts = exchange(acts, RING)
-    grad_all = gather(grad_columns, SEQ)
-    grad_att, acts, moe_all = after(grad_att, acts, moe_all)
-    grad_att = exchange(grad_att.reshape(HQ, HD, T))
-    parts = expert_weights(acts, moe_all, cot_all)
-    mine, sent = attend_back(place, received, grad_att, full, log_total, q, k, cosine, sine)
+    grad_att, normed_all = after(grad_att, normed_all)
+    acts = [acts[0:2]] + [
+        lax.ppermute(acts[2 * back : 2 * back + 2], "y", [(i, (i + back) % 4) for i in range(4)])
+        for back in (1, 2, 3)
+    ]
+    grad_all = gather(grad_columns, COLUMN)
+    grad_att = exchange(grad_att)
+    mine, sent = attend_back(
+        place, received, grad_att, full, log_total, q, k, cosine, sine
+    )
+    sent, *acts = after(sent, *acts)
+    theirs = swapped(sent, "xl")
+    acts_theirs = swapped(jnp.stack([a[1] for a in acts]), "core")
+    parts = expert_weights(place, [a[0] for a in acts], acts_theirs, moe_all, cot_all)
+    theirs, parts = after(theirs, parts)
     expert_part = part_sum(parts, PLANE)
-    grads, weights = project_weights(
-        place, mine, swapped(sent, "core"), att_mine, att_theirs, normed_all, grad_all
-    )
+    grads, weights = project_weights(place, mine, theirs, normed_all)
+    expert_part, weights = after(expert_part, weights)
+    weights = output_weights(place, att_mine, att_theirs, grad_all, weights)
     project_part = part_sum(weights, REST)
     gathered = gather(jnp.concatenate([expert_part, project_part], axis=0), ALL)
     grads, project_part = after(grads, project_part)
     token_grad, small = project_back(
-        exchange(grads, CHIPS), tokens, attn_gain, w_query, w_key, w_value, resid_grad, small
-    )
-    small = spread_sum(spread_sum(small, REST, NR), CHIPS, NC)
+        exchange(grads, COLUMN), tokens, attn_gain, w_query, w_key, w_value, resid_grad, small
+    )
+    small = spread_sum(spread_sum(small, REST, NR), COLUMN, NC)
     dwq, dwk, dwv, dwo, dwg, dwu, dwd = assemble(
         gathered.reshape(4, 4, 2, 2, 2, PART + MINE, T)
     )

time: 289 us -> 272 us (0.941)
  waiting for transfers between devices: 102 us -> 77.4 us
  blocking collectives: 39.5 us -> 61.4 us
  starting transfers between devices: 40.5 us -> 30.7 us
  Pallas kernels: 81.7 us -> 74.9 us
  local copies, waits for them, and re-layouts: 6.91 us -> 10.5 us
    all_to_all x3 -> x4, blocking collectives: 39.5 us -> 61.4 us  [exchange(): return lax.all_to_all(array, axes, 0, 0, tiled=True)]
    all_gather x4 -> x5, waiting for transfers between devices: 47.6 us -> 32.8 us  [gather(): return lax.all_gather(array, axes, axis=0)]
    all_to_all x6 -> x4, starting transfers between devices: 37 us -> 23.2 us  [exchange(): return lax.all_to_all(array, axes, 0, 0, tiled=True)]
    ppermute x3, waiting for transfers between devices: 14.9 us -> 3.1 us  [swapped(): return lax.ppermute(array, axis, [(0, 1), (1, 0)])]
    ppermute x3, waiting for transfers between devices: 0.01 us -> 8.46 us  [shards(): lax.ppermute(acts[2 * back:2 * back + 2], 'y', [(i, (i + back) % 4) for i...]
    all_to_all x6 -> x4, waiting for transfers between devices: 38.7 us -> 32.3 us  [exchange(): return lax.all_to_all(array, axes, 0, 0, tiled=True)]
    pallas_call x1, Pallas kernels: 11.9 us -> 8.71 us  [attend(): pl.pallas_call(attend_kernel, in_specs=[PLACE] + in_vmem(1), out_shape=(j...]
    pallas_call x4 -> x5, Pallas kernels: 44.3 us -> 41.7 us  [the longest x1 17.7 us: assemble(): pl.pallas_call(assemble_kernel, grid=(4, 2), in_specs=[experts_of(0), exp...]
  transfers between devices with their start and end apart: 16 -> 15, of which waited for: 9 -> 9; matrix products, arithmetic and copies ran while one was open for 2% -> 3% of each run, Pallas kernels for 20% -> 20%
where the time goes in v3:
time: 272 us; the launch traced here: 271 us
  waiting for transfers between devices  77.4 us (28%)
  Pallas kernels  74.9 us (28%)
  blocking collectives  61.4 us (23%)
  starting transfers between devices  30.7 us (11%)
  between operations  13.9 us (5%)
  local copies, waits for them, and re-layouts  10.5 us (4%)
    all_to_all x4, blocking collectives, exchange(): return lax.all_to_all(array, axes, 0, 0, tiled=True)  61.4 us
    all_gather x5, waiting for transfers between devices, gather(): return lax.all_gather(array, axes, axis=0)  32.8 us
    all_to_all x4, waiting for transfers between devices, exchange(): return lax.all_to_all(array, axes, 0, 0, tiled=True)  32.3 us
    all_to_all x4, starting transfers between devices, exchange(): return lax.all_to_all(array, axes, 0, 0, tiled=True)  23.2 us
    pallas_call x1, Pallas kernels, assemble(): pl.pallas_call(assemble_kernel, grid=(4, 2), in_specs=[experts_of(0), exp...  17.7 us
    pallas_call x1, Pallas kernels, experts(): pl.pallas_call(experts_kernel, grid=(EXPERTS, NF), in_specs=[PLACE, whole...  11.4 us
    pallas_call x1, Pallas kernels, attend_back(): pl.pallas_call(attend_back_kernel, in_specs=[PLACE] + in_vmem(8), out_sha...  10.2 us
    pallas_call x1, Pallas kernels, attend(): pl.pallas_call(attend_kernel, in_specs=[PLACE] + in_vmem(1), out_shape=(j...  8.71 us
  transfers between devices with their start and end apart: 15, of which 9 were waited for; matrix products, arithmetic and copies ran while one was open for 3% of the time, Pallas kernels for 20%

profile of v3, /device:TPU:1, one launch (start us, length us, event | category | flops | bytes accessed | tf_op | source)
XLA Modules:
  0.0 270.6 jit_solution(16074574397393640356)
XLA Ops:
  7.9 1.3 reshape.41.gain_ref
  9.2 4.1 %project.1 = bf16[16,208,128]{2,1,0:T(8,128)(2,1)} custom-call(bf16[128,1024]{1,0:T(8,128)(2,1)} %bitcast.43, s32[1,128]{1,0:T(1,128)} %seg_ref.1, bf16[1,1024]{1,0:T(2,128)(2,1)} %reshape.41.gain_ref, bf16[1024,1024]{1,0:T(8,128)(2,1)} %wq_ref.3, bf16[1024,512]{1,0:T(8,128)(2,1)} %wk_ref.3, bf16[1024,512]{1,0:T(8,128)(2,1)} %wv_ref.3), custom_call_target="tpu_custom_call" | custom-call | flops 4000000000 | bytes 1048576 | tf_op jit(solution)/shard_map/project/pallas_call | solution.py:95
  13.3 7.8 %all-to-all-start = ((bf16[16,208,128]{2,1,0:T(8,128)(2,1)}), bf16[16,208,128]{2,1,0:T(8,128)(2,1)S(1)}, u32[]{:S(2)}, u32[]{:S(2)}) async-start(bf16[16,208,128]{2,1,0:T(8,128)(2,1)} %project.1), calls=%async_computation | async-start | bytes 1703936 | tf_op jit(solution)/shard_map/all_to_all | solution.py:699
  21.1 1.9 normed_columns.1
  23.0 11.7 %all-to-all-done.x_ref = bf16[16,208,128]{2,1,0:T(8,128)(2,1)S(1)} async-done(((bf16[16,208,128]{2,1,0:T(8,128)(2,1)}), bf16[16,208,128]{2,1,0:T(8,128)(2,1)S(1)}, u32[]{:S(2)}, u32[]{:S(2)}) %all-to-all-start) | async-done | bytes 852000 | tf_op jit(solution)/shard_map/all_to_all | solution.py:699
  35.6 8.7 %attend.1 = (bf16[16,64,128]{2,1,0:T(8,128)(2,1)}, bf16[8,64,128]{2,1,0:T(8,128)(2,1)}, bf16[8,64,128]{2,1,0:T(8,128)(2,1)}, f32[8,64,256]{2,1,0:T(8,128)}, f32[...) custom-call(s32[4]{0:T(128)} %pad_add_fusion.place_ref, ...), custom_call_target="tpu_custom_call" | custom-call | flops 12999999488 | bytes 1048576 | tf_op jit(solution)/shard_map/attend/pallas_call | solution.py:219
  44.3 4.2 %all-to-all-start.1 = ((bf16[16,64,128]{2,1,0:T(8,128)(2,1)}), bf16[16,64,128]{2,1,0:T(8,128)(2,1)S(1)}, u32[]{:S(2)}, u32[]{:S(2)}) async-start(bf16[16,64,128]{2,1,0:T(8,128)(2,1)} %get-tuple-element.62), calls=%async_computation.1 | async-start | bytes 524288 | tf_op jit(solution)/shard_map/all_to_all | solution.py:699
  50.6 5.2 %all-to-all-done.1.att_ref = bf16[16,64,128]{2,1,0:T(8,128)(2,1)S(1)} async-done(((bf16[16,64,128]{2,1,0:T(8,128)(2,1)}), bf16[16,64,128]{2,1,0:T(8,128)(2,1)S(1)}, u32[]{:S(2)}, u32[]{:S(2)}) %all-to-all-start.1) | async-done | bytes 262176 | tf_op jit(solution)/shard_map/all_to_all | solution.py:699
  56.5 3.4 %residual.1 = (f32[128,1024]{1,0:T(8,128)}, bf16[128,1024]{1,0:T(8,128)(2,1)}, bf16[1024,128]{1,0:T(8,128)(2,1)}, f32[128,128]{1,0:T(8,128)}) custom-call(bf16[16,64,128]{2,1,0:T(8,128)(2,1)} %copy-done.3, bf16[128,1024]{1,0:T(8,128)(2,1)} %bitcast.45, s32[128,2]{1,0:T(8,128)} %bitcast.34, bf16[1,1024]{1,0:T(2,128)(2,1)} %reshape.42.gain_ref, ...), custom_call_target="tpu_custom_call" | custom-call | flops 4000000000 | bytes 1048576 | tf_op jit(solution)/shard_map/residual/pallas_call | solution.py:352
  60.0 11.4 %experts.1 = (bf16[128,1024]{1,0:T(8,128)(2,1)}, f32[128,1024]{1,0:T(8,128)}, bf16[16,64,128]{2,1,0:T(8,128)(2,1)}, bf16[1024,128]{1,0:T(8,128)(2,1)}, bf16[8,576,128]{2,1,0:T(8,128)(2,1)}, /*index=5*/f32[16,1024]{1,0:T(8,128)}) custom-call(s32[4]{0:T(128)} %pad_add_fusion.place_ref, f32[128,1024]{1,0:T(8,128)} %get-tuple-element.63.resid_ref, ...), custom_call_target="tpu_custom_call" | custom-call | flops 12999999488 | bytes 1048576 | tf_op jit(solution)/shard_map/experts/pallas_call | solution.py:443
  71.4 4.5 %all-to-all-start.2 = ((bf16[16,64,128]{2,1,0:T(8,128)(2,1)}), bf16[16,64,128]{2,1,0:T(8,128)(2,1)S(1)}, u32[]{:S(2)}, u32[]{:S(2)}) async-start(bf16[16,64,128]{2,1,0:T(8,128)(2,1)} %get-tuple-element.69), calls=%async_computation.2 | async-start | bytes 524288 | tf_op jit(solution)/shard_map/all_to_all | solution.py:699
  75.9 1.3 fusion
  77.3 2.2 collective-permute-start.2
  80.8 2.3 all-to-all-done.2.g_ref
  83.8 10.2 %attend_back.1 = (bf16[8,192,128]{2,1,0:T(8,128)(2,1)}, bf16[8,192,128]{2,1,0:T(8,128)(2,1)}) custom-call(s32[4]{0:T(128)} %pad_add_fusion.place_ref, bf16[16,208,128]{2,1,0:T(8,128)(2,1)} %copy-done, bf16[16,64,128]{2,1,0:T(8,128)(2,1)} %copy-done.2, f32[8,64,256]{2,1,0:T(8,128)} %get-tuple-element.70.full_ref, f32[8,1,256]{2,1,0:T(1,128)} %get-tuple-element.71.log_ref, ...), custom_call_target="tpu_custom_call" | custom-call | flops 12999999488 | bytes 1048576 | tf_op jit(solution)/shard_map/attend_back/pallas_call | solution.py:296
  94.0 8.4 %collective-permute-done = bf16[2,576,128]{2,1,0:T(8,128)(2,1)S(1)} collective-permute-done((bf16[2,576,128]{2,1,0:T(8,128)(2,1)S(1)}, bf16[2,576,128]{2,1,0:T(8,128)(2,1)S(1)}, u32[]{:S(2)}, u32[]{:S(2)}) %collective-permute-start) | collective-permute-done | bytes 294944 | tf_op jit(solution)/shard_map/ppermute | solution.py:750
  105.1 1.4 collective-permute-start.3
  107.6 5.4 %expert_weights.1 = bf16[16,288,128]{2,1,0:T(8,128)(2,1)} custom-call(s32[4]{0:T(128)} %pad_add_fusion.place_ref, bf16[576,128]{1,0:T(8,128)(2,1)} %get-tuple-element.113.acts0_ref, bf16[576,128]{1,0:T(8,128)(2,1)} %get-tuple-element.122.acts1_ref, bf16[576,128]{1,0:T(8,128)(2,1)} %get-tuple-element.117.acts2_ref, ...), custom_call_target="tpu_custom_call" | custom-call | flops 5000000000 | bytes 1048576 | tf_op jit(solution)/shard_map/expert_weights/pallas_call | solution.py:503
  113.0 2.8 %collective-permute-done.3.theirs_ref = bf16[8,192,128]{2,1,0:T(8,128)(2,1)S(1)} collective-permute-done((bf16[8,192,128]{2,1,0:T(8,128)(2,1)S(1)}, bf16[8,192,128]{2,1,0:T(8,128)(2,1)S(1)}, u32[]{:S(2)}, u32[]{:S(2)}) %collective-permute-start.3) | collective-permute-done | bytes 393248 | tf_op jit(solution)/shard_map/ppermute | solution.py:703
  115.8 6.7 %all-to-all-start.3 = ((bf16[16,288,128]{2,1,0:T(8,128)(2,1)}), bf16[16,288,128]{2,1,0:T(8,128)(2,1)S(1)}, u32[]{:S(2)}, u32[]{:S(2)}) async-start(bf16[16,288,128]{2,1,0:T(8,128)(2,1)} %expert_weights.1), calls=%async_computation.3 | async-start | bytes 2359296 | tf_op jit(solution)/shard_map/all_to_all | solution.py:699
  122.6 1.4 collective-permute-start.5
  124.0 3.6 %project_weights.1 = (bf16[8,256,128]{2,1,0:T(8,128)(2,1)}, bf16[16,192,128]{2,1,0:T(8,128)(2,1)}) custom-call(s32[4]{0:T(128)} %pad_add_fusion.place_ref, bf16[8,192,128]{2,1,0:T(8,128)(2,1)} %get-tuple-element.76.mine_ref, bf16[8,192,128]{2,1,0:T(8,128)(2,1)} %copy-done.9, bf16[8,1024,128]{2,1,0:T(8,128)(2,1)} %bitcast.40), custom_call_target="tpu_custom_call" | custom-call | flops 4000000000 | bytes 1048576 | tf_op jit(solution)/shard_map/project_weights/pallas_call | solution.py:537
  127.6 13.0 %all-to-all-done.3 = bf16[16,288,128]{2,1,0:T(8,128)(2,1)S(1)} async-done(((bf16[16,288,128]{2,1,0:T(8,128)(2,1)}), bf16[16,288,128]{2,1,0:T(8,128)(2,1)S(1)}, u32[]{:S(2)}, u32[]{:S(2)}) %all-to-all-start.3) | async-done | bytes 1179680 | tf_op jit(solution)/shard_map/all_to_all | solution.py:699
  140.8 2.5 all-gather.16.cloned.1.call-done
  143.3 3.6 %output_weights.1 = bf16[16,192,128]{2,1,0:T(8,128)(2,1)} custom-call(s32[4]{0:T(128)} %pad_add_fusion.place_ref, bf16[8,64,128]{2,1,0:T(8,128)(2,1)} %get-tuple-element.89.att_ref, bf16[8,64,128]{2,1,0:T(8,128)(2,1)} %copy-done.11, bf16[8,1024,128]{2,1,0:T(8,128)(2,1)} %bitcast.42, bf16[16,192,128]{2,1,0:T(8,128)(2,1)} %get-tuple-element.94.parts_ref), custom_call_target="tpu_custom_call" | custom-call | flops 3000000000 | bytes 1048576 | tf_op jit(solution)/shard_map/output_weights/pallas_call | solution.py:567
  146.9 21.5 %all_to_all.40 = bf16[16,192,128]{2,1,0:T(8,128)(2,1)S(1)} all-to-all(bf16[16,192,128]{2,1,0:T(8,128)(2,1)} %output_weights.1), channel_id=1, replica_groups=mesh['y'=4,'xh'=2,'z'=4,'xl'=2,'core'=2] {'y','xh','xl'}, dimensions={0} | all-to-all | bytes 1572864 | tf_op jit(solution)/shard_map/all_to_all | solution.py:699
  169.2 14.4 %all_to_all.41.g_ref = bf16[8,256,128]{2,1,0:T(8,128)(2,1)} all-to-all(bf16[8,256,128]{2,1,0:T(8,128)(2,1)S(1)} %copy-done.1), channel_id=1, replica_groups=mesh['y'=4,'xh'=2,'z'=4,'xl'=2,'core'=2] {'z','core'}, dimensions={0} | all-to-all | bytes 1048576 | tf_op jit(solution)/shard_map/all_to_all | solution.py:699
  183.6 4.9 %project_back.1 = (bf16[128,1024]{1,0:T(8,128)(2,1)}, f32[8,1024]{1,0:T(8,128)}) custom-call(bf16[8,256,128]{2,1,0:T(8,128)(2,1)} %all_to_all.41.g_ref, bf16[128,1024]{1,0:T(8,128)(2,1)} %bitcast.46, bf16[1,1024]{1,0:T(2,128)(2,1)} %reshape.41.gain_ref, bf16[1024,1024]{1,0:T(8,128)(2,1)} %wq_ref.3, bf16[1024,512]{1,0:T(8,128)(2,1)} %wk_ref.3, ...), custom_call_target="tpu_custom_call" | custom-call | flops 5000000000 | bytes 1048576 | tf_op jit(solution)/shard_map/project_back/pallas_call | solution.py:604
  189.3 13.2 %all_to_all.42 = f32[16,8,1024]{2,1,0:T(8,128)S(1)} all-to-all(f32[16,8,1024]{2,1,0:T(8,128)S(1)} %broadcast_in_dim.20), channel_id=1, replica_groups=mesh['y'=4,'xh'=2,'z'=4,'xl'=2,'core'=2] {'y','xh','xl'}, dimensions={0} | all-to-all | bytes 1048576 | tf_op jit(solution)/shard_map/all_to_all | solution.py:699
  202.6 12.3 %all_to_all.43 = f32[8,8,1024]{2,1,0:T(8,128)S(1)} all-to-all(f32[8,8,1024]{2,1,0:T(8,128)S(1)} %broadcast_in_dim.21), channel_id=1, replica_groups=mesh['y'=4,'xh'=2,'z'=4,'xl'=2,'core'=2] {'z','core'}, dimensions={0} | all-to-all | bytes 524288 | tf_op jit(solution)/shard_map/all_to_all | solution.py:699
  216.1 30.3 %all-gather.18.cloned.1.call-done = bf16[61440,128]{1,0:T(8,128)(2,1)} async-done(((bf16[480,128]{1,0:T(8,128)(2,1)}), bf16[61440,128]{1,0:T(8,128)(2,1)}) %all-gather.18.cloned.1.call-update) | async-done | bytes 15728656 | tf_op jit(solution)/shard_map/all_gather | solution.py:707
  246.4 17.7 %assemble.1 = (f32[1024,1024]{1,0:T(8,128)}, f32[1024,512]{1,0:T(8,128)}, f32[1024,512]{1,0:T(8,128)}, f32[8,2,64,1024]{3,2,1,0:T(8,128)}, f32[3,1024,512]{2,1,0...) custom-call(bf16[4,4,2,2,2,480,128]{6,5,4,3,2,1,0:T(8,128)(2,1)} %bitcast.28, ...), custom_call_target="tpu_custom_call" | custom-call | flops 20000000000 | bytes 1048576 | tf_op jit(solution)/shard_map/assemble/pallas_call | solution.py:674
  (60 shorter events, 13.3 us)
Async XLA Ops:
  7.2 37.2 %all-gather.10.cloned.1.call-start = ((), (), s32[]{:S(2)}) async-start(), calls=%async_computation.8 | async-start | bytes 2359296 | tf_op jit(solution)/shard_map/all_gather | solution.py:707
  13.3 21.4 %all-to-all-start = ((bf16[16,208,128]{2,1,0:T(8,128)(2,1)}), bf16[16,208,128]{2,1,0:T(8,128)(2,1)S(1)}, u32[]{:S(2)}, u32[]{:S(2)}) async-start(bf16[16,208,128]{2,1,0:T(8,128)(2,1)} %project.1), calls=%async_computation | async-start | bytes 1703936 | tf_op jit(solution)/shard_map/all_to_all | solution.py:699
  21.0 50.4 %all-gather.12.cloned.1.call-start = ((), (), s32[]{:S(2)}) async-start(), calls=%async_computation.9 | async-start | bytes 2359296 | tf_op jit(solution)/shard_map/all_gather | solution.py:707
  34.7 0.9 copy-start
  35.6 13.0 %copy-start.5 = (bf16[1024]{0:T(1024)(128)(2,1)S(1)}, bf16[1024]{0:T(1024)(128)(2,1)}, u32[]{:S(2)}) copy-start(bf16[1024]{0:T(1024)(128)(2,1)} %param.23) | copy-start | bytes 6148
  35.6 13.6 %copy-start.6 = (s32[1,128,2]{1,2,0:T(2,128)S(1)}, s32[1,128,2]{1,2,0:T(2,128)}, u32[]{:S(2)}) copy-start(s32[1,128,2]{1,2,0:T(2,128)} %param.17) | copy-start | bytes 3076
  35.6 14.3 %copy-start.4 = (bf16[1024,3]{0,1:T(4,128)(2,1)S(1)}, bf16[1024,3]{0,1:T(4,128)(2,1)}, u32[]{:S(2)}) copy-start(bf16[1024,3]{0,1:T(4,128)(2,1)} %param.24) | copy-start | bytes 18436
  44.3 11.5 %all-to-all-start.1 = ((bf16[16,64,128]{2,1,0:T(8,128)(2,1)}), bf16[16,64,128]{2,1,0:T(8,128)(2,1)S(1)}, u32[]{:S(2)}, u32[]{:S(2)}) async-start(bf16[16,64,128]{2,1,0:T(8,128)(2,1)} %get-tuple-element.62), calls=%async_computation.1 | async-start | bytes 524288 | tf_op jit(solution)/shard_map/all_to_all | solution.py:699
  48.5 58.2 %all-gather.14.cloned.1.call-start = ((), (), s32[]{:S(2)}) async-start(), calls=%async_computation.10 | async-start | bytes 2359296 | tf_op jit(solution)/shard_map/all_gather | solution.py:707
  55.8 0.7 copy-start.3
  71.4 11.7 %all-to-all-start.2 = ((bf16[16,64,128]{2,1,0:T(8,128)(2,1)}), bf16[16,64,128]{2,1,0:T(8,128)(2,1)S(1)}, u32[]{:S(2)}, u32[]{:S(2)}) async-start(bf16[16,64,128]{2,1,0:T(8,128)(2,1)} %get-tuple-element.69), calls=%async_computation.2 | async-start | bytes 524288 | tf_op jit(solution)/shard_map/all_to_all | solution.py:699
  75.9 67.4 %all-gather.16.cloned.1.call-start = ((), (), s32[]{:S(2)}) async-start(), calls=%async_computation.11 | async-start | bytes 2359296 | tf_op jit(solution)/shard_map/all_gather | solution.py:707
  77.3 16.7 %collective-permute-start.2 = (bf16[2,576,128]{2,1,0:T(8,128)(2,1)S(1)}, bf16[2,576,128]{2,1,0:T(8,128)(2,1)S(1)}, u32[]{:S(2)}, u32[]{:S(2)}) collective-permute-start(bf16[2,576,128]{2,1,0:T(8,128)(2,1)S(1)} %get-tuple-element.108), channel_id=1, source_target_pairs={{0,96},{32,0},{64,32},{96,64},{1,97},{33,1},{65,33},{97,65},{2,98}... | collective-permute-start | bytes 884744 | tf_op jit(solution)/shard_map/ppermute | solution.py:750
  79.5 14.6 %collective-permute-start.1 = (bf16[2,576,128]{2,1,0:T(8,128)(2,1)S(1)}, bf16[2,576,128]{2,1,0:T(8,128)(2,1)S(1)}, u32[]{:S(2)}, u32[]{:S(2)}) collective-permute-start(bf16[2,576,128]{2,1,0:T(8,128)(2,1)S(1)} %get-tuple-element.109), channel_id=1, source_target_pairs={{0,64},{32,96},{64,0},{96,32},{1,65},{33,97},{65,1},{97,33},{2,66}... | collective-permute-start | bytes 884744 | tf_op jit(solution)/shard_map/ppermute | solution.py:750
  80.0 22.5 %collective-permute-start = (bf16[2,576,128]{2,1,0:T(8,128)(2,1)S(1)}, bf16[2,576,128]{2,1,0:T(8,128)(2,1)S(1)}, u32[]{:S(2)}, u32[]{:S(2)}) collective-permute-start(bf16[2,576,128]{2,1,0:T(8,128)(2,1)S(1)} %get-tuple-element.110), channel_id=1, source_target_pairs={{0,32},{32,64},{64,96},{96,0},{1,33},{33,65},{65,97},{97,1},{2,34}... | collective-permute-start | bytes 884744 | tf_op jit(solution)/shard_map/ppermute | solution.py:750
  83.1 0.7 copy-start.2
  94.0 11.1 %copy-start.8 = (bf16[8,192,128]{2,1,0:T(8,128)(2,1)S(1)}, bf16[8,192,128]{2,1,0:T(8,128)(2,1)}, u32[]{:S(2)}) copy-start(bf16[8,192,128]{2,1,0:T(8,128)(2,1)} %get-tuple-element.79) | copy-start | bytes 1179652
  104.0 2.7 %collective-permute-start.4 = (bf16[4,576,128]{2,1,0:T(8,128)(2,1)S(1)}, bf16[4,576,128]{2,1,0:T(8,128)(2,1)S(1)}, u32[]{:S(2)}, u32[]{:S(2)}) collective-permute-start(bf16[4,576,128]{2,1,0:T(8,128)(2,1)S(1)} %pad_maximum_fusion), channel_id=1, source_target_pairs={{0,1},{1,0},{2,3},{3,2},{4,5},{5,4},{6,7},{7,6},{8,9},{9,8},{10,11... | collective-permute-start | bytes 1769480 | tf_op jit(solution)/shard_map/ppermute | solution.py:703
  105.1 10.7 %collective-permute-start.3 = (bf16[8,192,128]{2,1,0:T(8,128)(2,1)S(1)}, bf16[8,192,128]{2,1,0:T(8,128)(2,1)S(1)}, u32[]{:S(2)}, u32[]{:S(2)}) collective-permute-start(bf16[8,192,128]{2,1,0:T(8,128)(2,1)S(1)} %copy-done.8), channel_id=1, source_target_pairs={{0,2},{2,0},{1,3},{3,1},{4,6},{6,4},{5,7},{7,5},{8,10},{10,8},{9,1... | collective-permute-start | bytes 1179656 | tf_op jit(solution)/shard_map/ppermute | solution.py:703
  106.8 0.8 copy-start.7
  113.0 9.6 %copy-start.10 = (bf16[8,64,128]{2,1,0:T(8,128)(2,1)S(1)}, bf16[8,64,128]{2,1,0:T(8,128)(2,1)}, u32[]{:S(2)}) copy-start(bf16[8,64,128]{2,1,0:T(8,128)(2,1)} %get-tuple-element.90) | copy-start | bytes 393220
  115.8 8.2 %copy-start.9 = (bf16[8,192,128]{2,1,0:T(8,128)(2,1)}, bf16[8,192,128]{2,1,0:T(8,128)(2,1)S(1)}, u32[]{:S(2)}) copy-start(bf16[8,192,128]{2,1,0:T(8,128)(2,1)S(1)} %collective-permute-done.3.theirs_ref) | copy-start | bytes 1179652
  115.8 24.8 %all-to-all-start.3 = ((bf16[16,288,128]{2,1,0:T(8,128)(2,1)}), bf16[16,288,128]{2,1,0:T(8,128)(2,1)S(1)}, u32[]{:S(2)}, u32[]{:S(2)}) async-start(bf16[16,288,128]{2,1,0:T(8,128)(2,1)} %expert_weights.1), calls=%async_computation.3 | async-start | bytes 2359296 | tf_op jit(solution)/shard_map/all_to_all | solution.py:699
  122.5 123.9 %all-gather.18.cloned.1.call-start = ((), (), s32[]{:S(2)}) async-start(), calls=%async_computation.12 | async-start | bytes 15851520 | tf_op jit(solution)/shard_map/all_gather | solution.py:707
  122.6 18.2 %collective-permute-start.5 = (bf16[8,64,128]{2,1,0:T(8,128)(2,1)S(1)}, bf16[8,64,128]{2,1,0:T(8,128)(2,1)S(1)}, u32[]{:S(2)}, u32[]{:S(2)}) collective-permute-start(bf16[8,64,128]{2,1,0:T(8,128)(2,1)S(1)} %copy-done.10), channel_id=1, source_target_pairs={{0,2},{2,0},{1,3},{3,1},{4,6},{6,4},{5,7},{7,5},{8,10},{10,8},{9,1... | collective-permute-start | bytes 393224 | tf_op jit(solution)/shard_map/ppermute | solution.py:703
  140.8 2.5 copy-start.11
  146.9 22.3 %copy-start.1 = (bf16[8,256,128]{2,1,0:T(8,128)(2,1)S(1)}, bf16[8,256,128]{2,1,0:T(8,128)(2,1)}, u32[]{:S(2)}) copy-start(bf16[8,256,128]{2,1,0:T(8,128)(2,1)} %get-tuple-element.95) | copy-start | bytes 1572868
Sparse Core Ops, SparseCore 0:
  9.7 28.8 all-gather.9
  40.4 27.0 all-gather.11
  69.2 35.8 all-gather.13
  106.6 36.6 all-gather.15
  169.3 77.0 all-gather.17

commit v4 on v3

--- a/solution.py
+++ b/solution.py
@@ -73,7 +73,7 @@
 def project_kernel(tok_ref, seg_ref, gain_ref, wq_ref, wk_ref, wv_ref, out_ref):
     x = tok_ref[...].astype(F32)
     inverse = lax.rsqrt(jnp.mean(x * x, axis=1, keepdims=True) + EPSILON)
-    normed = (x * inverse * gain_ref[...].astype(F32)).astype(BF)
+    normed = (x * inverse * gain_ref[...].astype(F32).reshape(1, D)).astype(BF)
     ids = jnp.broadcast_to(seg_ref[...].astype(F32), (16, T)).astype(BF)
     for h in range(HQ):
         out_ref[h, 3 * HD :, :] = ids
@@ -120,9 +120,9 @@
     return jnp.concatenate([ref[2 * i, at : at + HD, :], ref[2 * i + 1, at : at + HD, :]], axis=1)
 
 
-def put_pair(place_ref, keep_ref, send_ref, i, rows, a):
+def put_pair(keep_ref, send_ref, i, rows, a):
     low = a.astype(BF)
-    for ref, half in ((keep_ref, place_ref[2]), (send_ref, 1 - place_ref[2])):
+    for ref, half in ((keep_ref, lax.axis_index("xl")), (send_ref, 1 - lax.axis_index("xl"))):
 
         @pl.when((i & 1) == half)
         def _(ref=ref):
@@ -148,7 +148,7 @@
     return allowed
 
 
-def attend_kernel(place_ref, x_ref, att_ref, keep_ref, send_ref, full_ref, log_ref, q_ref, k_ref, cos_ref, sin_ref, kt_ref, v_ref):
+def attend_kernel(x_ref, att_ref, keep_ref, send_ref, full_ref, log_ref, q_ref, k_ref, cos_ref, sin_ref, kt_ref, v_ref):
     bounds = starts_of(x_ref)
     frequency = jnp.exp(
         lax.broadcasted_iota(jnp.int32, (HALF, 1), 0).astype(F32)
@@ -200,7 +200,7 @@
             low = attended.astype(BF)
             att_ref[2 * i] = low[:, :T]
             att_ref[2 * i + 1] = low[:, T:]
-            put_pair(place_ref, keep_ref, send_ref, i, slice(0, HD), attended)
+            put_pair(keep_ref, send_ref, i, slice(0, HD), attended)
 
         windowed(i, bounds, attend_window)
         return carry
@@ -208,17 +208,9 @@
     lax.fori_loop(0, NB, query_block, 0)
 
 
-PLACE = pl.BlockSpec(memory_space=pltpu.SMEM)
-
-
-def in_vmem(count):
-    return [pl.BlockSpec(memory_space=pltpu.VMEM)] * count
-
-
-def attend(place, received):
+def attend(received):
     return pl.pallas_call(
         attend_kernel,
-        in_specs=[PLACE] + in_vmem(1),
         out_shape=(
             jax.ShapeDtypeStruct((HQ, HD, T), BF),
             jax.ShapeDtypeStruct((NC, HD, T), BF),
@@ -233,11 +225,11 @@
         scratch_shapes=[pltpu.VMEM((NB, BLK, HD), BF), pltpu.VMEM((NB, HD, BLK), BF)],
         cost_estimate=cost(13),
         name="attend",
-    )(place, received)
+    )(received)
 
 
 def attend_back_kernel(
-    place_ref, x_ref, g_ref, full_ref, log_ref, q_ref, k_ref, cos_ref, sin_ref, keep_ref, send_ref,
+    x_ref, g_ref, full_ref, log_ref, q_ref, k_ref, cos_ref, sin_ref, keep_ref, send_ref,
     kt_ref, vt_ref, dk_ref, dv_ref,
 ):
     bounds = starts_of(x_ref)
@@ -257,7 +249,7 @@
         return jnp.concatenate([low * cosine + high * sine, high * cosine - low * sine], axis=0)
 
     def put(i, at, a):
-        put_pair(place_ref, keep_ref, send_ref, i, slice(at, at + HD), a)
+        put_pair(keep_ref, send_ref, i, slice(at, at + HD), a)
 
     def query_block(i, carry):
         q = q_ref[i]
@@ -292,10 +284,9 @@
     lax.fori_loop(0, NB, finish, 0, unroll=True)
 
 
-def attend_back(place, received, grad, full, log_total, q, k, cosine, sine):
+def attend_back(received, grad, full, log_total, q, k, cosine, sine):
     return pl.pallas_call(
         attend_back_kernel,
-        in_specs=[PLACE] + in_vmem(8),
         out_shape=(
             jax.ShapeDtypeStruct((NC, 3 * HD, T), BF),
             jax.ShapeDtypeStruct((NC, 3 * HD, T), BF),
@@ -308,13 +299,13 @@
         ],
         cost_estimate=cost(13),
         name="attend_back",
-    )(place, received, grad, full, log_total, q, k, cosine, sine)
+    )(received, grad, full, log_total, q, k, cosine, sine)
 
 
 def normed_kernel(tok_ref, gain_ref, out_ref):
     x = tok_ref[...].astype(F32)
     inverse = lax.rsqrt(jnp.mean(x * x, axis=1, keepdims=True) + EPSILON)
-    out_ref[...] = swap(x * inverse * gain_ref[...].astype(F32)).astype(BF)
+    out_ref[...] = swap(x * inverse * gain_ref[...].astype(F32).reshape(1, D)).astype(BF)
 
 
 def normed_columns(tokens, gain):
@@ -330,7 +321,7 @@
     attended = swap(jnp.concatenate(heads, axis=0).astype(F32)).astype(BF)
     resid = tok_ref[...].astype(F32) + dot(attended, wo_ref[...])
     inverse = lax.rsqrt(jnp.mean(resid * resid, axis=1, keepdims=True) + EPSILON)
-    normed = resid * inverse * gain_ref[...].astype(F32)
+    normed = resid * inverse * gain_ref[...].astype(F32).reshape(1, D)
     moe_low = normed.astype(BF)
     resid_ref[...] = resid
     moe_ref[...] = moe_low
@@ -363,7 +354,7 @@
 
 
 def experts_kernel(
-    place_ref, resid_ref, moe_ref, combine_ref, cot_ref, gain_ref, wr_ref, wo_ref, wg_ref, wu_ref, wd_ref,
+    resid_ref, moe_ref, combine_ref, cot_ref, gain_ref, wr_ref, wo_ref, wg_ref, wu_ref, wd_ref,
     out_ref, resid_grad_ref, grad_att_ref, grad_t_ref, acts_ref, small_ref,
     mix_ref, moe_grad_ref, cgrad_ref,
 ):
@@ -399,7 +390,7 @@
     act_t = swap(combine * act_low.astype(F32)).astype(BF)
     at_gu = pl.multiple_of(2 * FS * e, FS)
     at_down = pl.multiple_of(GU + FS * e, FS)
-    core, y = place_ref[0], place_ref[3]
+    core, y = lax.axis_index("core"), lax.axis_index("y")
     for i in range(FC // FS):
         j = f * (FC // FS) + i
         j = 2 * ((j // 2 - y) & 3) + ((j & 1) ^ core)
@@ -419,7 +410,7 @@
         inverse = lax.rsqrt(jnp.mean(resid * resid, axis=1, keepdims=True) + EPSILON)
         n = resid * inverse
         small_ref[8:16, :] = jnp.broadcast_to(jnp.sum(moe_grad * n, axis=0, keepdims=True), (8, D))
-        scaled = moe_grad * gain_ref[...].astype(F32)
+        scaled = moe_grad * gain_ref[...].astype(F32).reshape(1, D)
         resid_grad = grad_out + inverse * (
             scaled - n * jnp.mean(n * scaled, axis=1, keepdims=True)
         )
@@ -430,7 +421,7 @@
             grad_att_ref[device_of(h)] = grad_att[HD * h : HD * (h + 1)]
 
 
-def experts(place, resid, moe_low, combine, cotangent, gain, w_router, w_output, w_gate, w_up, w_down):
+def experts(resid, moe_low, combine, cotangent, gain, w_router, w_output, w_gate, w_up, w_down):
     def whole(*shape):
         return pl.BlockSpec(shape, lambda e, f: (0,) * len(shape))
 
@@ -444,7 +435,7 @@
         experts_kernel,
         grid=(EXPERTS, NF),
         in_specs=[
-            PLACE, whole(T, D), whole(T, D), whole(T, T), whole(T, D), whole(1, D), whole(8, D),
+            whole(T, D), whole(T, D), whole(T, T), whole(T, D), whole(D), whole(8, D),
             whole(D, D), columns(), columns(), rows(),
         ],
         out_specs=(
@@ -466,7 +457,7 @@
         ],
         cost_estimate=cost(13),
         name="experts",
-    )(place, resid, moe_low, combine, cotangent, gain, w_router, w_output, w_gate, w_up, w_down)
+    )(resid, moe_low, combine, cotangent, gain, w_router, w_output, w_gate, w_up, w_down)
 
 
 def side_by_side(ref, i, j):
@@ -474,16 +465,17 @@
 
 
 def expert_weights_kernel(
-    place_ref, acts0_ref, acts1_ref, acts2_ref, acts3_ref, other_ref, moe_ref, cot_ref,
-    out_ref, wide_ref, down_ref,
-):
-    core, y = place_ref[0], place_ref[3]
+    acts0_ref, acts1_ref, acts2_ref, acts3_ref, other_ref, moe_ref,
+    cot0_ref, cot1_ref, cot2_ref, cot3_ref, out_ref, wide_ref, down_ref,
+):
+    core, y = lax.axis_index("core"), lax.axis_index("y")
+    cot_refs = (cot0_ref, cot1_ref, cot2_ref, cot3_ref)
     for back, acts_ref in enumerate((acts0_ref, acts1_ref, acts2_ref, acts3_ref)):
         chip = 2 * ((y - back) & 3)
         near, far = chip + core, chip + 1 - core
-        acts = jnp.concatenate([acts_ref[...], other_ref[back]], axis=1)
+        acts = jnp.concatenate([acts_ref[0], other_ref[back]], axis=1)
         wide = dot(side_by_side(moe_ref, near, far), acts[0:GU], NT)
-        down = dot(acts[GU:], jnp.concatenate([cot_ref[near], cot_ref[far]], axis=0))
+        down = dot(acts[GU:], cot_refs[back][...].reshape(2 * T, D))
         if back == 0:
             wide_ref[...] = wide
             down_ref[...] = down
@@ -499,15 +491,14 @@
         out_ref[i, 192:288, :] = down_ref[half : half + 96, lanes : lanes + 128].astype(BF)
 
 
-def expert_weights(place, acts, others, moe, cotangent):
+def expert_weights(acts, others, moe, cotangent):
     return pl.pallas_call(
         expert_weights_kernel,
-        in_specs=[PLACE] + in_vmem(7),
         out_shape=jax.ShapeDtypeStruct((NR, PART, T), BF),
         scratch_shapes=[pltpu.VMEM((D, GU), F32), pltpu.VMEM((FS * EXPERTS, D), F32)],
         cost_estimate=cost(5),
         name="expert_weights",
-    )(place, *acts, others, moe, cotangent)
+    )(*acts, others, moe, *cotangent)
 
 
 def own_rows(half):
@@ -515,9 +506,9 @@
 
 
 def project_weights_kernel(
-    place_ref, mine_ref, theirs_ref, normed_ref, back_ref, out_ref
-):
-    own, partner = own_rows(place_ref[2])
+    mine_ref, theirs_ref, normed_ref, back_ref, out_ref
+):
+    own, partner = own_rows(lax.axis_index("xl"))
     for b in range(NC):
         back_ref[b, own, :] = mine_ref[b, 0:HD, :]
         back_ref[b, partner, :] = theirs_ref[b, 0:HD, :]
@@ -533,23 +524,22 @@
         out_ref[i, 64:128, :] = low[64 * i : 64 * (i + 1), 128:256]
 
 
-def project_weights(place, mine, theirs, normed):
+def project_weights(mine, theirs, normed):
     return pl.pallas_call(
         project_weights_kernel,
-        in_specs=[PLACE] + in_vmem(3),
         out_shape=(
             jax.ShapeDtypeStruct((NC, 4 * HD, T), BF),
             jax.ShapeDtypeStruct((NR, MINE, T), BF),
         ),
         cost_estimate=cost(4),
         name="project_weights",
-    )(place, mine, theirs, normed)
+    )(mine, theirs, normed)
 
 
 def output_weights_kernel(
-    place_ref, att_ref, att_other_ref, grad_ref, parts_ref, out_ref, heads_ref
-):
-    own, partner = own_rows(place_ref[2])
+    att_ref, att_other_ref, grad_ref, parts_ref, out_ref, heads_ref
+):
+    own, partner = own_rows(lax.axis_index("xl"))
     o = jnp.zeros((2 * HD, D), F32)
     for b in range(NC):
         heads_ref[b, own, :] = att_ref[b]
@@ -563,22 +553,21 @@
         out_ref[i, 128:192, :] = low[half : half + 64, lanes : lanes + 128]
 
 
-def output_weights(place, attended, attended_other, grad, parts):
+def output_weights(attended, attended_other, grad, parts):
     return pl.pallas_call(
         output_weights_kernel,
-        in_specs=[PLACE] + in_vmem(4),
         out_shape=jax.ShapeDtypeStruct((NR, MINE, T), BF),
         scratch_shapes=[pltpu.VMEM((NC, 2 * HD, T), BF)],
         cost_estimate=cost(3),
         name="output_weights",
-    )(place, attended, attended_other, grad, parts)
+    )(attended, attended_other, grad, parts)
 
 
 def project_back_kernel(
     g_ref, tok_ref, gain_ref, wq_ref, wk_ref, wv_ref, resid_grad_ref, small_ref, out_ref, sums_ref
 ):
     x = tok_ref[...].astype(F32)
-    gain = gain_ref[...].astype(F32)
+    gain = gain_ref[...].astype(F32).reshape(1, D)
     inverse = lax.rsqrt(jnp.mean(x * x, axis=1, keepdims=True) + EPSILON)
     n = x * inverse
 
@@ -703,6 +692,10 @@
     return lax.ppermute(array, axis, [(0, 1), (1, 0)])
 
 
+def ring_moved(array, back):
+    return lax.ppermute(array, "y", [(i, (i + back) % 4) for i in range(4)])
+
+
 def gather(array, axes):
     return lax.all_gather(array, axes, axis=0)
 
@@ -724,46 +717,46 @@
     expert_norm_gain, w_router, w_gate, w_up, w_down,
 ):
     tokens, cotangent = tokens[0], cotangent[0]
-    attn_gain = attn_gain.reshape(1, D)
-    expert_norm_gain = expert_norm_gain.reshape(1, D)
     router_rows = jnp.pad(w_router.T, ((0, 8 - EXPERTS), (0, 0)))
-    place = jnp.stack([lax.axis_index(a) for a in ("core", "z", "xl", "y")]).astype(jnp.int32)
-
-    cot_all = gather(cotangent, RING)
-    received = exchange(project(tokens, segment, attn_gain, w_query, w_key, w_value))
-    received, normed = after(received, normed_columns(tokens, attn_gain))
+
+    projected = project(tokens, segment, attn_gain, w_query, w_key, w_value)
+    projected, cot = after(projected, cotangent)
+    received = exchange(projected)
+    cot = jnp.stack([cot, swapped(cot, "core")])
+    received, normed, cot, cot3 = after(
+        received, normed_columns(tokens, attn_gain), cot, ring_moved(cot, 3)
+    )
+    cot1, cot2 = ring_moved(cot, 1), ring_moved(cot, 2)
     normed_all = gather(normed, COLUMN)
-    attended, att_mine, att_sent, full, log_total, q, k, cosine, sine = attend(place, received)
-    attended, cot_all = after(attended, cot_all)
-    attended = exchange(attended)
+    attended, att_mine, att_sent, full, log_total, q, k, cosine, sine = attend(received)
+    attended, cot1, cot2 = after(exchange(attended), cot1, cot2)
     att_theirs = swapped(att_sent, "xl")
     resid, moe_low, moe_columns, combine = residual(
         attended, tokens, routes[0], expert_norm_gain, router_rows, w_output
     )
     moe_all = gather(moe_columns, RING)
     output, resid_grad, grad_att, grad_columns, acts, small = experts(
-        place, resid, moe_low, combine, cotangent, expert_norm_gain, router_rows, w_output,
+        resid, moe_low, combine, cotangent, expert_norm_gain, router_rows, w_output,
         w_gate, w_up, w_down,
     )
-    grad_att, normed_all = after(grad_att, normed_all)
+    grad_att, normed_all, att_theirs = after(grad_att, normed_all, att_theirs)
     acts = [acts[0:2]] + [
-        lax.ppermute(acts[2 * back : 2 * back + 2], "y", [(i, (i + back) % 4) for i in range(4)])
-        for back in (1, 2, 3)
+        ring_moved(acts[2 * back : 2 * back + 2], back) for back in (1, 2, 3)
     ]
     grad_all = gather(grad_columns, COLUMN)
     grad_att = exchange(grad_att)
     mine, sent = attend_back(
-        place, received, grad_att, full, log_total, q, k, cosine, sine
+        received, grad_att, full, log_total, q, k, cosine, sine
     )
     sent, *acts = after(sent, *acts)
     theirs = swapped(sent, "xl")
     acts_theirs = swapped(jnp.stack([a[1] for a in acts]), "core")
-    parts = expert_weights(place, [a[0] for a in acts], acts_theirs, moe_all, cot_all)
+    parts = expert_weights(acts, acts_theirs, moe_all, (cot, cot1, cot2, cot3))
     theirs, parts = after(theirs, parts)
     expert_part = part_sum(parts, PLANE)
-    grads, weights = project_weights(place, mine, theirs, normed_all)
+    grads, weights = project_weights(mine, theirs, normed_all)
+    weights = output_weights(att_mine, att_theirs, grad_all, weights)
     expert_part, weights = after(expert_part, weights)
-    weights = output_weights(place, att_mine, att_theirs, grad_all, weights)
     project_part = part_sum(weights, REST)
     gathered = gather(jnp.concatenate([expert_part, project_part], axis=0), ALL)
     grads, project_part = after(grads, project_part)

time: 272 us -> 263 us (0.967)
  waiting for transfers between devices: 77.4 us -> 66.4 us
  starting transfers between devices: 30.7 us -> 41 us
  local copies, waits for them, and re-layouts: 10.5 us -> 7.01 us
  blocking collectives: 61.4 us -> 58.5 us
    all_to_all x4, waiting for transfers between devices: 32.3 us -> 18.8 us  [exchange(): return lax.all_to_all(array, axes, 0, 0, tiled=True)]
    ppermute x3 -> x6, starting transfers between devices: 3.47 us -> 10.3 us  [ring_moved(): return lax.ppermute(array, 'y', [(i, (i + back) % 4) for i in range(4)])]
    ppermute x3 -> x4, waiting for transfers between devices: 3.1 us -> 6.28 us  [swapped(): return lax.ppermute(array, axis, [(0, 1), (1, 0)])]
    all_to_all x4, blocking collectives: 61.4 us -> 58.5 us  [exchange(): return lax.all_to_all(array, axes, 0, 0, tiled=True)]
    ppermute x3 -> x6, waiting for transfers between devices: 8.46 us -> 10.9 us  [ring_moved(): return lax.ppermute(array, 'y', [(i, (i + back) % 4) for i in range(4)])]
    all_gather x5 -> x4, waiting for transfers between devices: 32.8 us -> 30.3 us  [gather(): return lax.all_gather(array, axes, axis=0)]
  transfers between devices with their start and end apart: 15 -> 18, of which waited for: 9 -> 9; matrix products, arithmetic and copies ran while one was open for 3% -> 2% of each run, Pallas kernels for 20% -> 20%
where the time goes in v4:
time: 263 us; the launch traced here: 262 us
  Pallas kernels  73.7 us (28%)
  waiting for transfers between devices  66.4 us (25%)
  blocking collectives  58.5 us (22%)
  starting transfers between devices  41 us (16%)
  between operations  14 us (5%)
  local copies, waits for them, and re-layouts  7.01 us (3%)
    all_to_all x4, blocking collectives, exchange(): return lax.all_to_all(array, axes, 0, 0, tiled=True)  58.5 us
    all_gather x4, waiting for transfers between devices, gather(): return lax.all_gather(array, axes, axis=0)  30.3 us
    all_to_all x4, starting transfers between devices, exchange(): return lax.all_to_all(array, axes, 0, 0, tiled=True)  25.6 us
    all_to_all x4, waiting for transfers between devices, exchange(): return lax.all_to_all(array, axes, 0, 0, tiled=True)  18.8 us
    pallas_call x1, Pallas kernels, assemble(): pl.pallas_call(assemble_kernel, grid=(4, 2), in_specs=[experts_of(0), exp...  17.7 us
    pallas_call x1, Pallas kernels, experts(): pl.pallas_call(experts_kernel, grid=(EXPERTS, NF), in_specs=[whole(T, D),...  11.3 us
    ppermute x6, waiting for transfers between devices, ring_moved(): return lax.ppermute(array, 'y', [(i, (i + back) % 4) for i in range(4)])  10.9 us
    ppermute x6, starting transfers between devices, ring_moved(): return lax.ppermute(array, 'y', [(i, (i + back) % 4) for i in range(4)])  10.3 us
  transfers between devices with their start and end apart: 18, of which 9 were waited for; matrix products, arithmetic and copies ran while one was open for 2% of the time, Pallas kernels for 20%

profile of v4, /device:TPU:1, one launch (start us, length us, event | category | flops | bytes accessed | tf_op | source)
XLA Modules:
  0.0 261.7 jit_solution(7298944602780489151)
XLA Ops:
  7.2 4.1 %project.1 = bf16[16,208,128]{2,1,0:T(8,128)(2,1)} custom-call(bf16[128,1024]{1,0:T(8,128)(2,1)} %bitcast.35, s32[1,128]{1,0:T(1,128)} %seg_ref.1, bf16[1024]{0:T(1024)(128)(2,1)} %gain_ref.9, bf16[1024,1024]{1,0:T(8,128)(2,1)} %wq_ref.3, bf16[1024,512]{1,0:T(8,128)(2,1)} %wk_ref.3, bf16[1024,512]{1,0:T(8,128)(2,1)} %wv_ref.3), custom_call_target="tpu_custom_call" | custom-call | flops 4000000000 | bytes 1048576 | tf_op jit(solution)/shard_map/project/pallas_call | solution.py:95
  12.7 6.5 %all-to-all-start = ((bf16[16,208,128]{2,1,0:T(8,128)(2,1)}), bf16[16,208,128]{2,1,0:T(8,128)(2,1)S(1)}, u32[]{:S(2)}, u32[]{:S(2)}) async-start(bf16[16,208,128]{2,1,0:T(8,128)(2,1)} %project.1), calls=%async_computation | async-start | bytes 1703936 | tf_op jit(solution)/shard_map/all_to_all | solution.py:688
  19.3 2.8 %collective-permute-start.1 = (bf16[2,128,1024]{2,1,0:T(8,128)(2,1)S(1)}, bf16[2,128,1024]{2,1,0:T(8,128)(2,1)S(1)}, u32[]{:S(2)}, u32[]{:S(2)}) collective-permute-start(bf16[2,128,1024]{2,1,0:T(8,128)(2,1)S(1)} %pad_maximum_fusion.1.cot0_ref), channel_id=1, source_target_pairs={{0,96},{32,0},{64,32},{96,64},{1,97},{33,1},{65,33},{97,65},{2,98}... | collective-permute-start | bytes 1572872 | tf_op jit(solution)/shard_map/ppermute | solution.py:696
  22.1 1.9 normed_columns.1
  24.0 9.4 %collective-permute-done.1.cot3_ref = bf16[2,128,1024]{2,1,0:T(8,128)(2,1)S(1)} collective-permute-done((bf16[2,128,1024]{2,1,0:T(8,128)(2,1)S(1)}, bf16[2,128,1024]{2,1,0:T(8,128)(2,1)S(1)}, u32[]{:S(2)}, u32[]{:S(2)}) %collective-permute-start.1) | collective-permute-done | bytes 524320 | tf_op jit(solution)/shard_map/ppermute | solution.py:696
  33.5 2.5 collective-permute-start.3
  35.9 1.6 collective-permute-start.2
  37.5 8.3 %attend.1 = (bf16[16,64,128]{2,1,0:T(8,128)(2,1)}, bf16[8,64,128]{2,1,0:T(8,128)(2,1)}, bf16[8,64,128]{2,1,0:T(8,128)(2,1)}, f32[8,64,256]{2,1,0:T(8,128)}, f32[...) custom-call(bf16[16,208,128]{2,1,0:T(8,128)(2,1)} %copy-done), custom_call_target="tpu_custom_call" | custom-call | flops 12999999488 | bytes 1048576 | tf_op jit(solution)/shard_map/attend/pallas_call | solution.py:212
  45.9 6.8 %all-to-all-start.1 = ((bf16[16,64,128]{2,1,0:T(8,128)(2,1)}), bf16[16,64,128]{2,1,0:T(8,128)(2,1)S(1)}, u32[]{:S(2)}, u32[]{:S(2)}) async-start(bf16[16,64,128]{2,1,0:T(8,128)(2,1)} %get-tuple-element.69), calls=%async_computation.1 | async-start | bytes 524288 | tf_op jit(solution)/shard_map/all_to_all | solution.py:688
  54.1 6.3 %all-to-all-done.1.att_ref = bf16[16,64,128]{2,1,0:T(8,128)(2,1)S(1)} async-done(((bf16[16,64,128]{2,1,0:T(8,128)(2,1)}), bf16[16,64,128]{2,1,0:T(8,128)(2,1)S(1)}, u32[]{:S(2)}, u32[]{:S(2)}) %all-to-all-start.1) | async-done | bytes 262176 | tf_op jit(solution)/shard_map/all_to_all | solution.py:688
  61.1 3.4 %residual.1 = (f32[128,1024]{1,0:T(8,128)}, bf16[128,1024]{1,0:T(8,128)(2,1)}, bf16[1024,128]{1,0:T(8,128)(2,1)}, f32[128,128]{1,0:T(8,128)}) custom-call(bf16[16,64,128]{2,1,0:T(8,128)(2,1)} %copy-done.5, bf16[128,1024]{1,0:T(8,128)(2,1)} %bitcast.37, s32[128,2]{1,0:T(8,128)} %bitcast.26, bf16[1024]{0:T(1024)(128)(2,1)} %gain_ref.8, ...), custom_call_target="tpu_custom_call" | custom-call | flops 4000000000 | bytes 1048576 | tf_op jit(solution)/shard_map/residual/pallas_call | solution.py:343
  64.6 11.3 %experts.1 = (bf16[128,1024]{1,0:T(8,128)(2,1)}, f32[128,1024]{1,0:T(8,128)}, bf16[16,64,128]{2,1,0:T(8,128)(2,1)}, bf16[1024,128]{1,0:T(8,128)(2,1)}, bf16[8,576,128]{2,1,0:T(8,128)(2,1)}, /*index=5*/f32[16,1024]{1,0:T(8,128)}) custom-call(f32[128,1024]{1,0:T(8,128)} %get-tuple-element.72.resid_ref, bf16[128,1024]{1,0:T(8,128)(2,1)} %get-tuple-element.73.moe_ref, ...), custom_call_target="tpu_custom_call" | custom-call | flops 12999999488 | bytes 1048576 | tf_op jit(solution)/shard_map/experts/pallas_call | solution.py:434
  75.9 1.5 collective-permute-start.4
  77.4 3.2 %collective-permute-done.4.att_other_ref = bf16[8,64,128]{2,1,0:T(8,128)(2,1)S(1)} collective-permute-done((bf16[8,64,128]{2,1,0:T(8,128)(2,1)S(1)}, bf16[8,64,128]{2,1,0:T(8,128)(2,1)S(1)}, u32[]{:S(2)}, u32[]{:S(2)}) %collective-permute-start.4) | collective-permute-done | bytes 131104 | tf_op jit(solution)/shard_map/ppermute | solution.py:692
  80.6 5.5 %all-to-all-start.2 = ((bf16[16,64,128]{2,1,0:T(8,128)(2,1)}), bf16[16,64,128]{2,1,0:T(8,128)(2,1)S(1)}, u32[]{:S(2)}, u32[]{:S(2)}) async-start(bf16[16,64,128]{2,1,0:T(8,128)(2,1)} %get-tuple-element.79), calls=%async_computation.2 | async-start | bytes 524288 | tf_op jit(solution)/shard_map/all_to_all | solution.py:688
  88.4 1.8 collective-permute-start.6
  90.9 2.5 all-to-all-done.2.g_ref
  94.1 9.4 %attend_back.1 = (bf16[8,192,128]{2,1,0:T(8,128)(2,1)}, bf16[8,192,128]{2,1,0:T(8,128)(2,1)}) custom-call(bf16[16,208,128]{2,1,0:T(8,128)(2,1)} %copy-done, bf16[16,64,128]{2,1,0:T(8,128)(2,1)} %copy-done.4, f32[8,64,256]{2,1,0:T(8,128)} %get-tuple-element.80.full_ref, f32[8,1,256]{2,1,0:T(1,128)} %get-tuple-element.81.log_ref, ...), custom_call_target="tpu_custom_call" | custom-call | flops 12999999488 | bytes 1048576 | tf_op jit(solution)/shard_map/attend_back/pallas_call | solution.py:288
  103.6 1.6 collective-permute-done.5.acts1_ref
  108.3 5.5 %expert_weights.1 = bf16[16,288,128]{2,1,0:T(8,128)(2,1)} custom-call(bf16[2,576,128]{2,1,0:T(8,128)(2,1)} %copy-done.1, bf16[2,576,128]{2,1,0:T(8,128)(2,1)} %copy-done.9, bf16[2,576,128]{2,1,0:T(8,128)(2,1)} %copy-done.8, bf16[2,576,128]{2,1,0:T(8,128)(2,1)} %copy-done.7, bf16[4,576,128]{2,1,0:T(8,128)(2,1)} %copy-done.12, bf16[8,1024,128]{2,1,0:T(8,128)(2,1)} %bitcast.34, ...), custom_call_target="tpu_custom_call" | custom-call | flops 5000000000 | bytes 1048576 | tf_op jit(solution)/shard_map/expert_weights/pallas_call | solution.py:495
  113.8 2.8 %collective-permute-done.8.theirs_ref = bf16[8,192,128]{2,1,0:T(8,128)(2,1)S(1)} collective-permute-done((bf16[8,192,128]{2,1,0:T(8,128)(2,1)S(1)}, bf16[8,192,128]{2,1,0:T(8,128)(2,1)S(1)}, u32[]{:S(2)}, u32[]{:S(2)}) %collective-permute-start.8) | collective-permute-done | bytes 393248 | tf_op jit(solution)/shard_map/ppermute | solution.py:692
  116.7 6.9 %all-to-all-start.3 = ((bf16[16,288,128]{2,1,0:T(8,128)(2,1)}), bf16[16,288,128]{2,1,0:T(8,128)(2,1)S(1)}, u32[]{:S(2)}, u32[]{:S(2)}) async-start(bf16[16,288,128]{2,1,0:T(8,128)(2,1)} %expert_weights.1), calls=%async_computation.3 | async-start | bytes 2359296 | tf_op jit(solution)/shard_map/all_to_all | solution.py:688
  123.6 3.5 %project_weights.1 = (bf16[8,256,128]{2,1,0:T(8,128)(2,1)}, bf16[16,192,128]{2,1,0:T(8,128)(2,1)}) custom-call(bf16[8,192,128]{2,1,0:T(8,128)(2,1)} %get-tuple-element.86.mine_ref, bf16[8,192,128]{2,1,0:T(8,128)(2,1)} %copy-done.17, bf16[8,1024,128]{2,1,0:T(8,128)(2,1)} %bitcast.32), custom_call_target="tpu_custom_call" | custom-call | flops 4000000000 | bytes 1048576 | tf_op jit(solution)/shard_map/project_weights/pallas_call | solution.py:528
  127.2 3.6 %output_weights.1 = bf16[16,192,128]{2,1,0:T(8,128)(2,1)} custom-call(bf16[8,64,128]{2,1,0:T(8,128)(2,1)} %get-tuple-element.102.att_ref, bf16[8,64,128]{2,1,0:T(8,128)(2,1)} %copy-done.18, bf16[8,1024,128]{2,1,0:T(8,128)(2,1)} %bitcast.33, bf16[16,192,128]{2,1,0:T(8,128)(2,1)} %get-tuple-element.105.parts_ref), custom_call_target="tpu_custom_call" | custom-call | flops 3000000000 | bytes 1048576 | tf_op jit(solution)/shard_map/output_weights/pallas_call | solution.py:557
  130.8 10.0 %all-to-all-done.3 = bf16[16,288,128]{2,1,0:T(8,128)(2,1)S(1)} async-done(((bf16[16,288,128]{2,1,0:T(8,128)(2,1)}), bf16[16,288,128]{2,1,0:T(8,128)(2,1)S(1)}, u32[]{:S(2)}, u32[]{:S(2)}) %all-to-all-start.3) | async-done | bytes 1179680 | tf_op jit(solution)/shard_map/all_to_all | solution.py:688
  140.9 17.1 %all_to_all.40 = bf16[16,192,128]{2,1,0:T(8,128)(2,1)S(1)} all-to-all(bf16[16,192,128]{2,1,0:T(8,128)(2,1)} %output_weights.1), channel_id=1, replica_groups=mesh['y'=4,'xh'=2,'z'=4,'xl'=2,'core'=2] {'y','xh','xl'}, dimensions={0} | all-to-all | bytes 1572864 | tf_op jit(solution)/shard_map/all_to_all | solution.py:688
  158.8 15.9 %all_to_all.41.g_ref = bf16[8,256,128]{2,1,0:T(8,128)(2,1)} all-to-all(bf16[8,256,128]{2,1,0:T(8,128)(2,1)S(1)} %copy-done.3), channel_id=1, replica_groups=mesh['y'=4,'xh'=2,'z'=4,'xl'=2,'core'=2] {'z','core'}, dimensions={0} | all-to-all | bytes 1048576 | tf_op jit(solution)/shard_map/all_to_all | solution.py:688
  174.7 4.9 %project_back.1 = (bf16[128,1024]{1,0:T(8,128)(2,1)}, f32[8,1024]{1,0:T(8,128)}) custom-call(bf16[8,256,128]{2,1,0:T(8,128)(2,1)} %all_to_all.41.g_ref, bf16[128,1024]{1,0:T(8,128)(2,1)} %bitcast.38, bf16[1024]{0:T(1024)(128)(2,1)} %gain_ref.9, bf16[1024,1024]{1,0:T(8,128)(2,1)} %wq_ref.3, bf16[1024,512]{1,0:T(8,128)(2,1)} %wk_ref.3, ...), custom_call_target="tpu_custom_call" | custom-call | flops 5000000000 | bytes 1048576 | tf_op jit(solution)/shard_map/project_back/pallas_call | solution.py:593
  180.4 13.2 %all_to_all.42 = f32[16,8,1024]{2,1,0:T(8,128)S(1)} all-to-all(f32[16,8,1024]{2,1,0:T(8,128)S(1)} %broadcast_in_dim.20), channel_id=1, replica_groups=mesh['y'=4,'xh'=2,'z'=4,'xl'=2,'core'=2] {'y','xh','xl'}, dimensions={0} | all-to-all | bytes 1048576 | tf_op jit(solution)/shard_map/all_to_all | solution.py:688
  193.7 12.3 %all_to_all.43 = f32[8,8,1024]{2,1,0:T(8,128)S(1)} all-to-all(f32[8,8,1024]{2,1,0:T(8,128)S(1)} %broadcast_in_dim.21), channel_id=1, replica_groups=mesh['y'=4,'xh'=2,'z'=4,'xl'=2,'core'=2] {'z','core'}, dimensions={0} | all-to-all | bytes 524288 | tf_op jit(solution)/shard_map/all_to_all | solution.py:688
  207.2 30.3 %all-gather.15.cloned.1.call-done = bf16[61440,128]{1,0:T(8,128)(2,1)} async-done(((bf16[480,128]{1,0:T(8,128)(2,1)}), bf16[61440,128]{1,0:T(8,128)(2,1)}) %all-gather.15.cloned.1.call-update) | async-done | bytes 15728656 | tf_op jit(solution)/shard_map/all_gather | solution.py:700
  237.5 17.7 %assemble.1 = (f32[1024,1024]{1,0:T(8,128)}, f32[1024,512]{1,0:T(8,128)}, f32[1024,512]{1,0:T(8,128)}, f32[8,2,64,1024]{3,2,1,0:T(8,128)}, f32[3,1024,512]{2,1,0...) custom-call(bf16[4,4,2,2,2,480,128]{6,5,4,3,2,1,0:T(8,128)(2,1)} %bitcast.18, ...), custom_call_target="tpu_custom_call" | custom-call | flops 20000000000 | bytes 1048576 | tf_op jit(solution)/shard_map/assemble/pallas_call | solution.py:663
  (81 shorter events, 13.6 us)
Async XLA Ops:
  7.2 4.1 %copy-start.6 = (bf16[1,128,1024]{2,1,0:T(8,128)(2,1)S(1)}, bf16[1,128,1024]{2,1,0:T(8,128)(2,1)}, u32[]{:S(2)}) copy-start(bf16[1,128,1024]{2,1,0:T(8,128)(2,1)} %param.15) | copy-start | bytes 786436
  11.3 7.9 %collective-permute-start = (bf16[128,1024]{1,0:T(8,128)(2,1)S(1)}, bf16[128,1024]{1,0:T(8,128)(2,1)S(1)}, u32[]{:S(2)}, u32[]{:S(2)}) collective-permute-start(bf16[128,1024]{1,0:T(8,128)(2,1)S(1)} %bitcast.24), channel_id=1, source_target_pairs={{0,1},{1,0},{2,3},{3,2},{4,5},{5,4},{6,7},{7,6},{8,9},{9,8},{10,11... | collective-permute-start | bytes 786440 | tf_op jit(solution)/shard_map/ppermute | solution.py:692
  12.7 20.7 %all-to-all-start = ((bf16[16,208,128]{2,1,0:T(8,128)(2,1)}), bf16[16,208,128]{2,1,0:T(8,128)(2,1)S(1)}, u32[]{:S(2)}, u32[]{:S(2)}) async-start(bf16[16,208,128]{2,1,0:T(8,128)(2,1)} %project.1), calls=%async_computation | async-start | bytes 1703936 | tf_op jit(solution)/shard_map/all_to_all | solution.py:688
  19.2 61.5 %all-gather.9.cloned.1.call-start = ((), (), s32[]{:S(2)}) async-start(), calls=%async_computation.8 | async-start | bytes 2359296 | tf_op jit(solution)/shard_map/all_gather | solution.py:700
  19.3 16.6 %copy-start.2 = (bf16[2,128,1024]{2,1,0:T(8,128)(2,1)}, bf16[2,128,1024]{2,1,0:T(8,128)(2,1)S(1)}, u32[]{:S(2)}) copy-start(bf16[2,128,1024]{2,1,0:T(8,128)(2,1)S(1)} %pad_maximum_fusion.1.cot0_ref) | copy-start | bytes 1572868
  19.3 14.1 %collective-permute-start.1 = (bf16[2,128,1024]{2,1,0:T(8,128)(2,1)S(1)}, bf16[2,128,1024]{2,1,0:T(8,128)(2,1)S(1)}, u32[]{:S(2)}, u32[]{:S(2)}) collective-permute-start(bf16[2,128,1024]{2,1,0:T(8,128)(2,1)S(1)} %pad_maximum_fusion.1.cot0_ref), channel_id=1, source_target_pairs={{0,96},{32,0},{64,32},{96,64},{1,97},{33,1},{65,33},{97,65},{2,98}... | collective-permute-start | bytes 1572872 | tf_op jit(solution)/shard_map/ppermute | solution.py:696
  33.4 12.5 %copy-start.13 = (bf16[2,128,1024]{2,1,0:T(8,128)(2,1)}, bf16[2,128,1024]{2,1,0:T(8,128)(2,1)S(1)}, u32[]{:S(2)}) copy-start(bf16[2,128,1024]{2,1,0:T(8,128)(2,1)S(1)} %collective-permute-done.1.cot3_ref) | copy-start | bytes 1572868
  33.4 4.1 %copy-start = (bf16[16,208,128]{2,1,0:T(8,128)(2,1)}, bf16[16,208,128]{2,1,0:T(8,128)(2,1)S(1)}, u32[]{:S(2)}) copy-start(bf16[16,208,128]{2,1,0:T(8,128)(2,1)S(1)} %all-to-all-done.x_ref) | copy-start | bytes 2555908
  33.4 19.3 %copy-start.11 = (s32[1,128,2]{1,2,0:T(2,128)S(1)}, s32[1,128,2]{1,2,0:T(2,128)}, u32[]{:S(2)}) copy-start(s32[1,128,2]{1,2,0:T(2,128)} %param.17) | copy-start | bytes 3076
  33.4 20.0 %copy-start.10 = (bf16[1024,3]{0,1:T(4,128)(2,1)S(1)}, bf16[1024,3]{0,1:T(4,128)(2,1)}, u32[]{:S(2)}) copy-start(bf16[1024,3]{0,1:T(4,128)(2,1)} %param.24) | copy-start | bytes 18436
  33.5 27.0 %collective-permute-start.3 = (bf16[2,128,1024]{2,1,0:T(8,128)(2,1)S(1)}, bf16[2,128,1024]{2,1,0:T(8,128)(2,1)S(1)}, u32[]{:S(2)}, u32[]{:S(2)}) collective-permute-start(bf16[2,128,1024]{2,1,0:T(8,128)(2,1)S(1)} %pad_maximum_fusion.1.cot0_ref), channel_id=1, source_target_pairs={{0,64},{32,96},{64,0},{96,32},{1,65},{33,97},{65,1},{97,33},{2,66}... | collective-permute-start | bytes 1572872 | tf_op jit(solution)/shard_map/ppermute | solution.py:696
  35.9 24.5 %collective-permute-start.2 = (bf16[2,128,1024]{2,1,0:T(8,128)(2,1)S(1)}, bf16[2,128,1024]{2,1,0:T(8,128)(2,1)S(1)}, u32[]{:S(2)}, u32[]{:S(2)}) collective-permute-start(bf16[2,128,1024]{2,1,0:T(8,128)(2,1)S(1)} %pad_maximum_fusion.1.cot0_ref), channel_id=1, source_target_pairs={{0,32},{32,64},{64,96},{96,0},{1,33},{33,65},{65,97},{97,1},{2,34}... | collective-permute-start | bytes 1572872 | tf_op jit(solution)/shard_map/ppermute | solution.py:696
  45.9 14.5 %all-to-all-start.1 = ((bf16[16,64,128]{2,1,0:T(8,128)(2,1)}), bf16[16,64,128]{2,1,0:T(8,128)(2,1)S(1)}, u32[]{:S(2)}, u32[]{:S(2)}) async-start(bf16[16,64,128]{2,1,0:T(8,128)(2,1)} %get-tuple-element.69), calls=%async_computation.1 | async-start | bytes 524288 | tf_op jit(solution)/shard_map/all_to_all | solution.py:688
  52.7 54.6 %all-gather.11.cloned.1.call-start = ((), (), s32[]{:S(2)}) async-start(), calls=%async_computation.9 | async-start | bytes 2359296 | tf_op jit(solution)/shard_map/all_gather | solution.py:700
  60.4 4.1 %copy-start.14 = (bf16[2,128,1024]{2,1,0:T(8,128)(2,1)}, bf16[2,128,1024]{2,1,0:T(8,128)(2,1)S(1)}, u32[]{:S(2)}) copy-start(bf16[2,128,1024]{2,1,0:T(8,128)(2,1)S(1)} %collective-permute-done.3.cot2_ref) | copy-start | bytes 1572868
  60.4 4.1 %copy-start.15 = (bf16[2,128,1024]{2,1,0:T(8,128)(2,1)}, bf16[2,128,1024]{2,1,0:T(8,128)(2,1)S(1)}, u32[]{:S(2)}) copy-start(bf16[2,128,1024]{2,1,0:T(8,128)(2,1)S(1)} %collective-permute-done.2.cot1_ref) | copy-start | bytes 1572868
  64.6 62.6 %all-gather.13.cloned.1.call-start = ((), (), s32[]{:S(2)}) async-start(), calls=%async_computation.10 | async-start | bytes 2359296 | tf_op jit(solution)/shard_map/all_gather | solution.py:700
  64.6 11.3 %copy-start.19 = (bf16[8,64,128]{2,1,0:T(8,128)(2,1)S(1)}, bf16[8,64,128]{2,1,0:T(8,128)(2,1)}, u32[]{:S(2)}) copy-start(bf16[8,64,128]{2,1,0:T(8,128)(2,1)} %get-tuple-element.78) | copy-start | bytes 393220
  75.9 4.7 %collective-permute-start.4 = (bf16[8,64,128]{2,1,0:T(8,128)(2,1)S(1)}, bf16[8,64,128]{2,1,0:T(8,128)(2,1)S(1)}, u32[]{:S(2)}, u32[]{:S(2)}) collective-permute-start(bf16[8,64,128]{2,1,0:T(8,128)(2,1)S(1)} %copy-done.19), channel_id=1, source_target_pairs={{0,2},{2,0},{1,3},{3,1},{4,6},{6,4},{5,7},{7,5},{8,10},{10,8},{9,1... | collective-permute-start | bytes 393224 | tf_op jit(solution)/shard_map/ppermute | solution.py:692
  80.6 22.9 %copy-start.18 = (bf16[8,64,128]{2,1,0:T(8,128)(2,1)}, bf16[8,64,128]{2,1,0:T(8,128)(2,1)S(1)}, u32[]{:S(2)}) copy-start(bf16[8,64,128]{2,1,0:T(8,128)(2,1)S(1)} %collective-permute-done.4.att_other_ref) | copy-start | bytes 393220
  80.6 12.8 %all-to-all-start.2 = ((bf16[16,64,128]{2,1,0:T(8,128)(2,1)}), bf16[16,64,128]{2,1,0:T(8,128)(2,1)S(1)}, u32[]{:S(2)}, u32[]{:S(2)}) async-start(bf16[16,64,128]{2,1,0:T(8,128)(2,1)} %get-tuple-element.79), calls=%async_computation.2 | async-start | bytes 524288 | tf_op jit(solution)/shard_map/all_to_all | solution.py:688
  87.5 17.7 %copy-start.1 = (bf16[2,576,128]{2,1,0:T(8,128)(2,1)}, bf16[2,576,128]{2,1,0:T(8,128)(2,1)S(1)}, u32[]{:S(2)}) copy-start(bf16[2,576,128]{2,1,0:T(8,128)(2,1)S(1)} %get-tuple-element.90.acts0_ref) | copy-start | bytes 884740
  87.5 16.0 %collective-permute-start.7 = (bf16[2,576,128]{2,1,0:T(8,128)(2,1)S(1)}, bf16[2,576,128]{2,1,0:T(8,128)(2,1)S(1)}, u32[]{:S(2)}, u32[]{:S(2)}) collective-permute-start(bf16[2,576,128]{2,1,0:T(8,128)(2,1)S(1)} %get-tuple-element.120), channel_id=1, source_target_pairs={{0,96},{32,0},{64,32},{96,64},{1,97},{33,1},{65,33},{97,65},{2,98}... | collective-permute-start | bytes 884744 | tf_op jit(solution)/shard_map/ppermute | solution.py:696
  88.4 15.2 %collective-permute-start.6 = (bf16[2,576,128]{2,1,0:T(8,128)(2,1)S(1)}, bf16[2,576,128]{2,1,0:T(8,128)(2,1)S(1)}, u32[]{:S(2)}, u32[]{:S(2)}) collective-permute-start(bf16[2,576,128]{2,1,0:T(8,128)(2,1)S(1)} %get-tuple-element.121), channel_id=1, source_target_pairs={{0,64},{32,96},{64,0},{96,32},{1,65},{33,97},{65,1},{97,33},{2,66}... | collective-permute-start | bytes 884744 | tf_op jit(solution)/shard_map/ppermute | solution.py:696
  90.2 15.0 %collective-permute-start.5 = (bf16[2,576,128]{2,1,0:T(8,128)(2,1)S(1)}, bf16[2,576,128]{2,1,0:T(8,128)(2,1)S(1)}, u32[]{:S(2)}, u32[]{:S(2)}) collective-permute-start(bf16[2,576,128]{2,1,0:T(8,128)(2,1)S(1)} %get-tuple-element.122), channel_id=1, source_target_pairs={{0,32},{32,64},{64,96},{96,0},{1,33},{33,65},{65,97},{97,1},{2,34}... | collective-permute-start | bytes 884744 | tf_op jit(solution)/shard_map/ppermute | solution.py:696
  103.5 4.0 %copy-start.7 = (bf16[2,576,128]{2,1,0:T(8,128)(2,1)}, bf16[2,576,128]{2,1,0:T(8,128)(2,1)S(1)}, u32[]{:S(2)}) copy-start(bf16[2,576,128]{2,1,0:T(8,128)(2,1)S(1)} %collective-permute-done.7.acts3_ref) | copy-start | bytes 884740
  105.3 2.2 collective-permute-start.9
  105.9 10.8 %collective-permute-start.8 = (bf16[8,192,128]{2,1,0:T(8,128)(2,1)S(1)}, bf16[8,192,128]{2,1,0:T(8,128)(2,1)S(1)}, u32[]{:S(2)}, u32[]{:S(2)}) collective-permute-start(bf16[8,192,128]{2,1,0:T(8,128)(2,1)S(1)} %copy-done.16), channel_id=1, source_target_pairs={{0,2},{2,0},{1,3},{3,1},{4,6},{6,4},{5,7},{7,5},{8,10},{10,8},{9,1... | collective-permute-start | bytes 1179656 | tf_op jit(solution)/shard_map/ppermute | solution.py:692
  116.7 7.0 %copy-start.17 = (bf16[8,192,128]{2,1,0:T(8,128)(2,1)}, bf16[8,192,128]{2,1,0:T(8,128)(2,1)S(1)}, u32[]{:S(2)}) copy-start(bf16[8,192,128]{2,1,0:T(8,128)(2,1)S(1)} %collective-permute-done.8.theirs_ref) | copy-start | bytes 1179652
  116.7 24.1 %all-to-all-start.3 = ((bf16[16,288,128]{2,1,0:T(8,128)(2,1)}), bf16[16,288,128]{2,1,0:T(8,128)(2,1)S(1)}, u32[]{:S(2)}, u32[]{:S(2)}) async-start(bf16[16,288,128]{2,1,0:T(8,128)(2,1)} %expert_weights.1), calls=%async_computation.3 | async-start | bytes 2359296 | tf_op jit(solution)/shard_map/all_to_all | solution.py:688
  123.6 114.0 %all-gather.15.cloned.1.call-start = ((), (), s32[]{:S(2)}) async-start(), calls=%async_computation.11 | async-start | bytes 15851520 | tf_op jit(solution)/shard_map/all_gather | solution.py:700
  130.8 28.0 %copy-start.3 = (bf16[8,256,128]{2,1,0:T(8,128)(2,1)S(1)}, bf16[8,256,128]{2,1,0:T(8,128)(2,1)}, u32[]{:S(2)}) copy-start(bf16[8,256,128]{2,1,0:T(8,128)(2,1)} %get-tuple-element.107) | copy-start | bytes 1572868
  (6 other events, 10.9 us)
Sparse Core Ops, SparseCore 0:
  33.6 30.1 all-gather.8
  65.5 25.4 all-gather.10
  92.7 25.6 all-gather.12
  158.9 78.5 all-gather.14

commit v5 on v4

--- a/solution.py
+++ b/solution.py
@@ -30,7 +30,8 @@
 NR = 16
 FS = FF // NC
 GU = 2 * FS * EXPERTS
-ACTS = 3 * FS * EXPERTS
+SLOTS = 6 * FS
+ACTS = SLOTS + 16
 PIECE = 96
 PART = 3 * PIECE
 MINE = 2 * PIECE
@@ -315,7 +316,8 @@
 
 
 def resid_kernel(
-    att_ref, tok_ref, routes_ref, gain_ref, wr_ref, wo_ref, resid_ref, moe_ref, moe_t_ref, combine_ref
+    att_ref, tok_ref, routes_ref, gain_ref, wr_ref, wo_ref, resid_ref, moe_ref, moe_t_ref, combine_ref,
+    missing_ref,
 ):
     heads = [att_ref[device_of(h)] for h in range(HQ)]
     attended = swap(jnp.concatenate(heads, axis=0).astype(F32)).astype(BF)
@@ -331,6 +333,8 @@
     r0, r1 = routes_ref[:, 0:1], routes_ref[:, 1:2]
     l0 = jnp.sum(jnp.where(lane[:, :8] == r0, logits, 0.0), axis=1, keepdims=True)
     l1 = jnp.sum(jnp.where(lane[:, :8] == r1, logits, 0.0), axis=1, keepdims=True)
+    missing = (EXPERTS - r0 - r1).astype(F32)
+    missing_ref[...] = swap(jnp.broadcast_to(missing, (T, T)))[0:16].astype(BF)
     top = jnp.maximum(l0, l1)
     e0, e1 = jnp.exp(l0 - top), jnp.exp(l1 - top)
     total = e0 + e1
@@ -347,6 +351,7 @@
             jax.ShapeDtypeStruct((T, D), BF),
             jax.ShapeDtypeStruct((D, T), BF),
             jax.ShapeDtypeStruct((T, T), F32),
+            jax.ShapeDtypeStruct((16, T), BF),
         ),
         cost_estimate=cost(4),
         name="residual",
@@ -354,8 +359,8 @@
 
 
 def experts_kernel(
-    resid_ref, moe_ref, combine_ref, cot_ref, gain_ref, wr_ref, wo_ref, wg_ref, wu_ref, wd_ref,
-    out_ref, resid_grad_ref, grad_att_ref, grad_t_ref, acts_ref, small_ref,
+    resid_ref, moe_ref, combine_ref, missing_ref, cot_ref, gain_ref, wr_ref, wo_ref,
+    wg_ref, wu_ref, wd_ref, out_ref, resid_grad_ref, grad_att_ref, grad_t_ref, acts_ref, small_ref,
     mix_ref, moe_grad_ref, cgrad_ref,
 ):
     e, f = pl.program_id(0), pl.program_id(1)
@@ -385,18 +390,45 @@
     moe_grad_ref[...] += dot(gate_grad.astype(BF), wg_ref[0], NT) + dot(
         up_grad.astype(BF), wu_ref[0], NT
     )
-    gate_t = swap(gate_grad).astype(BF)
-    up_t = swap(up_grad).astype(BF)
-    act_t = swap(combine * act_low.astype(F32)).astype(BF)
-    at_gu = pl.multiple_of(2 * FS * e, FS)
-    at_down = pl.multiple_of(GU + FS * e, FS)
+    gate_t, up_t = swap(gate_grad), swap(up_grad)
+    act_t = swap(combine * act_low.astype(F32))
     core, y = lax.axis_index("core"), lax.axis_index("y")
-    for i in range(FC // FS):
-        j = f * (FC // FS) + i
-        j = 2 * ((j // 2 - y) & 3) + ((j & 1) ^ core)
-        acts_ref[j, pl.ds(at_gu, FS), :] = gate_t[FS * i : FS * (i + 1)]
-        acts_ref[j, pl.ds(at_gu + FS, FS), :] = up_t[FS * i : FS * (i + 1)]
-        acts_ref[j, pl.ds(at_down, FS), :] = act_t[FS * i : FS * (i + 1)]
+    missing = missing_ref[0:1].astype(F32)
+
+    def slices(put):
+        for i in range(FC // FS):
+            j = f * (FC // FS) + i
+            j = 2 * ((j // 2 - y) & 3) + ((j & 1) ^ core)
+            for k, a in enumerate((gate_t, up_t, act_t)):
+                put(j, (0, FS, 4 * FS)[k], (2 * FS, 3 * FS, 5 * FS)[k], a[FS * i : FS * (i + 1)])
+
+    @pl.when(e == 0)
+    def _():
+        def put(j, at_a, at_b, a):
+            acts_ref[j, at_a : at_a + FS, :] = a.astype(BF)
+
+        slices(put)
+        for j in range(NC):
+            acts_ref[j, SLOTS:, :] = missing_ref[...]
+
+    @pl.when(e == 1)
+    def _():
+        def put(j, at_a, at_b, a):
+            rows = slice(at_a, at_a + FS)
+            old = acts_ref[j, rows, :].astype(F32)
+            acts_ref[j, rows, :] = jnp.where(missing == 0.0, a, old).astype(BF)
+            acts_ref[j, at_b : at_b + FS, :] = a.astype(BF)
+
+        slices(put)
+
+    @pl.when(e == 2)
+    def _():
+        def put(j, at_a, at_b, a):
+            rows = slice(at_b, at_b + FS)
+            old = acts_ref[j, rows, :].astype(F32)
+            acts_ref[j, rows, :] = jnp.where(missing == 2.0, old, a).astype(BF)
+
+        slices(put)
 
     @pl.when((e == EXPERTS - 1) & (f == NF - 1))
     def _():
@@ -421,7 +453,7 @@
             grad_att_ref[device_of(h)] = grad_att[HD * h : HD * (h + 1)]
 
 
-def experts(resid, moe_low, combine, cotangent, gain, w_router, w_output, w_gate, w_up, w_down):
+def experts(resid, moe_low, combine, missing, cotangent, gain, w_router, w_output, w_gate, w_up, w_down):
     def whole(*shape):
         return pl.BlockSpec(shape, lambda e, f: (0,) * len(shape))
 
@@ -435,7 +467,7 @@
         experts_kernel,
         grid=(EXPERTS, NF),
         in_specs=[
-            whole(T, D), whole(T, D), whole(T, T), whole(T, D), whole(D), whole(8, D),
+            whole(T, D), whole(T, D), whole(T, T), whole(16, T), whole(T, D), whole(D), whole(8, D),
             whole(D, D), columns(), columns(), rows(),
         ],
         out_specs=(
@@ -457,7 +489,7 @@
         ],
         cost_estimate=cost(13),
         name="experts",
-    )(resid, moe_low, combine, cotangent, gain, w_router, w_output, w_gate, w_up, w_down)
+    )(resid, moe_low, combine, missing, cotangent, gain, w_router, w_output, w_gate, w_up, w_down)
 
 
 def side_by_side(ref, i, j):
@@ -474,8 +506,16 @@
         chip = 2 * ((y - back) & 3)
         near, far = chip + core, chip + 1 - core
         acts = jnp.concatenate([acts_ref[0], other_ref[back]], axis=1)
-        wide = dot(side_by_side(moe_ref, near, far), acts[0:GU], NT)
-        down = dot(acts[GU:], cot_refs[back][...].reshape(2 * T, D))
+        missing = acts[SLOTS : SLOTS + 1].astype(F32)
+        first, last = (jnp.where(missing == e, 0.0, 1.0).astype(BF) for e in (0.0, 2.0))
+
+        def by_expert(at, rows):
+            a, b = acts[at : at + rows], acts[at + rows : at + 2 * rows]
+            middle = a * (1 - first) + b * (1 - last)
+            return jnp.concatenate([a * first, middle, b * last], axis=0)
+
+        wide = dot(side_by_side(moe_ref, near, far), by_expert(0, 2 * FS), NT)
+        down = dot(by_expert(4 * FS, FS), cot_refs[back][...].reshape(2 * T, D))
         if back == 0:
             wide_ref[...] = wide
             down_ref[...] = down
@@ -540,6 +580,7 @@
     att_ref, att_other_ref, grad_ref, parts_ref, out_ref, heads_ref
 ):
     own, partner = own_rows(lax.axis_index("xl"))
+    y = lax.axis_index("y")
     o = jnp.zeros((2 * HD, D), F32)
     for b in range(NC):
         heads_ref[b, own, :] = att_ref[b]
@@ -549,8 +590,9 @@
     low = o.astype(BF)
     for i in range(NR):
         half, lanes = 64 * (i % 2), 128 * (i // 2)
-        out_ref[i, 0:128, :] = parts_ref[i, 0:128, :]
-        out_ref[i, 128:192, :] = low[half : half + 64, lanes : lanes + 128]
+        at = 4 * ((i // 4 - y) & 3) + i % 4
+        out_ref[at, 0:128, :] = parts_ref[i, 0:128, :]
+        out_ref[at, 128:192, :] = low[half : half + 64, lanes : lanes + 128]
 
 
 def output_weights(attended, attended_other, grad, parts):
@@ -701,7 +743,8 @@
 
 
 def spread_sum(part, axes, count):
-    return jnp.sum(exchange(jnp.broadcast_to(part[None], (count, *part.shape)), axes), axis=0)
+    parts = exchange(jnp.broadcast_to(part[None], (count, *part.shape)), axes)
+    return jnp.sum(parts.astype(F32), axis=0)
 
 
 def part_sum(parts, axes):
@@ -731,12 +774,12 @@
     attended, att_mine, att_sent, full, log_total, q, k, cosine, sine = attend(received)
     attended, cot1, cot2 = after(exchange(attended), cot1, cot2)
     att_theirs = swapped(att_sent, "xl")
-    resid, moe_low, moe_columns, combine = residual(
+    resid, moe_low, moe_columns, combine, missing = residual(
         attended, tokens, routes[0], expert_norm_gain, router_rows, w_output
     )
     moe_all = gather(moe_columns, RING)
     output, resid_grad, grad_att, grad_columns, acts, small = experts(
-        resid, moe_low, combine, cotangent, expert_norm_gain, router_rows, w_output,
+        resid, moe_low, combine, missing, cotangent, expert_norm_gain, router_rows, w_output,
         w_gate, w_up, w_down,
     )
     grad_att, normed_all, att_theirs = after(grad_att, normed_all, att_theirs)
@@ -756,14 +799,16 @@
     expert_part = part_sum(parts, PLANE)
     grads, weights = project_weights(mine, theirs, normed_all)
     weights = output_weights(att_mine, att_theirs, grad_all, weights)
+    ring = [weights[0:4]] + [ring_moved(weights[4 * r : 4 * r + 4], r) for r in (1, 2, 3)]
+    weights = sum(a.astype(F32) for a in ring).astype(BF)
     expert_part, weights = after(expert_part, weights)
-    project_part = part_sum(weights, REST)
+    project_part = part_sum(weights, ("xh", "xl"))
     gathered = gather(jnp.concatenate([expert_part, project_part], axis=0), ALL)
     grads, project_part = after(grads, project_part)
     token_grad, small = project_back(
         exchange(grads, COLUMN), tokens, attn_gain, w_query, w_key, w_value, resid_grad, small
     )
-    small = spread_sum(spread_sum(small, REST, NR), COLUMN, NC)
+    small = spread_sum(spread_sum(small.astype(BF), REST, NR), COLUMN, NC)
     dwq, dwk, dwv, dwo, dwg, dwu, dwd = assemble(
         gathered.reshape(4, 4, 2, 2, 2, PART + MINE, T)
     )

time: 263 us -> 259 us (0.985)
  blocking collectives: 58.5 us -> 50 us
    all_to_all x4, waiting for transfers between devices: 18.8 us -> 9.26 us  [exchange(): return lax.all_to_all(array, axes, 0, 0, tiled=True)]
    all_to_all x4, blocking collectives: 58.5 us -> 50 us  [exchange(): return lax.all_to_all(array, axes, 0, 0, tiled=True)]
    ppermute x6 -> x9, waiting for transfers between devices: 10.9 us -> 16.6 us  [ring_moved(): return lax.ppermute(array, 'y', [(i, (i + back) % 4) for i in range(4)])]
    ppermute x6 -> x9, starting transfers between devices: 10.3 us -> 13.9 us  [ring_moved(): return lax.ppermute(array, 'y', [(i, (i + back) % 4) for i in range(4)])]
    all_gather x4, waiting for transfers between devices: 30.3 us -> 33.7 us  [gather(): return lax.all_gather(array, axes, axis=0)]
    all_to_all x4, starting transfers between devices: 25.6 us -> 22.4 us  [exchange(): return lax.all_to_all(array, axes, 0, 0, tiled=True)]
  transfers between devices with their start and end apart: 18 -> 21, of which waited for: 9 -> 9; matrix products, arithmetic and copies ran while one was open for 2% -> 3% of each run, Pallas kernels for 20% -> 21%
where the time goes in v5:
time: 259 us; the launch traced here: 258 us
  Pallas kernels  75.5 us (29%)
  waiting for transfers between devices  67.4 us (26%)
  blocking collectives  50 us (19%)
  starting transfers between devices  40.6 us (16%)
  between operations  14.1 us (5%)
  local copies, waits for them, and re-layouts  7.34 us (3%)
  other arithmetic  2.82 us (1%)
    all_to_all x4, blocking collectives, exchange(): return lax.all_to_all(array, axes, 0, 0, tiled=True)  50 us
    all_gather x4, waiting for transfers between devices, gather(): return lax.all_gather(array, axes, axis=0)  33.7 us
    all_to_all x4, starting transfers between devices, exchange(): return lax.all_to_all(array, axes, 0, 0, tiled=True)  22.4 us
    pallas_call x1, Pallas kernels, assemble(): pl.pallas_call(assemble_kernel, grid=(4, 2), in_specs=[experts_of(0), exp...  17.7 us
    ppermute x9, waiting for transfers between devices, ring_moved(): return lax.ppermute(array, 'y', [(i, (i + back) % 4) for i in range(4)])  16.6 us
    ppermute x9, starting transfers between devices, ring_moved(): return lax.ppermute(array, 'y', [(i, (i + back) % 4) for i in range(4)])  13.9 us
    pallas_call x1, Pallas kernels, experts(): pl.pallas_call(experts_kernel, grid=(EXPERTS, NF), in_specs=[whole(T, D),...  11.4 us
    pallas_call x1, Pallas kernels, attend_back(): pl.pallas_call(attend_back_kernel, out_shape=(jax.ShapeDtypeStruct((NC, 3...  10.5 us
  transfers between devices with their start and end apart: 21, of which 9 were waited for; matrix products, arithmetic and copies ran while one was open for 3% of the time, Pallas kernels for 21%

profile of v5, /device:TPU:1, one launch (start us, length us, event | category | flops | bytes accessed | tf_op | source)
XLA Modules:
  0.0 257.7 jit_solution(16651011617958949275)
XLA Ops:
  7.2 4.1 %project.1 = bf16[16,208,128]{2,1,0:T(8,128)(2,1)} custom-call(bf16[128,1024]{1,0:T(8,128)(2,1)} %bitcast.35, s32[1,128]{1,0:T(1,128)} %seg_ref.1, bf16[1024]{0:T(1024)(128)(2,1)} %gain_ref.9, bf16[1024,1024]{1,0:T(8,128)(2,1)} %wq_ref.3, bf16[1024,512]{1,0:T(8,128)(2,1)} %wk_ref.3, bf16[1024,512]{1,0:T(8,128)(2,1)} %wv_ref.3), custom_call_target="tpu_custom_call" | custom-call | flops 4000000000 | bytes 1048576 | tf_op jit(solution)/shard_map/project/pallas_call | solution.py:96
  11.3 1.4 collective-permute-start
  12.7 6.5 %all-to-all-start = ((bf16[16,208,128]{2,1,0:T(8,128)(2,1)}), bf16[16,208,128]{2,1,0:T(8,128)(2,1)S(1)}, u32[]{:S(2)}, u32[]{:S(2)}) async-start(bf16[16,208,128]{2,1,0:T(8,128)(2,1)} %project.1), calls=%async_computation | async-start | bytes 1703936 | tf_op jit(solution)/shard_map/all_to_all | solution.py:730
  19.3 2.8 %collective-permute-start.1 = (bf16[2,128,1024]{2,1,0:T(8,128)(2,1)S(1)}, bf16[2,128,1024]{2,1,0:T(8,128)(2,1)S(1)}, u32[]{:S(2)}, u32[]{:S(2)}) collective-permute-start(bf16[2,128,1024]{2,1,0:T(8,128)(2,1)S(1)} %pad_maximum_fusion.cot0_ref), channel_id=1, source_target_pairs={{0,96},{32,0},{64,32},{96,64},{1,97},{33,1},{65,33},{97,65},{2,98}... | collective-permute-start | bytes 1572872 | tf_op jit(solution)/shard_map/ppermute | solution.py:738
  22.1 1.9 normed_columns.1
  24.1 9.3 %collective-permute-done.1.cot3_ref = bf16[2,128,1024]{2,1,0:T(8,128)(2,1)S(1)} collective-permute-done((bf16[2,128,1024]{2,1,0:T(8,128)(2,1)S(1)}, bf16[2,128,1024]{2,1,0:T(8,128)(2,1)S(1)}, u32[]{:S(2)}, u32[]{:S(2)}) %collective-permute-start.1) | collective-permute-done | bytes 524320 | tf_op jit(solution)/shard_map/ppermute | solution.py:738
  33.5 2.5 collective-permute-start.3
  35.9 1.6 collective-permute-start.2
  37.5 8.8 %attend.1 = (bf16[16,64,128]{2,1,0:T(8,128)(2,1)}, bf16[8,64,128]{2,1,0:T(8,128)(2,1)}, bf16[8,64,128]{2,1,0:T(8,128)(2,1)}, f32[8,64,256]{2,1,0:T(8,128)}, f32[...) custom-call(bf16[16,208,128]{2,1,0:T(8,128)(2,1)} %copy-done), custom_call_target="tpu_custom_call" | custom-call | flops 12999999488 | bytes 1048576 | tf_op jit(solution)/shard_map/attend/pallas_call | solution.py:213
  46.4 6.8 %all-to-all-start.1 = ((bf16[16,64,128]{2,1,0:T(8,128)(2,1)}), bf16[16,64,128]{2,1,0:T(8,128)(2,1)S(1)}, u32[]{:S(2)}, u32[]{:S(2)}) async-start(bf16[16,64,128]{2,1,0:T(8,128)(2,1)} %get-tuple-element.70), calls=%async_computation.1 | async-start | bytes 524288 | tf_op jit(solution)/shard_map/all_to_all | solution.py:730
  54.6 6.3 %all-to-all-done.1.att_ref = bf16[16,64,128]{2,1,0:T(8,128)(2,1)S(1)} async-done(((bf16[16,64,128]{2,1,0:T(8,128)(2,1)}), bf16[16,64,128]{2,1,0:T(8,128)(2,1)S(1)}, u32[]{:S(2)}, u32[]{:S(2)}) %all-to-all-start.1) | async-done | bytes 262176 | tf_op jit(solution)/shard_map/all_to_all | solution.py:730
  61.6 3.5 %residual.1 = (f32[128,1024]{1,0:T(8,128)}, bf16[128,1024]{1,0:T(8,128)(2,1)}, bf16[1024,128]{1,0:T(8,128)(2,1)}, f32[128,128]{1,0:T(8,128)}, bf16[16,128]{1,0:T(8,128)(2,1)}) custom-call(bf16[16,64,128]{2,1,0:T(8,128)(2,1)} %copy-done.5, bf16[128,1024]{1,0:T(8,128)(2,1)} %bitcast.37, s32[128,2]{1,0:T(8,128)} %bitcast.26, bf16[1024]{0:T(1024)(128)(2,1)} %gain_ref.8, ...), custom_call_target="tpu_custom_call" | custom-call | flops 4000000000 | bytes 1048576 | tf_op jit(solution)/shard_map/residual/pallas_call | solution.py:347
  65.2 11.4 %experts.1 = (bf16[128,1024]{1,0:T(8,128)(2,1)}, f32[128,1024]{1,0:T(8,128)}, bf16[16,64,128]{2,1,0:T(8,128)(2,1)}, bf16[1024,128]{1,0:T(8,128)(2,1)}, bf16[8,400,128]{2,1,0:T(8,128)(2,1)}, /*index=5*/f32[16,1024]{1,0:T(8,128)}) custom-call(f32[128,1024]{1,0:T(8,128)} %get-tuple-element.73.resid_ref, bf16[128,1024]{1,0:T(8,128)(2,1)} %get-tuple-element.74.moe_ref, ...), custom_call_target="tpu_custom_call" | custom-call | flops 12999999488 | bytes 1048576 | tf_op jit(solution)/shard_map/experts/pallas_call | solution.py:466
  77.9 3.5 %collective-permute-done.4.att_other_ref = bf16[8,64,128]{2,1,0:T(8,128)(2,1)S(1)} collective-permute-done((bf16[8,64,128]{2,1,0:T(8,128)(2,1)S(1)}, bf16[8,64,128]{2,1,0:T(8,128)(2,1)S(1)}, u32[]{:S(2)}, u32[]{:S(2)}) %collective-permute-start.4) | collective-permute-done | bytes 131104 | tf_op jit(solution)/shard_map/ppermute | solution.py:734
  81.4 5.5 %all-to-all-start.2 = ((bf16[16,64,128]{2,1,0:T(8,128)(2,1)}), bf16[16,64,128]{2,1,0:T(8,128)(2,1)S(1)}, u32[]{:S(2)}, u32[]{:S(2)}) async-start(bf16[16,64,128]{2,1,0:T(8,128)(2,1)} %get-tuple-element.81), calls=%async_computation.2 | async-start | bytes 524288 | tf_op jit(solution)/shard_map/all_to_all | solution.py:730
  91.2 2.9 %all-to-all-done.2.g_ref = bf16[16,64,128]{2,1,0:T(8,128)(2,1)S(1)} async-done(((bf16[16,64,128]{2,1,0:T(8,128)(2,1)}), bf16[16,64,128]{2,1,0:T(8,128)(2,1)S(1)}, u32[]{:S(2)}, u32[]{:S(2)}) %all-to-all-start.2) | async-done | bytes 262176 | tf_op jit(solution)/shard_map/all_to_all | solution.py:730
  94.8 10.5 %attend_back.1 = (bf16[8,192,128]{2,1,0:T(8,128)(2,1)}, bf16[8,192,128]{2,1,0:T(8,128)(2,1)}) custom-call(bf16[16,208,128]{2,1,0:T(8,128)(2,1)} %copy-done, bf16[16,64,128]{2,1,0:T(8,128)(2,1)} %copy-done.4, f32[8,64,256]{2,1,0:T(8,128)} %get-tuple-element.82.full_ref, f32[8,1,256]{2,1,0:T(1,128)} %get-tuple-element.83.log_ref, ...), custom_call_target="tpu_custom_call" | custom-call | flops 12999999488 | bytes 1048576 | tf_op jit(solution)/shard_map/attend_back/pallas_call | solution.py:289
  108.6 5.5 %expert_weights.1 = bf16[16,288,128]{2,1,0:T(8,128)(2,1)} custom-call(bf16[2,400,128]{2,1,0:T(8,128)(2,1)} %copy-done.3, bf16[2,400,128]{2,1,0:T(8,128)(2,1)} %copy-done.9, bf16[2,400,128]{2,1,0:T(8,128)(2,1)} %copy-done.8, bf16[2,400,128]{2,1,0:T(8,128)(2,1)} %copy-done.7, bf16[4,400,128]{2,1,0:T(8,128)(2,1)} %copy-done.15, bf16[8,1024,128]{2,1,0:T(8,128)(2,1)} %bitcast.34, ...), custom_call_target="tpu_custom_call" | custom-call | flops 5000000000 | bytes 1048576 | tf_op jit(solution)/shard_map/expert_weights/pallas_call | solution.py:535
  114.1 3.3 %collective-permute-done.8.theirs_ref = bf16[8,192,128]{2,1,0:T(8,128)(2,1)S(1)} collective-permute-done((bf16[8,192,128]{2,1,0:T(8,128)(2,1)}, bf16[8,192,128]{2,1,0:T(8,128)(2,1)S(1)}, u32[]{:S(2)}, u32[]{:S(2)}) %collective-permute-start.8) | collective-permute-done | bytes 393248 | tf_op jit(solution)/shard_map/ppermute | solution.py:734
  117.4 3.7 %all-to-all-start.3 = ((bf16[16,288,128]{2,1,0:T(8,128)(2,1)}), bf16[16,288,128]{2,1,0:T(8,128)(2,1)S(1)}, u32[]{:S(2)}, u32[]{:S(2)}) async-start(bf16[16,288,128]{2,1,0:T(8,128)(2,1)} %expert_weights.1), calls=%async_computation.3 | async-start | bytes 2359296 | tf_op jit(solution)/shard_map/all_to_all | solution.py:730
  121.1 3.5 %project_weights.1 = (bf16[8,256,128]{2,1,0:T(8,128)(2,1)}, bf16[16,192,128]{2,1,0:T(8,128)(2,1)}) custom-call(bf16[8,192,128]{2,1,0:T(8,128)(2,1)} %get-tuple-element.88.mine_ref, bf16[8,192,128]{2,1,0:T(8,128)(2,1)} %copy-done.16, bf16[8,1024,128]{2,1,0:T(8,128)(2,1)} %bitcast.32), custom_call_target="tpu_custom_call" | custom-call | flops 4000000000 | bytes 1048576 | tf_op jit(solution)/shard_map/project_weights/pallas_call | solution.py:568
  124.7 3.6 %output_weights.1 = bf16[16,192,128]{2,1,0:T(8,128)(2,1)} custom-call(bf16[8,64,128]{2,1,0:T(8,128)(2,1)} %get-tuple-element.104.att_ref, bf16[8,64,128]{2,1,0:T(8,128)(2,1)} %copy-done.17, bf16[8,1024,128]{2,1,0:T(8,128)(2,1)} %bitcast.33, bf16[16,192,128]{2,1,0:T(8,128)(2,1)} %get-tuple-element.107.parts_ref), custom_call_target="tpu_custom_call" | custom-call | flops 3000000000 | bytes 1048576 | tf_op jit(solution)/shard_map/output_weights/pallas_call | solution.py:599
  129.6 2.7 %collective-permute-start.12 = (bf16[4,192,128]{2,1,0:T(8,128)(2,1)S(1)}, bf16[4,192,128]{2,1,0:T(8,128)(2,1)S(1)}, u32[]{:S(2)}, u32[]{:S(2)}) collective-permute-start(bf16[4,192,128]{2,1,0:T(8,128)(2,1)S(1)} %get-tuple-element.127), channel_id=1, source_target_pairs={{0,96},{32,0},{64,32},{96,64},{1,97},{33,1},{65,33},{97,65},{2,98}... | collective-permute-start | bytes 589832 | tf_op jit(solution)/shard_map/ppermute | solution.py:738
  133.6 2.7 %collective-permute-done.10 = bf16[4,192,128]{2,1,0:T(8,128)(2,1)S(1)} collective-permute-done((bf16[4,192,128]{2,1,0:T(8,128)(2,1)S(1)}, bf16[4,192,128]{2,1,0:T(8,128)(2,1)S(1)}, u32[]{:S(2)}, u32[]{:S(2)}) %collective-permute-start.10) | collective-permute-done | bytes 196640 | tf_op jit(solution)/shard_map/ppermute | solution.py:738
  136.3 4.5 %collective-permute-done.11 = bf16[4,192,128]{2,1,0:T(8,128)(2,1)S(1)} collective-permute-done((bf16[4,192,128]{2,1,0:T(8,128)(2,1)S(1)}, bf16[4,192,128]{2,1,0:T(8,128)(2,1)S(1)}, u32[]{:S(2)}, u32[]{:S(2)}) %collective-permute-start.11) | collective-permute-done | bytes 196640 | tf_op jit(solution)/shard_map/ppermute | solution.py:738
  142.0 9.0 %all_to_all.40 = bf16[4,192,128]{2,1,0:T(8,128)(2,1)S(1)} all-to-all(bf16[4,192,128]{2,1,0:T(8,128)(2,1)S(1)} %add_convert_fusion), channel_id=1, replica_groups=mesh['y'=4,'xh'=2,'z'=4,'xl'=2,'core'=2] {'xh','xl'}, dimensions={0} | all-to-all | bytes 393216 | tf_op jit(solution)/shard_map/all_to_all | solution.py:730
  151.7 16.6 %all_to_all.41.g_ref = bf16[8,256,128]{2,1,0:T(8,128)(2,1)} all-to-all(bf16[8,256,128]{2,1,0:T(8,128)(2,1)S(1)} %copy-done.2), channel_id=1, replica_groups=mesh['y'=4,'xh'=2,'z'=4,'xl'=2,'core'=2] {'z','core'}, dimensions={0} | all-to-all | bytes 1048576 | tf_op jit(solution)/shard_map/all_to_all | solution.py:730
  168.2 5.0 %project_back.1 = (bf16[128,1024]{1,0:T(8,128)(2,1)}, f32[8,1024]{1,0:T(8,128)}) custom-call(bf16[8,256,128]{2,1,0:T(8,128)(2,1)} %all_to_all.41.g_ref, bf16[128,1024]{1,0:T(8,128)(2,1)} %bitcast.38, bf16[1024]{0:T(1024)(128)(2,1)} %gain_ref.9, bf16[1024,1024]{1,0:T(8,128)(2,1)} %wq_ref.3, bf16[1024,512]{1,0:T(8,128)(2,1)} %wk_ref.3, ...), custom_call_target="tpu_custom_call" | custom-call | flops 5000000000 | bytes 1048576 | tf_op jit(solution)/shard_map/project_back/pallas_call | solution.py:635
  174.0 12.1 %all_to_all.42 = bf16[16,8,1024]{2,1,0:T(8,128)(2,1)S(1)} all-to-all(bf16[16,8,1024]{2,1,0:T(8,128)(2,1)S(1)} %broadcast_in_dim.20), channel_id=1, replica_groups=mesh['y'=4,'xh'=2,'z'=4,'xl'=2,'core'=2] {'y','xh','xl'}, dimensions={0} | all-to-all | bytes 524288 | tf_op jit(solution)/shard_map/all_to_all | solution.py:730
  186.2 12.4 %all_to_all.43 = f32[8,8,1024]{2,1,0:T(8,128)S(1)} all-to-all(f32[8,8,1024]{2,1,0:T(8,128)S(1)} %broadcast_in_dim.21), channel_id=1, replica_groups=mesh['y'=4,'xh'=2,'z'=4,'xl'=2,'core'=2] {'z','core'}, dimensions={0} | all-to-all | bytes 524288 | tf_op jit(solution)/shard_map/all_to_all | solution.py:730
  199.8 33.7 %all-gather.15.cloned.1.call-done = bf16[61440,128]{1,0:T(8,128)(2,1)} async-done(((bf16[480,128]{1,0:T(8,128)(2,1)}), bf16[61440,128]{1,0:T(8,128)(2,1)}) %all-gather.15.cloned.1.call-update) | async-done | bytes 15728656 | tf_op jit(solution)/shard_map/all_gather | solution.py:742
  233.5 17.7 %assemble.1 = (f32[1024,1024]{1,0:T(8,128)}, f32[1024,512]{1,0:T(8,128)}, f32[1024,512]{1,0:T(8,128)}, f32[8,2,64,1024]{3,2,1,0:T(8,128)}, f32[3,1024,512]{2,1,0...) custom-call(bf16[4,4,2,2,2,480,128]{6,5,4,3,2,1,0:T(8,128)(2,1)} %bitcast.18, ...), custom_call_target="tpu_custom_call" | custom-call | flops 20000000000 | bytes 1048576 | tf_op jit(solution)/shard_map/assemble/pallas_call | solution.py:705
  (88 shorter events, 18.4 us)
Async XLA Ops:
  7.2 4.1 %copy-start.6 = (bf16[1,128,1024]{2,1,0:T(8,128)(2,1)S(1)}, bf16[1,128,1024]{2,1,0:T(8,128)(2,1)}, u32[]{:S(2)}) copy-start(bf16[1,128,1024]{2,1,0:T(8,128)(2,1)} %param.15) | copy-start | bytes 786436
  11.3 7.9 %collective-permute-start = (bf16[128,1024]{1,0:T(8,128)(2,1)S(1)}, bf16[128,1024]{1,0:T(8,128)(2,1)S(1)}, u32[]{:S(2)}, u32[]{:S(2)}) collective-permute-start(bf16[128,1024]{1,0:T(8,128)(2,1)S(1)} %bitcast.24), channel_id=1, source_target_pairs={{0,1},{1,0},{2,3},{3,2},{4,5},{5,4},{6,7},{7,6},{8,9},{9,8},{10,11... | collective-permute-start | bytes 786440 | tf_op jit(solution)/shard_map/ppermute | solution.py:734
  12.7 20.7 %all-to-all-start = ((bf16[16,208,128]{2,1,0:T(8,128)(2,1)}), bf16[16,208,128]{2,1,0:T(8,128)(2,1)S(1)}, u32[]{:S(2)}, u32[]{:S(2)}) async-start(bf16[16,208,128]{2,1,0:T(8,128)(2,1)} %project.1), calls=%async_computation | async-start | bytes 1703936 | tf_op jit(solution)/shard_map/all_to_all | solution.py:730
  19.2 62.2 %all-gather.9.cloned.1.call-start = ((), (), s32[]{:S(2)}) async-start(), calls=%async_computation.8 | async-start | bytes 2359296 | tf_op jit(solution)/shard_map/all_gather | solution.py:742
  19.3 16.6 %copy-start.1 = (bf16[2,128,1024]{2,1,0:T(8,128)(2,1)}, bf16[2,128,1024]{2,1,0:T(8,128)(2,1)S(1)}, u32[]{:S(2)}) copy-start(bf16[2,128,1024]{2,1,0:T(8,128)(2,1)S(1)} %pad_maximum_fusion.cot0_ref) | copy-start | bytes 1572868
  19.3 14.1 %collective-permute-start.1 = (bf16[2,128,1024]{2,1,0:T(8,128)(2,1)S(1)}, bf16[2,128,1024]{2,1,0:T(8,128)(2,1)S(1)}, u32[]{:S(2)}, u32[]{:S(2)}) collective-permute-start(bf16[2,128,1024]{2,1,0:T(8,128)(2,1)S(1)} %pad_maximum_fusion.cot0_ref), channel_id=1, source_target_pairs={{0,96},{32,0},{64,32},{96,64},{1,97},{33,1},{65,33},{97,65},{2,98}... | collective-permute-start | bytes 1572872 | tf_op jit(solution)/shard_map/ppermute | solution.py:738
  33.4 13.0 %copy-start.12 = (bf16[2,128,1024]{2,1,0:T(8,128)(2,1)}, bf16[2,128,1024]{2,1,0:T(8,128)(2,1)S(1)}, u32[]{:S(2)}) copy-start(bf16[2,128,1024]{2,1,0:T(8,128)(2,1)S(1)} %collective-permute-done.1.cot3_ref) | copy-start | bytes 1572868
  33.4 19.8 %copy-start.11 = (s32[1,128,2]{1,2,0:T(2,128)S(1)}, s32[1,128,2]{1,2,0:T(2,128)}, u32[]{:S(2)}) copy-start(s32[1,128,2]{1,2,0:T(2,128)} %param.17) | copy-start | bytes 3076
  33.4 20.5 %copy-start.10 = (bf16[1024,3]{0,1:T(4,128)(2,1)S(1)}, bf16[1024,3]{0,1:T(4,128)(2,1)}, u32[]{:S(2)}) copy-start(bf16[1024,3]{0,1:T(4,128)(2,1)} %param.24) | copy-start | bytes 18436
  33.5 27.5 %collective-permute-start.3 = (bf16[2,128,1024]{2,1,0:T(8,128)(2,1)S(1)}, bf16[2,128,1024]{2,1,0:T(8,128)(2,1)S(1)}, u32[]{:S(2)}, u32[]{:S(2)}) collective-permute-start(bf16[2,128,1024]{2,1,0:T(8,128)(2,1)S(1)} %pad_maximum_fusion.cot0_ref), channel_id=1, source_target_pairs={{0,64},{32,96},{64,0},{96,32},{1,65},{33,97},{65,1},{97,33},{2,66}... | collective-permute-start | bytes 1572872 | tf_op jit(solution)/shard_map/ppermute | solution.py:738
  35.9 25.0 %collective-permute-start.2 = (bf16[2,128,1024]{2,1,0:T(8,128)(2,1)S(1)}, bf16[2,128,1024]{2,1,0:T(8,128)(2,1)S(1)}, u32[]{:S(2)}, u32[]{:S(2)}) collective-permute-start(bf16[2,128,1024]{2,1,0:T(8,128)(2,1)S(1)} %pad_maximum_fusion.cot0_ref), channel_id=1, source_target_pairs={{0,32},{32,64},{64,96},{96,0},{1,33},{33,65},{65,97},{97,1},{2,34}... | collective-permute-start | bytes 1572872 | tf_op jit(solution)/shard_map/ppermute | solution.py:738
  46.4 14.5 %all-to-all-start.1 = ((bf16[16,64,128]{2,1,0:T(8,128)(2,1)}), bf16[16,64,128]{2,1,0:T(8,128)(2,1)S(1)}, u32[]{:S(2)}, u32[]{:S(2)}) async-start(bf16[16,64,128]{2,1,0:T(8,128)(2,1)} %get-tuple-element.70), calls=%async_computation.1 | async-start | bytes 524288 | tf_op jit(solution)/shard_map/all_to_all | solution.py:730
  53.2 53.7 %all-gather.11.cloned.1.call-start = ((), (), s32[]{:S(2)}) async-start(), calls=%async_computation.9 | async-start | bytes 2359296 | tf_op jit(solution)/shard_map/all_gather | solution.py:742
  60.9 4.2 %copy-start.13 = (bf16[2,128,1024]{2,1,0:T(8,128)(2,1)}, bf16[2,128,1024]{2,1,0:T(8,128)(2,1)S(1)}, u32[]{:S(2)}) copy-start(bf16[2,128,1024]{2,1,0:T(8,128)(2,1)S(1)} %collective-permute-done.3.cot2_ref) | copy-start | bytes 1572868
  60.9 4.2 %copy-start.14 = (bf16[2,128,1024]{2,1,0:T(8,128)(2,1)}, bf16[2,128,1024]{2,1,0:T(8,128)(2,1)S(1)}, u32[]{:S(2)}) copy-start(bf16[2,128,1024]{2,1,0:T(8,128)(2,1)S(1)} %collective-permute-done.2.cot1_ref) | copy-start | bytes 1572868
  65.2 59.5 %all-gather.13.cloned.1.call-start = ((), (), s32[]{:S(2)}) async-start(), calls=%async_computation.10 | async-start | bytes 2359296 | tf_op jit(solution)/shard_map/all_gather | solution.py:742
  65.2 11.5 %copy-start.18 = (bf16[8,64,128]{2,1,0:T(8,128)(2,1)S(1)}, bf16[8,64,128]{2,1,0:T(8,128)(2,1)}, u32[]{:S(2)}) copy-start(bf16[8,64,128]{2,1,0:T(8,128)(2,1)} %get-tuple-element.80) | copy-start | bytes 393220
  76.7 4.7 %collective-permute-start.4 = (bf16[8,64,128]{2,1,0:T(8,128)(2,1)S(1)}, bf16[8,64,128]{2,1,0:T(8,128)(2,1)S(1)}, u32[]{:S(2)}, u32[]{:S(2)}) collective-permute-start(bf16[8,64,128]{2,1,0:T(8,128)(2,1)S(1)} %copy-done.18), channel_id=1, source_target_pairs={{0,2},{2,0},{1,3},{3,1},{4,6},{6,4},{5,7},{7,5},{8,10},{10,8},{9,1... | collective-permute-start | bytes 393224 | tf_op jit(solution)/shard_map/ppermute | solution.py:734
  81.4 23.8 %copy-start.17 = (bf16[8,64,128]{2,1,0:T(8,128)(2,1)}, bf16[8,64,128]{2,1,0:T(8,128)(2,1)S(1)}, u32[]{:S(2)}) copy-start(bf16[8,64,128]{2,1,0:T(8,128)(2,1)S(1)} %collective-permute-done.4.att_other_ref) | copy-start | bytes 393220
  81.4 12.6 %all-to-all-start.2 = ((bf16[16,64,128]{2,1,0:T(8,128)(2,1)}), bf16[16,64,128]{2,1,0:T(8,128)(2,1)S(1)}, u32[]{:S(2)}, u32[]{:S(2)}) async-start(bf16[16,64,128]{2,1,0:T(8,128)(2,1)} %get-tuple-element.81), calls=%async_computation.2 | async-start | bytes 524288 | tf_op jit(solution)/shard_map/all_to_all | solution.py:730
  88.2 17.1 %copy-start.3 = (bf16[2,400,128]{2,1,0:T(8,128)(2,1)}, bf16[2,400,128]{2,1,0:T(8,128)(2,1)S(1)}, u32[]{:S(2)}) copy-start(bf16[2,400,128]{2,1,0:T(8,128)(2,1)S(1)} %get-tuple-element.92.acts0_ref) | copy-start | bytes 614404
  88.2 17.0 %collective-permute-start.7 = (bf16[2,400,128]{2,1,0:T(8,128)(2,1)S(1)}, bf16[2,400,128]{2,1,0:T(8,128)(2,1)S(1)}, u32[]{:S(2)}, u32[]{:S(2)}) collective-permute-start(bf16[2,400,128]{2,1,0:T(8,128)(2,1)S(1)} %get-tuple-element.122), channel_id=1, source_target_pairs={{0,96},{32,0},{64,32},{96,64},{1,97},{33,1},{65,33},{97,65},{2,98}... | collective-permute-start | bytes 614408 | tf_op jit(solution)/shard_map/ppermute | solution.py:738
  89.0 16.2 %collective-permute-start.6 = (bf16[2,400,128]{2,1,0:T(8,128)(2,1)S(1)}, bf16[2,400,128]{2,1,0:T(8,128)(2,1)S(1)}, u32[]{:S(2)}, u32[]{:S(2)}) collective-permute-start(bf16[2,400,128]{2,1,0:T(8,128)(2,1)S(1)} %get-tuple-element.123), channel_id=1, source_target_pairs={{0,64},{32,96},{64,0},{96,32},{1,65},{33,97},{65,1},{97,33},{2,66}... | collective-permute-start | bytes 614408 | tf_op jit(solution)/shard_map/ppermute | solution.py:738
  90.4 14.9 %collective-permute-start.5 = (bf16[2,400,128]{2,1,0:T(8,128)(2,1)S(1)}, bf16[2,400,128]{2,1,0:T(8,128)(2,1)S(1)}, u32[]{:S(2)}, u32[]{:S(2)}) collective-permute-start(bf16[2,400,128]{2,1,0:T(8,128)(2,1)S(1)} %get-tuple-element.124), channel_id=1, source_target_pairs={{0,32},{32,64},{64,96},{96,0},{1,33},{33,65},{65,97},{97,1},{2,34}... | collective-permute-start | bytes 614408 | tf_op jit(solution)/shard_map/ppermute | solution.py:738
  105.4 2.4 collective-permute-start.9
  106.5 10.9 %collective-permute-start.8 = (bf16[8,192,128]{2,1,0:T(8,128)(2,1)}, bf16[8,192,128]{2,1,0:T(8,128)(2,1)S(1)}, u32[]{:S(2)}, u32[]{:S(2)}) collective-permute-start(bf16[8,192,128]{2,1,0:T(8,128)(2,1)} %get-tuple-element.91), channel_id=1, source_target_pairs={{0,2},{2,0},{1,3},{3,1},{4,6},{6,4},{5,7},{7,5},{8,10},{10,8},{9,1... | collective-permute-start | bytes 1179656 | tf_op jit(solution)/shard_map/ppermute | solution.py:734
  117.4 24.4 %all-to-all-start.3 = ((bf16[16,288,128]{2,1,0:T(8,128)(2,1)}), bf16[16,288,128]{2,1,0:T(8,128)(2,1)S(1)}, u32[]{:S(2)}, u32[]{:S(2)}) async-start(bf16[16,288,128]{2,1,0:T(8,128)(2,1)} %expert_weights.1), calls=%async_computation.3 | async-start | bytes 2359296 | tf_op jit(solution)/shard_map/all_to_all | solution.py:730
  121.1 112.4 %all-gather.15.cloned.1.call-start = ((), (), s32[]{:S(2)}) async-start(), calls=%async_computation.11 | async-start | bytes 15851520 | tf_op jit(solution)/shard_map/all_gather | solution.py:742
  128.3 23.4 %copy-start.2 = (bf16[8,256,128]{2,1,0:T(8,128)(2,1)S(1)}, bf16[8,256,128]{2,1,0:T(8,128)(2,1)}, u32[]{:S(2)}) copy-start(bf16[8,256,128]{2,1,0:T(8,128)(2,1)} %get-tuple-element.109) | copy-start | bytes 1572868
  129.5 6.8 %collective-permute-start.10 = (bf16[4,192,128]{2,1,0:T(8,128)(2,1)S(1)}, bf16[4,192,128]{2,1,0:T(8,128)(2,1)S(1)}, u32[]{:S(2)}, u32[]{:S(2)}) collective-permute-start(bf16[4,192,128]{2,1,0:T(8,128)(2,1)S(1)} %get-tuple-element.126), channel_id=1, source_target_pairs={{0,32},{32,64},{64,96},{96,0},{1,33},{33,65},{65,97},{97,1},{2,34}... | collective-permute-start | bytes 589832 | tf_op jit(solution)/shard_map/ppermute | solution.py:738
  129.6 6.7 %collective-permute-start.12 = (bf16[4,192,128]{2,1,0:T(8,128)(2,1)S(1)}, bf16[4,192,128]{2,1,0:T(8,128)(2,1)S(1)}, u32[]{:S(2)}, u32[]{:S(2)}) collective-permute-start(bf16[4,192,128]{2,1,0:T(8,128)(2,1)S(1)} %get-tuple-element.127), channel_id=1, source_target_pairs={{0,96},{32,0},{64,32},{96,64},{1,97},{33,1},{65,33},{97,65},{2,98}... | collective-permute-start | bytes 589832 | tf_op jit(solution)/shard_map/ppermute | solution.py:738
  132.2 8.5 %collective-permute-start.11 = (bf16[4,192,128]{2,1,0:T(8,128)(2,1)S(1)}, bf16[4,192,128]{2,1,0:T(8,128)(2,1)S(1)}, u32[]{:S(2)}, u32[]{:S(2)}) collective-permute-start(bf16[4,192,128]{2,1,0:T(8,128)(2,1)S(1)} %get-tuple-element.128), channel_id=1, source_target_pairs={{0,64},{32,96},{64,0},{96,32},{1,65},{33,97},{65,1},{97,33},{2,66}... | collective-permute-start | bytes 589832 | tf_op jit(solution)/shard_map/ppermute | solution.py:738
  (8 other events, 17.9 us)
Sparse Core Ops, SparseCore 0:
  33.6 29.8 all-gather.8
  65.3 25.6 all-gather.10
  92.7 25.6 all-gather.12
  151.8 81.6 all-gather.14

commit v6 on v5

--- a/solution.py
+++ b/solution.py
@@ -772,8 +772,9 @@
     cot1, cot2 = ring_moved(cot, 1), ring_moved(cot, 2)
     normed_all = gather(normed, COLUMN)
     attended, att_mine, att_sent, full, log_total, q, k, cosine, sine = attend(received)
-    attended, cot1, cot2 = after(exchange(attended), cot1, cot2)
-    att_theirs = swapped(att_sent, "xl")
+    attended, cot1, cot2, att_theirs = after(
+        exchange(attended), cot1, cot2, swapped(att_sent, "xl")
+    )
     resid, moe_low, moe_columns, combine, missing = residual(
         attended, tokens, routes[0], expert_norm_gain, router_rows, w_output
     )
@@ -782,12 +783,11 @@
         resid, moe_low, combine, missing, cotangent, expert_norm_gain, router_rows, w_output,
         w_gate, w_up, w_down,
     )
-    grad_att, normed_all, att_theirs = after(grad_att, normed_all, att_theirs)
-    acts = [acts[0:2]] + [
-        ring_moved(acts[2 * back : 2 * back + 2], back) for back in (1, 2, 3)
-    ]
+    grad_att, normed_all = after(grad_att, normed_all)
     grad_all = gather(grad_columns, COLUMN)
-    grad_att = exchange(grad_att)
+    acts = [acts[2 * back : 2 * back + 2] for back in range(4)]
+    grad_att, *acts = after(exchange(grad_att), *acts)
+    acts = acts[:1] + [ring_moved(acts[back], back) for back in (1, 2, 3)]
     mine, sent = attend_back(
         received, grad_att, full, log_total, q, k, cosine, sine
     )

time: 259 us -> 258 us (level)
    all_to_all x4, waiting for transfers between devices: 9.26 us -> 5.85 us  [exchange(): return lax.all_to_all(array, axes, 0, 0, tiled=True)]
  transfers between devices with their start and end apart: 21 -> 21, of which waited for: 9 -> 8; matrix products, arithmetic and copies ran while one was open for 3% -> 3% of each run, Pallas kernels for 21% -> 21%
where the time goes in v6:
time: 258 us; the launch traced here: 256 us
  Pallas kernels  75.4 us (29%)
  waiting for transfers between devices  65.6 us (25%)
  blocking collectives  51.1 us (20%)
  starting transfers between devices  40.8 us (16%)
  between operations  14.1 us (5%)
  local copies, waits for them, and re-layouts  6.69 us (3%)
  other arithmetic  2.82 us (1%)
    all_to_all x4, blocking collectives, exchange(): return lax.all_to_all(array, axes, 0, 0, tiled=True)  51.1 us
    all_gather x4, waiting for transfers between devices, gather(): return lax.all_gather(array, axes, axis=0)  33.7 us
    all_to_all x4, starting transfers between devices, exchange(): return lax.all_to_all(array, axes, 0, 0, tiled=True)  22 us
    pallas_call x1, Pallas kernels, assemble(): pl.pallas_call(assemble_kernel, grid=(4, 2), in_specs=[experts_of(0), exp...  17.7 us
    ppermute x9, waiting for transfers between devices, ring_moved(): return lax.ppermute(array, 'y', [(i, (i + back) % 4) for i in range(4)])  16.3 us
    ppermute x9, starting transfers between devices, ring_moved(): return lax.ppermute(array, 'y', [(i, (i + back) % 4) for i in range(4)])  13.5 us
    pallas_call x1, Pallas kernels, experts(): pl.pallas_call(experts_kernel, grid=(EXPERTS, NF), in_specs=[whole(T, D),...  11.4 us
    pallas_call x1, Pallas kernels, attend_back(): pl.pallas_call(attend_back_kernel, out_shape=(jax.ShapeDtypeStruct((NC, 3...  10.4 us
  transfers between devices with their start and end apart: 21, of which 8 were waited for; matrix products, arithmetic and copies ran while one was open for 3% of the time, Pallas kernels for 21%

profile of v6, /device:TPU:1, one launch (start us, length us, event | category | flops | bytes accessed | tf_op | source)
XLA Modules:
  0.0 256.4 jit_solution(12404001014131712385)
XLA Ops:
  7.2 4.1 %project.1 = bf16[16,208,128]{2,1,0:T(8,128)(2,1)} custom-call(bf16[128,1024]{1,0:T(8,128)(2,1)} %bitcast.35, s32[1,128]{1,0:T(1,128)} %seg_ref.1, bf16[1024]{0:T(1024)(128)(2,1)} %gain_ref.9, bf16[1024,1024]{1,0:T(8,128)(2,1)} %wq_ref.3, bf16[1024,512]{1,0:T(8,128)(2,1)} %wk_ref.3, bf16[1024,512]{1,0:T(8,128)(2,1)} %wv_ref.3), custom_call_target="tpu_custom_call" | custom-call | flops 4000000000 | bytes 1048576 | tf_op jit(solution)/shard_map/project/pallas_call | solution.py:96
  12.7 6.5 %all-to-all-start = ((bf16[16,208,128]{2,1,0:T(8,128)(2,1)}), bf16[16,208,128]{2,1,0:T(8,128)(2,1)S(1)}, u32[]{:S(2)}, u32[]{:S(2)}) async-start(bf16[16,208,128]{2,1,0:T(8,128)(2,1)} %project.1), calls=%async_computation | async-start | bytes 1703936 | tf_op jit(solution)/shard_map/all_to_all | solution.py:730
  19.3 2.8 %collective-permute-start.1 = (bf16[2,128,1024]{2,1,0:T(8,128)(2,1)S(1)}, bf16[2,128,1024]{2,1,0:T(8,128)(2,1)S(1)}, u32[]{:S(2)}, u32[]{:S(2)}) collective-permute-start(bf16[2,128,1024]{2,1,0:T(8,128)(2,1)S(1)} %pad_maximum_fusion.cot0_ref), channel_id=1, source_target_pairs={{0,96},{32,0},{64,32},{96,64},{1,97},{33,1},{65,33},{97,65},{2,98}... | collective-permute-start | bytes 1572872 | tf_op jit(solution)/shard_map/ppermute | solution.py:738
  22.1 1.9 normed_columns.1
  24.1 9.3 %collective-permute-done.1.cot3_ref = bf16[2,128,1024]{2,1,0:T(8,128)(2,1)S(1)} collective-permute-done((bf16[2,128,1024]{2,1,0:T(8,128)(2,1)S(1)}, bf16[2,128,1024]{2,1,0:T(8,128)(2,1)S(1)}, u32[]{:S(2)}, u32[]{:S(2)}) %collective-permute-start.1) | collective-permute-done | bytes 524320 | tf_op jit(solution)/shard_map/ppermute | solution.py:738
  33.5 2.5 collective-permute-start.3
  35.9 1.6 collective-permute-start.2
  37.5 8.8 %attend.1 = (bf16[16,64,128]{2,1,0:T(8,128)(2,1)}, bf16[8,64,128]{2,1,0:T(8,128)(2,1)}, bf16[8,64,128]{2,1,0:T(8,128)(2,1)}, f32[8,64,256]{2,1,0:T(8,128)}, f32[...) custom-call(bf16[16,208,128]{2,1,0:T(8,128)(2,1)} %copy-done), custom_call_target="tpu_custom_call" | custom-call | flops 12999999488 | bytes 1048576 | tf_op jit(solution)/shard_map/attend/pallas_call | solution.py:213
  46.4 6.8 %all-to-all-start.1 = ((bf16[16,64,128]{2,1,0:T(8,128)(2,1)}), bf16[16,64,128]{2,1,0:T(8,128)(2,1)S(1)}, u32[]{:S(2)}, u32[]{:S(2)}) async-start(bf16[16,64,128]{2,1,0:T(8,128)(2,1)} %get-tuple-element.75), calls=%async_computation.1 | async-start | bytes 524288 | tf_op jit(solution)/shard_map/all_to_all | solution.py:730
  56.0 5.2 %collective-permute-done.4.att_other_ref = bf16[8,64,128]{2,1,0:T(8,128)(2,1)S(1)} collective-permute-done((bf16[8,64,128]{2,1,0:T(8,128)(2,1)}, bf16[8,64,128]{2,1,0:T(8,128)(2,1)S(1)}, u32[]{:S(2)}, u32[]{:S(2)}) %collective-permute-start.4) | collective-permute-done | bytes 131104 | tf_op jit(solution)/shard_map/ppermute | solution.py:734
  62.0 3.5 %residual.1 = (f32[128,1024]{1,0:T(8,128)}, bf16[128,1024]{1,0:T(8,128)(2,1)}, bf16[1024,128]{1,0:T(8,128)(2,1)}, f32[128,128]{1,0:T(8,128)}, bf16[16,128]{1,0:T(8,128)(2,1)}) custom-call(bf16[16,64,128]{2,1,0:T(8,128)(2,1)} %copy-done.5, bf16[128,1024]{1,0:T(8,128)(2,1)} %bitcast.37, s32[128,2]{1,0:T(8,128)} %bitcast.26, bf16[1024]{0:T(1024)(128)(2,1)} %gain_ref.8, ...), custom_call_target="tpu_custom_call" | custom-call | flops 4000000000 | bytes 1048576 | tf_op jit(solution)/shard_map/residual/pallas_call | solution.py:347
  65.6 11.4 %experts.1 = (bf16[128,1024]{1,0:T(8,128)(2,1)}, f32[128,1024]{1,0:T(8,128)}, bf16[16,64,128]{2,1,0:T(8,128)(2,1)}, bf16[1024,128]{1,0:T(8,128)(2,1)}, bf16[8,400,128]{2,1,0:T(8,128)(2,1)}, /*index=5*/f32[16,1024]{1,0:T(8,128)}) custom-call(f32[128,1024]{1,0:T(8,128)} %get-tuple-element.79.resid_ref, bf16[128,1024]{1,0:T(8,128)(2,1)} %get-tuple-element.80.moe_ref, ...), custom_call_target="tpu_custom_call" | custom-call | flops 12999999488 | bytes 1048576 | tf_op jit(solution)/shard_map/experts/pallas_call | solution.py:466
  77.1 5.0 %all-to-all-start.2 = ((bf16[16,64,128]{2,1,0:T(8,128)(2,1)}), bf16[16,64,128]{2,1,0:T(8,128)(2,1)S(1)}, u32[]{:S(2)}, u32[]{:S(2)}) async-start(bf16[16,64,128]{2,1,0:T(8,128)(2,1)} %get-tuple-element.86), calls=%async_computation.2 | async-start | bytes 524288 | tf_op jit(solution)/shard_map/all_to_all | solution.py:730
  83.4 5.8 %all-to-all-done.2.g_ref = bf16[16,64,128]{2,1,0:T(8,128)(2,1)S(1)} async-done(((bf16[16,64,128]{2,1,0:T(8,128)(2,1)}), bf16[16,64,128]{2,1,0:T(8,128)(2,1)S(1)}, u32[]{:S(2)}, u32[]{:S(2)}) %all-to-all-start.2) | async-done | bytes 262176 | tf_op jit(solution)/shard_map/all_to_all | solution.py:730
  89.3 1.8 collective-permute-start.6
  92.6 10.4 %attend_back.1 = (bf16[8,192,128]{2,1,0:T(8,128)(2,1)}, bf16[8,192,128]{2,1,0:T(8,128)(2,1)}) custom-call(bf16[16,208,128]{2,1,0:T(8,128)(2,1)} %copy-done, bf16[16,64,128]{2,1,0:T(8,128)(2,1)} %copy-done.4, f32[8,64,256]{2,1,0:T(8,128)} %get-tuple-element.89.full_ref, f32[8,1,256]{2,1,0:T(1,128)} %get-tuple-element.90.log_ref, ...), custom_call_target="tpu_custom_call" | custom-call | flops 12999999488 | bytes 1048576 | tf_op jit(solution)/shard_map/attend_back/pallas_call | solution.py:289
  103.2 1.9 collective-permute-start.9
  107.2 5.4 %expert_weights.1 = bf16[16,288,128]{2,1,0:T(8,128)(2,1)} custom-call(bf16[2,400,128]{2,1,0:T(8,128)(2,1)} %copy-done.3, bf16[2,400,128]{2,1,0:T(8,128)(2,1)} %copy-done.7, bf16[2,400,128]{2,1,0:T(8,128)(2,1)} %copy-done.8, bf16[2,400,128]{2,1,0:T(8,128)(2,1)} %copy-done.9, bf16[4,400,128]{2,1,0:T(8,128)(2,1)} %copy-done.15, bf16[8,1024,128]{2,1,0:T(8,128)(2,1)} %bitcast.34, ...), custom_call_target="tpu_custom_call" | custom-call | flops 5000000000 | bytes 1048576 | tf_op jit(solution)/shard_map/expert_weights/pallas_call | solution.py:535
  112.6 3.5 %collective-permute-done.8.theirs_ref = bf16[8,192,128]{2,1,0:T(8,128)(2,1)S(1)} collective-permute-done((bf16[8,192,128]{2,1,0:T(8,128)(2,1)}, bf16[8,192,128]{2,1,0:T(8,128)(2,1)S(1)}, u32[]{:S(2)}, u32[]{:S(2)}) %collective-permute-start.8) | collective-permute-done | bytes 393248 | tf_op jit(solution)/shard_map/ppermute | solution.py:734
  116.1 3.7 %all-to-all-start.3 = ((bf16[16,288,128]{2,1,0:T(8,128)(2,1)}), bf16[16,288,128]{2,1,0:T(8,128)(2,1)S(1)}, u32[]{:S(2)}, u32[]{:S(2)}) async-start(bf16[16,288,128]{2,1,0:T(8,128)(2,1)} %expert_weights.1), calls=%async_computation.3 | async-start | bytes 2359296 | tf_op jit(solution)/shard_map/all_to_all | solution.py:730
  119.8 3.5 %project_weights.1 = (bf16[8,256,128]{2,1,0:T(8,128)(2,1)}, bf16[16,192,128]{2,1,0:T(8,128)(2,1)}) custom-call(bf16[8,192,128]{2,1,0:T(8,128)(2,1)} %get-tuple-element.95.mine_ref, bf16[8,192,128]{2,1,0:T(8,128)(2,1)} %copy-done.16, bf16[8,1024,128]{2,1,0:T(8,128)(2,1)} %bitcast.32), custom_call_target="tpu_custom_call" | custom-call | flops 4000000000 | bytes 1048576 | tf_op jit(solution)/shard_map/project_weights/pallas_call | solution.py:568
  123.4 3.6 %output_weights.1 = bf16[16,192,128]{2,1,0:T(8,128)(2,1)} custom-call(bf16[8,64,128]{2,1,0:T(8,128)(2,1)} %get-tuple-element.114.att_ref, bf16[8,64,128]{2,1,0:T(8,128)(2,1)} %copy-done.17, bf16[8,1024,128]{2,1,0:T(8,128)(2,1)} %bitcast.33, bf16[16,192,128]{2,1,0:T(8,128)(2,1)} %get-tuple-element.117.parts_ref), custom_call_target="tpu_custom_call" | custom-call | flops 3000000000 | bytes 1048576 | tf_op jit(solution)/shard_map/output_weights/pallas_call | solution.py:599
  128.3 2.7 %collective-permute-start.12 = (bf16[4,192,128]{2,1,0:T(8,128)(2,1)S(1)}, bf16[4,192,128]{2,1,0:T(8,128)(2,1)S(1)}, u32[]{:S(2)}, u32[]{:S(2)}) collective-permute-start(bf16[4,192,128]{2,1,0:T(8,128)(2,1)S(1)} %get-tuple-element.137), channel_id=1, source_target_pairs={{0,96},{32,0},{64,32},{96,64},{1,97},{33,1},{65,33},{97,65},{2,98}... | collective-permute-start | bytes 589832 | tf_op jit(solution)/shard_map/ppermute | solution.py:738
  131.5 3.7 %collective-permute-done.10 = bf16[4,192,128]{2,1,0:T(8,128)(2,1)S(1)} collective-permute-done((bf16[4,192,128]{2,1,0:T(8,128)(2,1)S(1)}, bf16[4,192,128]{2,1,0:T(8,128)(2,1)S(1)}, u32[]{:S(2)}, u32[]{:S(2)}) %collective-permute-start.10) | collective-permute-done | bytes 196640 | tf_op jit(solution)/shard_map/ppermute | solution.py:738
  135.1 3.3 %collective-permute-done.11 = bf16[4,192,128]{2,1,0:T(8,128)(2,1)S(1)} collective-permute-done((bf16[4,192,128]{2,1,0:T(8,128)(2,1)S(1)}, bf16[4,192,128]{2,1,0:T(8,128)(2,1)S(1)}, u32[]{:S(2)}, u32[]{:S(2)}) %collective-permute-start.11) | collective-permute-done | bytes 196640 | tf_op jit(solution)/shard_map/ppermute | solution.py:738
  139.7 9.0 %all_to_all.40 = bf16[4,192,128]{2,1,0:T(8,128)(2,1)S(1)} all-to-all(bf16[4,192,128]{2,1,0:T(8,128)(2,1)S(1)} %add_convert_fusion), channel_id=1, replica_groups=mesh['y'=4,'xh'=2,'z'=4,'xl'=2,'core'=2] {'xh','xl'}, dimensions={0} | all-to-all | bytes 393216 | tf_op jit(solution)/shard_map/all_to_all | solution.py:730
  149.4 17.6 %all_to_all.41.g_ref = bf16[8,256,128]{2,1,0:T(8,128)(2,1)} all-to-all(bf16[8,256,128]{2,1,0:T(8,128)(2,1)S(1)} %copy-done.2), channel_id=1, replica_groups=mesh['y'=4,'xh'=2,'z'=4,'xl'=2,'core'=2] {'z','core'}, dimensions={0} | all-to-all | bytes 1048576 | tf_op jit(solution)/shard_map/all_to_all | solution.py:730
  167.0 5.0 %project_back.1 = (bf16[128,1024]{1,0:T(8,128)(2,1)}, f32[8,1024]{1,0:T(8,128)}) custom-call(bf16[8,256,128]{2,1,0:T(8,128)(2,1)} %all_to_all.41.g_ref, bf16[128,1024]{1,0:T(8,128)(2,1)} %bitcast.38, bf16[1024]{0:T(1024)(128)(2,1)} %gain_ref.9, bf16[1024,1024]{1,0:T(8,128)(2,1)} %wq_ref.3, bf16[1024,512]{1,0:T(8,128)(2,1)} %wk_ref.3, ...), custom_call_target="tpu_custom_call" | custom-call | flops 5000000000 | bytes 1048576 | tf_op jit(solution)/shard_map/project_back/pallas_call | solution.py:635
  172.7 12.1 %all_to_all.42 = bf16[16,8,1024]{2,1,0:T(8,128)(2,1)S(1)} all-to-all(bf16[16,8,1024]{2,1,0:T(8,128)(2,1)S(1)} %broadcast_in_dim.20), channel_id=1, replica_groups=mesh['y'=4,'xh'=2,'z'=4,'xl'=2,'core'=2] {'y','xh','xl'}, dimensions={0} | all-to-all | bytes 524288 | tf_op jit(solution)/shard_map/all_to_all | solution.py:730
  184.9 12.4 %all_to_all.43 = f32[8,8,1024]{2,1,0:T(8,128)S(1)} all-to-all(f32[8,8,1024]{2,1,0:T(8,128)S(1)} %broadcast_in_dim.21), channel_id=1, replica_groups=mesh['y'=4,'xh'=2,'z'=4,'xl'=2,'core'=2] {'z','core'}, dimensions={0} | all-to-all | bytes 524288 | tf_op jit(solution)/shard_map/all_to_all | solution.py:730
  198.5 33.7 %all-gather.15.cloned.1.call-done = bf16[61440,128]{1,0:T(8,128)(2,1)} async-done(((bf16[480,128]{1,0:T(8,128)(2,1)}), bf16[61440,128]{1,0:T(8,128)(2,1)}) %all-gather.15.cloned.1.call-update) | async-done | bytes 15728656 | tf_op jit(solution)/shard_map/all_gather | solution.py:742
  232.2 17.7 %assemble.1 = (f32[1024,1024]{1,0:T(8,128)}, f32[1024,512]{1,0:T(8,128)}, f32[1024,512]{1,0:T(8,128)}, f32[8,2,64,1024]{3,2,1,0:T(8,128)}, f32[3,1024,512]{2,1,0...) custom-call(bf16[4,4,2,2,2,480,128]{6,5,4,3,2,1,0:T(8,128)(2,1)} %bitcast.18, ...), custom_call_target="tpu_custom_call" | custom-call | flops 20000000000 | bytes 1048576 | tf_op jit(solution)/shard_map/assemble/pallas_call | solution.py:705
  (86 shorter events, 16.2 us)
Async XLA Ops:
  7.2 4.1 %copy-start.6 = (bf16[1,128,1024]{2,1,0:T(8,128)(2,1)S(1)}, bf16[1,128,1024]{2,1,0:T(8,128)(2,1)}, u32[]{:S(2)}) copy-start(bf16[1,128,1024]{2,1,0:T(8,128)(2,1)} %param.15) | copy-start | bytes 786436
  11.3 7.9 %collective-permute-start = (bf16[128,1024]{1,0:T(8,128)(2,1)S(1)}, bf16[128,1024]{1,0:T(8,128)(2,1)S(1)}, u32[]{:S(2)}, u32[]{:S(2)}) collective-permute-start(bf16[128,1024]{1,0:T(8,128)(2,1)S(1)} %bitcast.24), channel_id=1, source_target_pairs={{0,1},{1,0},{2,3},{3,2},{4,5},{5,4},{6,7},{7,6},{8,9},{9,8},{10,11... | collective-permute-start | bytes 786440 | tf_op jit(solution)/shard_map/ppermute | solution.py:734
  12.7 20.7 %all-to-all-start = ((bf16[16,208,128]{2,1,0:T(8,128)(2,1)}), bf16[16,208,128]{2,1,0:T(8,128)(2,1)S(1)}, u32[]{:S(2)}, u32[]{:S(2)}) async-start(bf16[16,208,128]{2,1,0:T(8,128)(2,1)} %project.1), calls=%async_computation | async-start | bytes 1703936 | tf_op jit(solution)/shard_map/all_to_all | solution.py:730
  19.2 57.9 %all-gather.9.cloned.1.call-start = ((), (), s32[]{:S(2)}) async-start(), calls=%async_computation.8 | async-start | bytes 2359296 | tf_op jit(solution)/shard_map/all_gather | solution.py:742
  19.3 16.6 %copy-start.1 = (bf16[2,128,1024]{2,1,0:T(8,128)(2,1)}, bf16[2,128,1024]{2,1,0:T(8,128)(2,1)S(1)}, u32[]{:S(2)}) copy-start(bf16[2,128,1024]{2,1,0:T(8,128)(2,1)S(1)} %pad_maximum_fusion.cot0_ref) | copy-start | bytes 1572868
  19.3 14.1 %collective-permute-start.1 = (bf16[2,128,1024]{2,1,0:T(8,128)(2,1)S(1)}, bf16[2,128,1024]{2,1,0:T(8,128)(2,1)S(1)}, u32[]{:S(2)}, u32[]{:S(2)}) collective-permute-start(bf16[2,128,1024]{2,1,0:T(8,128)(2,1)S(1)} %pad_maximum_fusion.cot0_ref), channel_id=1, source_target_pairs={{0,96},{32,0},{64,32},{96,64},{1,97},{33,1},{65,33},{97,65},{2,98}... | collective-permute-start | bytes 1572872 | tf_op jit(solution)/shard_map/ppermute | solution.py:738
  33.4 13.0 %copy-start.12 = (bf16[2,128,1024]{2,1,0:T(8,128)(2,1)}, bf16[2,128,1024]{2,1,0:T(8,128)(2,1)S(1)}, u32[]{:S(2)}) copy-start(bf16[2,128,1024]{2,1,0:T(8,128)(2,1)S(1)} %collective-permute-done.1.cot3_ref) | copy-start | bytes 1572868
  33.4 4.1 %copy-start = (bf16[16,208,128]{2,1,0:T(8,128)(2,1)}, bf16[16,208,128]{2,1,0:T(8,128)(2,1)S(1)}, u32[]{:S(2)}) copy-start(bf16[16,208,128]{2,1,0:T(8,128)(2,1)S(1)} %all-to-all-done.x_ref) | copy-start | bytes 2555908
  33.4 21.2 %copy-start.11 = (s32[1,128,2]{1,2,0:T(2,128)S(1)}, s32[1,128,2]{1,2,0:T(2,128)}, u32[]{:S(2)}) copy-start(s32[1,128,2]{1,2,0:T(2,128)} %param.17) | copy-start | bytes 3076
  33.4 22.0 %copy-start.10 = (bf16[1024,3]{0,1:T(4,128)(2,1)S(1)}, bf16[1024,3]{0,1:T(4,128)(2,1)}, u32[]{:S(2)}) copy-start(bf16[1024,3]{0,1:T(4,128)(2,1)} %param.24) | copy-start | bytes 18436
  33.5 27.8 %collective-permute-start.3 = (bf16[2,128,1024]{2,1,0:T(8,128)(2,1)S(1)}, bf16[2,128,1024]{2,1,0:T(8,128)(2,1)S(1)}, u32[]{:S(2)}, u32[]{:S(2)}) collective-permute-start(bf16[2,128,1024]{2,1,0:T(8,128)(2,1)S(1)} %pad_maximum_fusion.cot0_ref), channel_id=1, source_target_pairs={{0,64},{32,96},{64,0},{96,32},{1,65},{33,97},{65,1},{97,33},{2,66}... | collective-permute-start | bytes 1572872 | tf_op jit(solution)/shard_map/ppermute | solution.py:738
  35.9 25.3 %collective-permute-start.2 = (bf16[2,128,1024]{2,1,0:T(8,128)(2,1)S(1)}, bf16[2,128,1024]{2,1,0:T(8,128)(2,1)S(1)}, u32[]{:S(2)}, u32[]{:S(2)}) collective-permute-start(bf16[2,128,1024]{2,1,0:T(8,128)(2,1)S(1)} %pad_maximum_fusion.cot0_ref), channel_id=1, source_target_pairs={{0,32},{32,64},{64,96},{96,0},{1,33},{33,65},{65,97},{97,1},{2,34}... | collective-permute-start | bytes 1572872 | tf_op jit(solution)/shard_map/ppermute | solution.py:738
  46.4 14.9 %all-to-all-start.1 = ((bf16[16,64,128]{2,1,0:T(8,128)(2,1)}), bf16[16,64,128]{2,1,0:T(8,128)(2,1)S(1)}, u32[]{:S(2)}, u32[]{:S(2)}) async-start(bf16[16,64,128]{2,1,0:T(8,128)(2,1)} %get-tuple-element.75), calls=%async_computation.1 | async-start | bytes 524288 | tf_op jit(solution)/shard_map/all_to_all | solution.py:730
  53.2 52.3 %all-gather.11.cloned.1.call-start = ((), (), s32[]{:S(2)}) async-start(), calls=%async_computation.9 | async-start | bytes 2359296 | tf_op jit(solution)/shard_map/all_gather | solution.py:742
  53.2 8.0 %collective-permute-start.4 = (bf16[8,64,128]{2,1,0:T(8,128)(2,1)}, bf16[8,64,128]{2,1,0:T(8,128)(2,1)S(1)}, u32[]{:S(2)}, u32[]{:S(2)}) collective-permute-start(bf16[8,64,128]{2,1,0:T(8,128)(2,1)} %get-tuple-element.77), channel_id=1, source_target_pairs={{0,2},{2,0},{1,3},{3,1},{4,6},{6,4},{5,7},{7,5},{8,10},{10,8},{9,1... | collective-permute-start | bytes 393224 | tf_op jit(solution)/shard_map/ppermute | solution.py:734
  61.2 15.8 %copy-start.17 = (bf16[8,64,128]{2,1,0:T(8,128)(2,1)}, bf16[8,64,128]{2,1,0:T(8,128)(2,1)S(1)}, u32[]{:S(2)}) copy-start(bf16[8,64,128]{2,1,0:T(8,128)(2,1)S(1)} %collective-permute-done.4.att_other_ref) | copy-start | bytes 393220
  61.2 4.2 %copy-start.13 = (bf16[2,128,1024]{2,1,0:T(8,128)(2,1)}, bf16[2,128,1024]{2,1,0:T(8,128)(2,1)S(1)}, u32[]{:S(2)}) copy-start(bf16[2,128,1024]{2,1,0:T(8,128)(2,1)S(1)} %collective-permute-done.3.cot2_ref) | copy-start | bytes 1572868
  61.3 4.2 %copy-start.14 = (bf16[2,128,1024]{2,1,0:T(8,128)(2,1)}, bf16[2,128,1024]{2,1,0:T(8,128)(2,1)S(1)}, u32[]{:S(2)}) copy-start(bf16[2,128,1024]{2,1,0:T(8,128)(2,1)S(1)} %collective-permute-done.2.cot1_ref) | copy-start | bytes 1572868
  65.5 57.9 %all-gather.13.cloned.1.call-start = ((), (), s32[]{:S(2)}) async-start(), calls=%async_computation.10 | async-start | bytes 2359296 | tf_op jit(solution)/shard_map/all_gather | solution.py:742
  77.1 12.2 %all-to-all-start.2 = ((bf16[16,64,128]{2,1,0:T(8,128)(2,1)}), bf16[16,64,128]{2,1,0:T(8,128)(2,1)S(1)}, u32[]{:S(2)}, u32[]{:S(2)}) async-start(bf16[16,64,128]{2,1,0:T(8,128)(2,1)} %get-tuple-element.86), calls=%async_computation.2 | async-start | bytes 524288 | tf_op jit(solution)/shard_map/all_to_all | solution.py:730
  83.4 19.6 %copy-start.3 = (bf16[2,400,128]{2,1,0:T(8,128)(2,1)}, bf16[2,400,128]{2,1,0:T(8,128)(2,1)S(1)}, u32[]{:S(2)}) copy-start(bf16[2,400,128]{2,1,0:T(8,128)(2,1)S(1)} %get-tuple-element.102.acts0_ref) | copy-start | bytes 614404
  89.3 13.7 %collective-permute-start.5 = (bf16[2,400,128]{2,1,0:T(8,128)(2,1)S(1)}, bf16[2,400,128]{2,1,0:T(8,128)(2,1)S(1)}, u32[]{:S(2)}, u32[]{:S(2)}) collective-permute-start(bf16[2,400,128]{2,1,0:T(8,128)(2,1)S(1)} %get-tuple-element.98), channel_id=1, source_target_pairs={{0,32},{32,64},{64,96},{96,0},{1,33},{33,65},{65,97},{97,1},{2,34}... | collective-permute-start | bytes 614408 | tf_op jit(solution)/shard_map/ppermute | solution.py:738
  89.3 13.7 %collective-permute-start.6 = (bf16[2,400,128]{2,1,0:T(8,128)(2,1)S(1)}, bf16[2,400,128]{2,1,0:T(8,128)(2,1)S(1)}, u32[]{:S(2)}, u32[]{:S(2)}) collective-permute-start(bf16[2,400,128]{2,1,0:T(8,128)(2,1)S(1)} %get-tuple-element.99), channel_id=1, source_target_pairs={{0,64},{32,96},{64,0},{96,32},{1,65},{33,97},{65,1},{97,33},{2,66}... | collective-permute-start | bytes 614408 | tf_op jit(solution)/shard_map/ppermute | solution.py:738
  91.0 12.0 %collective-permute-start.7 = (bf16[2,400,128]{2,1,0:T(8,128)(2,1)S(1)}, bf16[2,400,128]{2,1,0:T(8,128)(2,1)S(1)}, u32[]{:S(2)}, u32[]{:S(2)}) collective-permute-start(bf16[2,400,128]{2,1,0:T(8,128)(2,1)S(1)} %get-tuple-element.100), channel_id=1, source_target_pairs={{0,96},{32,0},{64,32},{96,64},{1,97},{33,1},{65,33},{97,65},{2,98}... | collective-permute-start | bytes 614408 | tf_op jit(solution)/shard_map/ppermute | solution.py:738
  103.2 3.3 %collective-permute-start.9 = (bf16[4,400,128]{2,1,0:T(8,128)(2,1)S(1)}, bf16[4,400,128]{2,1,0:T(8,128)(2,1)S(1)}, u32[]{:S(2)}, u32[]{:S(2)}) collective-permute-start(bf16[4,400,128]{2,1,0:T(8,128)(2,1)S(1)} %pad_maximum_fusion.1), channel_id=1, source_target_pairs={{0,1},{1,0},{2,3},{3,2},{4,5},{5,4},{6,7},{7,6},{8,9},{9,8},{10,11... | collective-permute-start | bytes 1228808 | tf_op jit(solution)/shard_map/ppermute | solution.py:734
  105.1 11.0 %collective-permute-start.8 = (bf16[8,192,128]{2,1,0:T(8,128)(2,1)}, bf16[8,192,128]{2,1,0:T(8,128)(2,1)S(1)}, u32[]{:S(2)}, u32[]{:S(2)}) collective-permute-start(bf16[8,192,128]{2,1,0:T(8,128)(2,1)} %get-tuple-element.101), channel_id=1, source_target_pairs={{0,2},{2,0},{1,3},{3,1},{4,6},{6,4},{5,7},{7,5},{8,10},{10,8},{9,1... | collective-permute-start | bytes 1179656 | tf_op jit(solution)/shard_map/ppermute | solution.py:734
  116.1 23.4 %all-to-all-start.3 = ((bf16[16,288,128]{2,1,0:T(8,128)(2,1)}), bf16[16,288,128]{2,1,0:T(8,128)(2,1)S(1)}, u32[]{:S(2)}, u32[]{:S(2)}) async-start(bf16[16,288,128]{2,1,0:T(8,128)(2,1)} %expert_weights.1), calls=%async_computation.3 | async-start | bytes 2359296 | tf_op jit(solution)/shard_map/all_to_all | solution.py:730
  119.8 112.4 %all-gather.15.cloned.1.call-start = ((), (), s32[]{:S(2)}) async-start(), calls=%async_computation.11 | async-start | bytes 15851520 | tf_op jit(solution)/shard_map/all_gather | solution.py:742
  127.0 22.4 %copy-start.2 = (bf16[8,256,128]{2,1,0:T(8,128)(2,1)S(1)}, bf16[8,256,128]{2,1,0:T(8,128)(2,1)}, u32[]{:S(2)}) copy-start(bf16[8,256,128]{2,1,0:T(8,128)(2,1)} %get-tuple-element.119) | copy-start | bytes 1572868
  128.2 6.9 %collective-permute-start.10 = (bf16[4,192,128]{2,1,0:T(8,128)(2,1)S(1)}, bf16[4,192,128]{2,1,0:T(8,128)(2,1)S(1)}, u32[]{:S(2)}, u32[]{:S(2)}) collective-permute-start(bf16[4,192,128]{2,1,0:T(8,128)(2,1)S(1)} %get-tuple-element.136), channel_id=1, source_target_pairs={{0,32},{32,64},{64,96},{96,0},{1,33},{33,65},{65,97},{97,1},{2,34}... | collective-permute-start | bytes 589832 | tf_op jit(solution)/shard_map/ppermute | solution.py:738
  128.3 6.9 %collective-permute-start.12 = (bf16[4,192,128]{2,1,0:T(8,128)(2,1)S(1)}, bf16[4,192,128]{2,1,0:T(8,128)(2,1)S(1)}, u32[]{:S(2)}, u32[]{:S(2)}) collective-permute-start(bf16[4,192,128]{2,1,0:T(8,128)(2,1)S(1)} %get-tuple-element.137), channel_id=1, source_target_pairs={{0,96},{32,0},{64,32},{96,64},{1,97},{33,1},{65,33},{97,65},{2,98}... | collective-permute-start | bytes 589832 | tf_op jit(solution)/shard_map/ppermute | solution.py:738
  130.9 7.5 %collective-permute-start.11 = (bf16[4,192,128]{2,1,0:T(8,128)(2,1)S(1)}, bf16[4,192,128]{2,1,0:T(8,128)(2,1)S(1)}, u32[]{:S(2)}, u32[]{:S(2)}) collective-permute-start(bf16[4,192,128]{2,1,0:T(8,128)(2,1)S(1)} %get-tuple-element.138), channel_id=1, source_target_pairs={{0,64},{32,96},{64,0},{96,32},{1,65},{33,97},{65,1},{97,33},{2,66}... | collective-permute-start | bytes 589832 | tf_op jit(solution)/shard_map/ppermute | solution.py:738
  (7 other events, 18.9 us)
Sparse Core Ops, SparseCore 0:
  33.6 29.8 all-gather.8
  65.6 25.3 all-gather.10
  92.7 25.6 all-gather.12
  149.5 82.6 all-gather.14
